TPU v7x, 128 devices: a whole 4x4x4 slice. The times are simulated.
128 devices in a mesh: opair: 4 (over x), vpair: 32 (over z, y, core).
Axes of the slice: x: 4, y: 4, z: 4, core: 2. Of those that a mesh axis runs over, the one named last changes fastest.
Arguments:
- grid_tiles: bfloat16 [32768, 128, 128], P(('opair', 'vpair')), may hold values from -6 to 6
- tile_rows: int32 [32768], P(('opair', 'vpair')), may hold values from 0 to 127, as said below
- tile_cols: int32 [32768], P(('opair', 'vpair')), may hold values from 0 to 511, as said below
- tile_owner: int32 [32768], P(('opair', 'vpair')), may hold values from -1 to 16383, as said below
- integrals: bfloat16 [65536, 1024], P('vpair'), may hold values from -0.046875 to 0.046875
Outputs:
- ov_tiles: bfloat16 [16384, 128, 128], P(('opair', 'vpair'))
- cycle: float32 [16384, 1024], P(('opair', 'vpair'))
Inputs may be any that keep to these rules, and one draw needn't show every extreme that they name: `tile_owner`: every position 0 to 16383 is named by exactly one slot; the other slots hold -1. Position p belongs to device p // 128. The slots of one device send to each device either no tiles or exactly 2. A device has at most 254 slots that are not -1, and some device has exactly that many. The row tile of a slot that is not empty lies in the opair group of its owner: tile_rows // 32 equals the opair index of device tile_owner // 128. Empty slots hold 0. The (kc) tile of a slot that is not empty lies in the vpair group of its owner: tile_cols // 16 equals the vpair index of device tile_owner // 128. No two slots that are not empty hold the same pair of tile_rows and tile_cols. Empty slots hold 0.
All inputs are finite; a program needn't handle non-finite values.
Results may differ from a plain program's by a relative error of at most 0.001.
Values may be sent and summed in bfloat16 or wider, within the bound.
A program may use at most 256 MiB of HBM per device.

v0:
```python
import jax
import jax.numpy as jnp
from jax import lax
from jax.sharding import PartitionSpec as P

RT_OP = 32


def inverse_pick(landing, length):
    source_ids = jnp.arange(landing.shape[0], dtype=jnp.int32)
    equal = landing[:, None] == jnp.arange(length, dtype=jnp.int32)[None, :]
    found = jnp.any(equal, axis=0)
    picked = jnp.sum(jnp.where(equal, source_ids[:, None], 0), axis=0)
    return (picked, found)


def tile_incomplete_sum(tiles, row_local, col_local, int_table, row_count):
    owned_count, tile_width, _ = tiles.shape
    block_size = 64
    block_count = owned_count // block_size
    tile_blocks = tiles.reshape(block_count, block_size, tile_width, tile_width)
    row_blocks = row_local.reshape(block_count, block_size)
    col_blocks = col_local.reshape(block_count, block_size)
    row_ids = jnp.arange(row_count, dtype=jnp.int32)

    def advance(running, pieces):
        tile_fraction, row_part, col_part = pieces
        selected_entries = jnp.take(int_table, col_part, axis=0)
        pairwise_products = jnp.einsum(
            "wjf,wjq->wfq", tile_fraction, selected_entries, preferred_element_type=jnp.float32
        )
        selector = (row_ids[:, None] == row_part[None, :]).astype(jnp.float32)
        added = jnp.einsum(
            "rw,wfq->rfq", selector, pairwise_products, precision=lax.Precision.HIGHEST
        )
        return (running + added, None)

    start_sum = jnp.zeros((row_count, tile_width, int_table.shape[2]), jnp.float32)
    partial_value, _ = lax.scan(advance, start_sum, (tile_blocks, row_blocks, col_blocks))
    return partial_value.reshape(row_count * tile_width, int_table.shape[2])


def on_device(grid_tiles, tile_rows, tile_cols, tile_owner, integrals):
    op_count = lax.axis_size("opair")
    vp_count = lax.axis_size("vpair")
    devices = op_count * vp_count
    slot_count, tile_width, _ = grid_tiles.shape
    owned = slot_count // 2
    capacity = slot_count // devices
    kc_local = integrals.shape[0] // tile_width
    int_table = integrals.reshape(kc_local, tile_width, integrals.shape[1])
    live_slots = tile_owner >= 0
    target = jnp.where(live_slots, tile_owner // owned, devices)
    matches = (target[:, None] == jnp.arange(devices, dtype=jnp.int32)[None, :]).astype(jnp.int32)
    earlier = jnp.sum((jnp.cumsum(matches, axis=0) - matches) * matches, axis=1)
    placing = jnp.where(live_slots, target * capacity + earlier, devices * capacity)
    send_pick, send_found = inverse_pick(placing, devices * capacity)
    departing_tiles = jnp.where(
        send_found[:, None, None],
        jnp.take(grid_tiles, send_pick, axis=0),
        jnp.zeros((), jnp.bfloat16),
    )
    label_rows = jnp.stack([tile_owner, tile_rows, tile_cols], axis=1)
    labels = jnp.where(send_found[:, None], jnp.take(label_rows, send_pick, axis=0), -1)
    incoming, arrived = (
        lax.all_to_all(
            departing_tiles, ("opair", "vpair"), split_axis=0, concat_axis=0, tiled=True
        ),
        lax.all_to_all(labels, ("opair", "vpair"), split_axis=0, concat_axis=0, tiled=True),
    )
    position = arrived[:, 0]
    landing = jnp.where(position >= 0, position % owned, owned)
    land_pick, _ = inverse_pick(landing, owned)
    placed = jnp.take(incoming, land_pick, axis=0)
    ov_tiles = jnp.swapaxes(placed, 1, 2)
    arrived_owned = jnp.take(arrived, land_pick, axis=0)
    row_local = arrived_owned[:, 1] % RT_OP
    col_local = arrived_owned[:, 2] % kc_local
    partial_value = tile_incomplete_sum(placed, row_local, col_local, int_table, RT_OP)
    cycle_sum = lax.psum_scatter(partial_value, "vpair", scatter_dimension=0, tiled=True)
    return (ov_tiles, cycle_sum)


def solution(mesh):
    in_specs = (
        P(("opair", "vpair"), None, None),
        P(("opair", "vpair")),
        P(("opair", "vpair")),
        P(("opair", "vpair")),
        P("vpair", None),
    )
    out_specs = (P(("opair", "vpair"), None, None), P(("opair", "vpair"), None))
    return jax.shard_map(
        on_device, mesh=mesh, in_specs=in_specs, out_specs=out_specs, check_vma=False
    )
```

profile of v0, /device:TPU:0, one launch (start us, length us, event | category | flops | bytes accessed | tf_op | source)
XLA Modules:
  0.0 454.0 jit_solution(3060278601118796969)
XLA Ops:
  7.2 0.7 fusion.33
  9.1 0.7 add_select_fusion.1
  10.5 0.7 pad_add_fusion
  11.6 0.7 gather_fusion.1
  12.3 1.0 select_select_fusion.1
  13.3 11.1 %all-to-all-start = ((s32[128,2,3]{2,1,0:T(2,128)}), s32[128,2,3]{2,1,0:T(2,128)S(1)}, u32[]{:S(2)}, u32[]{:S(2)}) async-start(s32[128,2,3]{2,1,0:T(2,128)} %select_select_fusion.1), calls=%async_computation | async-start | bytes 262144 | tf_op jit(solution)/shard_map/all_to_all | solution.py:69
  24.4 12.0 %gather_fusion.2 = bf16[256,128,128]{2,1,0:T(8,128)(2,1)} fusion(bf16[256,128,128]{2,1,0:T(8,128)(2,1)} %param.7, s32[1024]{0:T(1024)S(1)} %pad_clamp_fusion.2), kind=kCustom, calls=%fused_computation.2 | custom fusion | bytes 16778240 | tf_op jit(solution)/shard_map/jit(_take)/gather | solution.py:60
  36.4 7.7 %select_select_fusion = bf16[256,128,128]{2,1,0:T(8,128)(2,1)} fusion(bf16[256,128,128]{2,1,0:T(8,128)(2,1)} %gather_fusion.2, pred[256]{0:T(512)(128)(4,1)S(1)} %compare_and_fusion.3, pred[256]{0:T(512)(128)(4,1)S(1)} %fusion.19), kind=kLoop, calls=%fused_computation.28 | loop fusion | flops 8388608 | bytes 16777728 | tf_op jit(solution)/shard_map/jit(_where)/select_n | solution.py:58
  44.1 10.3 %all-to-all-start.1 = ((bf16[256,128,128]{2,1,0:T(8,128)(2,1)}), bf16[256,128,128]{2,1,0:T(8,128)(2,1)}, u32[]{:S(2)}, u32[]{:S(2)}) async-start(bf16[256,128,128]{2,1,0:T(8,128)(2,1)} %select_select_fusion), calls=%async_computation.1 | async-start | bytes 16777216 | tf_op jit(solution)/shard_map/all_to_all | solution.py:66
  56.2 104.3 %all-to-all-done.1 = bf16[256,128,128]{2,1,0:T(8,128)(2,1)} async-done(((bf16[256,128,128]{2,1,0:T(8,128)(2,1)}), bf16[256,128,128]{2,1,0:T(8,128)(2,1)}, u32[]{:S(2)}, u32[]{:S(2)}) %all-to-all-start.1) | async-done | bytes 8388640 | tf_op jit(solution)/shard_map/all_to_all | solution.py:66
  160.6 6.5 %gather_fusion.3 = bf16[128,128,128]{2,1,0:T(8,128)(2,1)} fusion(bf16[256,128,128]{2,1,0:T(8,128)(2,1)} %all-to-all-done.1, s32[1024]{0:T(1024)S(1)} %pad_clamp_fusion.1), kind=kCustom, calls=%fused_computation.3 | custom fusion | bytes 8389120 | tf_op jit(solution)/shard_map/jit(_take)/gather | solution.py:74
  167.1 6.3 %copy.36 = bf16[2,64,128,128]{2,3,1,0:T(8,128)(2,1)} copy(bf16[2,64,128,128]{3,2,1,0:T(8,128)(2,1)} %bitcast.58) | data formatting | bytes 8388608 | tf_op jit(solution)/shard_map/jit(_take)/gather | solution.py:74
  173.4 4.6 %broadcast_select_fusion = bf16[2,64,128,128]{2,3,1,0:T(8,128)(2,1)} fusion(bf16[2,64,128,128]{2,3,1,0:T(8,128)(2,1)} %copy.36, pred[2,64]{1,0:T(4,128)(4,1)S(1)} %compare_and_fusion.2), kind=kLoop, calls=%fused_computation.30 | loop fusion | flops 2097152 | bytes 8388736 | tf_op jit(solution)/shard_map/jit(_take)/select_n | solution.py:74
  178.0 136.7 %while.11 = (s32[]{:T(128)}, f32[32,128,1024]{2,0,1:T(8,128)}, s32[2,64]{1,0:T(2,128)S(1)}, bf16[2,64,128,128]{2,3,1,0:T(8,128)(2,1)}, s32[2,64]{1,0:T(2,128)S(1...) while((s32[]{:T(128)}, f32[32,128,1024]{2,0,1:T(8,128)}, s32[2,64]{1,0:T(2,128)S(1)}, ...), condition=%wide.region_7.8_spmd.clone, body=%wide.region_6.7_spmd.clone.sunk | while | flops 5385489920 | bytes 153098496 | solution.py:39
  178.0 9.9 %gather_fusion = bf16[64,128,1024]{2,1,0:T(8,128)(2,1)} fusion(bf16[16,128,1024]{2,1,0:T(8,128)(2,1)} %get-tuple-element.143, s32[1024]{0:T(1024)S(1)} %pad_clamp_fusion.4), kind=kCustom, calls=%fused_computation.clone.clone.1 | custom fusion | bytes 33554688 | tf_op jit(solution)/shard_map/while/body/eval_jaxpr/jit(_take)/gather | solution.py:28
  187.9 16.9 %fusion.46 = f32[64,128,1024]{2,1,0:T(8,128)} fusion(bf16[64,128,1024]{2,1,0:T(8,128)(2,1)} %gather_fusion, pred[64]{0:T(512)(128)(4,1)S(1)} %compare_and_fusion.6, bf16[2,64,128,128]{2,3,1,0:T(8,128)(2,1)} %get-tuple-element.141, s32[]{:T(128)S(6)} %copy.47), kind=kOutput, calls=%fused_computation.9.clone.1 | convolution fusion | flops 2155872256 | bytes 52428868 | tf_op jit(solution)/shard_map/while/body/eval_jaxpr/wjf,wjq->wfq/dot_general | solution.py:29
  204.8 41.0 %select_add_fusion.2 = f32[32,128,1024]{2,0,1:T(8,128)} fusion(f32[32,128,1024]{2,0,1:T(8,128)} %get-tuple-element.131, f32[64,128,1024]{2,1,0:T(8,128)} %fusion.46, pred[]{:T(512)S(6)} %compare.8, s32[64]{0:T(128)S(1)} %fusion.47), kind=kOutput, calls=%fused_computation.8.clone.1 | convolution fusion | flops 3229616128 | bytes 67109120 | tf_op jit(solution)/shard_map/while/body/eval_jaxpr/rw,wfq->rfq/dot_general | solution.py:33
  245.8 9.9 %gather_fusion = bf16[64,128,1024]{2,1,0:T(8,128)(2,1)} fusion(bf16[16,128,1024]{2,1,0:T(8,128)(2,1)} %get-tuple-element.143, s32[1024]{0:T(1024)S(1)} %pad_clamp_fusion.4), kind=kCustom, calls=%fused_computation.clone.clone.1 | custom fusion | bytes 33554688 | tf_op jit(solution)/shard_map/while/body/eval_jaxpr/jit(_take)/gather | solution.py:28
  255.6 16.9 %fusion.46 = f32[64,128,1024]{2,1,0:T(8,128)} fusion(bf16[64,128,1024]{2,1,0:T(8,128)(2,1)} %gather_fusion, pred[64]{0:T(512)(128)(4,1)S(1)} %compare_and_fusion.6, bf16[2,64,128,128]{2,3,1,0:T(8,128)(2,1)} %get-tuple-element.141, s32[]{:T(128)S(6)} %copy.47), kind=kOutput, calls=%fused_computation.9.clone.1 | convolution fusion | flops 2155872256 | bytes 52428868 | tf_op jit(solution)/shard_map/while/body/eval_jaxpr/wjf,wjq->wfq/dot_general | solution.py:29
  272.5 42.2 %select_add_fusion.2 = f32[32,128,1024]{2,0,1:T(8,128)} fusion(f32[32,128,1024]{2,0,1:T(8,128)} %get-tuple-element.131, f32[64,128,1024]{2,1,0:T(8,128)} %fusion.46, pred[]{:T(512)S(6)} %compare.8, s32[64]{0:T(128)S(1)} %fusion.47), kind=kOutput, calls=%fused_computation.8.clone.1 | convolution fusion | flops 3229616128 | bytes 67109120 | tf_op jit(solution)/shard_map/while/body/eval_jaxpr/rw,wfq->rfq/dot_general | solution.py:33
  314.7 17.7 %copy.37 = f32[32,128,1024]{2,1,0:T(8,128)} copy(f32[32,128,1024]{2,0,1:T(8,128)} %get-tuple-element.39) | data formatting | bytes 33554432 | tf_op jit(solution)/shard_map/while | solution.py:39
  333.1 4.6 %select_bitcast_fusion = bf16[128,128,128]{1,2,0:T(8,128)(2,1)} fusion(bf16[128,128,128]{2,1,0:T(8,128)(2,1)} %gather_fusion.3, pred[128]{0:T(512)(128)(4,1)S(1)} %copy-done.1), kind=kLoop, calls=%fused_computation.29 | loop fusion | flops 2097152 | bytes 8388736 | tf_op jit(solution)/shard_map/jit(_take)/select_n | solution.py:74
  337.6 6.5 %copy.38 = bf16[128,128,128]{2,1,0:T(8,128)(2,1)} copy(bf16[128,128,128]{1,2,0:T(8,128)(2,1)} %select_bitcast_fusion) | data formatting | bytes 8388608
  344.1 103.1 %reduce-scatter.2.cloned.1.call-done = f32[128,1024]{1,0:T(8,128)} async-done(((f32[4096,1024]{1,0:T(8,128)}), f32[128,1024]{1,0:T(8,128)}) %reduce-scatter.2.cloned.1.call-update) | async-done | bytes 524304 | tf_op jit(solution)/shard_map/reduce_scatter | solution.py:80
  (49 shorter events, 4.7 us)
Async XLA Ops:
  13.3 30.8 %all-to-all-start = ((s32[128,2,3]{2,1,0:T(2,128)}), s32[128,2,3]{2,1,0:T(2,128)S(1)}, u32[]{:S(2)}, u32[]{:S(2)}) async-start(s32[128,2,3]{2,1,0:T(2,128)} %select_select_fusion.1), calls=%async_computation | async-start | bytes 262144 | tf_op jit(solution)/shard_map/all_to_all | solution.py:69
  44.1 116.5 %all-to-all-start.1 = ((bf16[256,128,128]{2,1,0:T(8,128)(2,1)}), bf16[256,128,128]{2,1,0:T(8,128)(2,1)}, u32[]{:S(2)}, u32[]{:S(2)}) async-start(bf16[256,128,128]{2,1,0:T(8,128)(2,1)} %select_select_fusion), calls=%async_computation.1 | async-start | bytes 16777216 | tf_op jit(solution)/shard_map/all_to_all | solution.py:66
  54.4 392.8 %reduce-scatter.2.cloned.1.call-start = ((), (), s32[]{:S(2)}) async-start(), calls=%async_computation.3 | async-start | bytes 17301504 | tf_op jit(solution)/shard_map/reduce_scatter | solution.py:80
  55.5 0.6 copy-start
  332.4 0.7 copy-start.1
Sparse Core Ops, SparseCore 0:
  332.5 114.6 reduce-scatter.1
where the time goes:
time: 455 us; the launch traced here: 454 us
  waiting for transfers between devices  207 us (45%)
  matrix products  117 us (26%)
  local copies, waits for them, and re-layouts  72.2 us (16%)
  other arithmetic  21.9 us (5%)
  starting transfers between devices  21.5 us (5%)
  between operations  14.2 us (3%)
    all_to_all x1, waiting for transfers between devices, on_device(): lax.all_to_all(departing_tiles, ('opair', 'vpair'), split_axis=0, concat_...  104 us
    reduce_scatter x1, waiting for transfers between devices, on_device(): lax.psum_scatter(partial_value, 'vpair', scatter_dimension=0, tiled=True)  103 us
    dot_general x2, matrix products, advance(): jnp.einsum('rw,wfq->rfq', selector, pairwise_products, precision=lax.Prec...  83.1 us
    dot_general x2, matrix products, advance(): jnp.einsum('wjf,wjq->wfq', tile_fraction, selected_entries, preferred_ele...  33.7 us
    gather x2, local copies, waits for them, and re-layouts, advance(): selected_entries = jnp.take(int_table, col_part, axis=0)  19.7 us
    while x1, local copies, waits for them, and re-layouts, tile_incomplete_sum(): lax.scan(advance, start_sum, (tile_blocks, row_blocks, col_blocks))  17.7 us
    gather x2, local copies, waits for them, and re-layouts, on_device(): placed = jnp.take(incoming, land_pick, axis=0)  12.8 us
    gather x1, local copies, waits for them, and re-layouts, on_device(): jnp.take(grid_tiles, send_pick, axis=0)  12 us
  transfers between devices with their start and end apart: 3, of which 2 were waited for; matrix products, arithmetic and copies ran while one was open for 7% of the time, Pallas kernels for 0%

commit v1 on v0

v1 whole, which is shorter than its diff:
```python
import jax
import jax.numpy as jnp
from jax import lax
from jax.experimental import pallas as pl
from jax.experimental.pallas import tpu as pltpu
from jax.sharding import PartitionSpec as P

RT_OP = 32
VMEM_LIMIT = 60 * 1024 * 1024


def gather_kernel(src_ref, grid_ref, out_ref):
    zero = jnp.zeros(out_ref.shape[1:], out_ref.dtype)

    def body(j, carry):
        s = src_ref[j]

        @pl.when(s >= 0)
        def _():
            out_ref[j] = grid_ref[jnp.maximum(s, 0)]

        @pl.when(s < 0)
        def _():
            out_ref[j] = zero

        return carry

    lax.fori_loop(0, out_ref.shape[0], body, 0)


def gather_tiles(src, grid_tiles):
    return pl.pallas_call(
        gather_kernel,
        out_shape=jax.ShapeDtypeStruct(grid_tiles.shape, grid_tiles.dtype),
        in_specs=[
            pl.BlockSpec(memory_space=pltpu.SMEM),
            pl.BlockSpec(memory_space=pltpu.VMEM),
        ],
        out_specs=pl.BlockSpec(memory_space=pltpu.VMEM),
        compiler_params=pltpu.CompilerParams(vmem_limit_bytes=VMEM_LIMIT),
    )(src, grid_tiles)


def place_kernel(meta_ref, inc_ref, int_ref, ov_ref, part_ref):
    slots = inc_ref.shape[0]
    part_ref[...] = jnp.zeros(part_ref.shape, part_ref.dtype)

    def body(i, carry):
        pos = meta_ref[i]
        row = meta_ref[slots + i]
        col = meta_ref[2 * slots + i]

        @pl.when(pos >= 0)
        def _():
            tile_t = inc_ref[i].T
            ov_ref[pos] = tile_t
            part_ref[row] += jnp.dot(
                tile_t, int_ref[col], preferred_element_type=jnp.float32
            )

        return carry

    lax.fori_loop(0, slots, body, 0)


def place_and_contract(meta, incoming, int_table, owned, rows):
    tile_width = incoming.shape[1]
    columns = int_table.shape[2]
    return pl.pallas_call(
        place_kernel,
        out_shape=(
            jax.ShapeDtypeStruct((owned, tile_width, tile_width), incoming.dtype),
            jax.ShapeDtypeStruct((rows, tile_width, columns), jnp.float32),
        ),
        in_specs=[
            pl.BlockSpec(memory_space=pltpu.SMEM),
            pl.BlockSpec(memory_space=pltpu.VMEM),
            pl.BlockSpec(memory_space=pltpu.VMEM),
        ],
        out_specs=(
            pl.BlockSpec(memory_space=pltpu.VMEM),
            pl.BlockSpec(memory_space=pltpu.VMEM),
        ),
        compiler_params=pltpu.CompilerParams(vmem_limit_bytes=VMEM_LIMIT),
    )(meta, incoming, int_table)


def on_device(grid_tiles, tile_rows, tile_cols, tile_owner, integrals):
    op_count = lax.axis_size("opair")
    vp_count = lax.axis_size("vpair")
    devices = op_count * vp_count
    slot_count, tile_width, _ = grid_tiles.shape
    owned = slot_count // 2
    capacity = slot_count // devices
    kc_local = integrals.shape[0] // tile_width
    int_table = integrals.reshape(kc_local, tile_width, integrals.shape[1])
    live_slots = tile_owner >= 0
    target = jnp.where(live_slots, tile_owner // owned, devices)
    matches = (target[:, None] == jnp.arange(devices, dtype=jnp.int32)[None, :]).astype(jnp.int32)
    earlier = jnp.sum((jnp.cumsum(matches, axis=0) - matches) * matches, axis=1)
    placing = jnp.where(live_slots, target * capacity + earlier, devices * capacity)
    src = (
        jnp.full((devices * capacity + 1,), -1, jnp.int32)
        .at[placing]
        .set(jnp.arange(slot_count, dtype=jnp.int32))[: devices * capacity]
    )
    departing_tiles = gather_tiles(src, grid_tiles)
    label_rows = jnp.stack([tile_owner % owned, tile_rows % RT_OP, tile_cols % kc_local], axis=1)
    labels = jnp.where((src >= 0)[:, None], jnp.take(label_rows, jnp.maximum(src, 0), axis=0), -1)
    arrived = lax.all_to_all(labels, ("opair", "vpair"), split_axis=0, concat_axis=0, tiled=True)
    incoming = lax.all_to_all(
        departing_tiles, ("opair", "vpair"), split_axis=0, concat_axis=0, tiled=True
    )
    meta = jnp.transpose(arrived).reshape(-1)
    ov_tiles, partial_value = place_and_contract(meta, incoming, int_table, owned, RT_OP)
    partial_value = partial_value.reshape(RT_OP * tile_width, int_table.shape[2])
    cycle_sum = lax.psum_scatter(partial_value, "vpair", scatter_dimension=0, tiled=True)
    return (ov_tiles, cycle_sum)


def solution(mesh):
    in_specs = (
        P(("opair", "vpair"), None, None),
        P(("opair", "vpair")),
        P(("opair", "vpair")),
        P(("opair", "vpair")),
        P("vpair", None),
    )
    out_specs = (P(("opair", "vpair"), None, None), P(("opair", "vpair"), None))
    return jax.shard_map(
        on_device, mesh=mesh, in_specs=in_specs, out_specs=out_specs, check_vma=False
    )
```

time: 455 us -> 324 us (0.71)
  matrix products: 117 us -> 0 us
  local copies, waits for them, and re-layouts: 72.2 us -> 3.4 us
  Pallas kernels: 0 us -> 59.2 us
  other arithmetic: 21.9 us -> 5.46 us
  waiting for transfers between devices: 207 us -> 220 us
    dot_general x4 -> x0, matrix products: 117 us -> none  [the longest x2 83.1 us: advance(): jnp.einsum('rw,wfq->rfq', selector, pairwise_products, precision=lax.Prec...]
    pallas_call x0 -> x2, Pallas kernels: none -> 59.2 us  [the longest x1 47.2 us: place_and_contract(): pl.pallas_call(place_kernel, out_shape=(jax.ShapeDtypeStruct((owned, tile...]
    gather x7 -> x1, local copies, waits for them, and re-layouts: 45.9 us -> 0.73 us  [on_device(): jnp.take(label_rows, jnp.maximum(src, 0), axis=0)]
    while x1 -> x0, local copies, waits for them, and re-layouts: 17.7 us -> none  [tile_incomplete_sum(): lax.scan(advance, start_sum, (tile_blocks, row_blocks, col_blocks))]
    select_n x12 -> x4, other arithmetic: 18.9 us -> 3.07 us  [the longest x1 0.99 us: on_device(): jnp.where((src >= 0)[:, None], jnp.take(label_rows, jnp.maximum(src, 0),...]
    reduce_scatter x1, waiting for transfers between devices: 103 us -> 115 us  [on_device(): lax.psum_scatter(partial_value, 'vpair', scatter_dimension=0, tiled=True)]
    unnamed x6 -> x1, local copies, waits for them, and re-layouts: 7.44 us -> 0.01 us
  transfers between devices with their start and end apart: 3 -> 3, of which waited for: 2 -> 2; matrix products, arithmetic and copies ran while one was open for 7% -> 0% of each run, Pallas kernels for 0% -> 4%
where the time goes in v1:
time: 324 us
  waiting for transfers between devices  220 us (68%)
  Pallas kernels  59.2 us (18%)
  starting transfers between devices  21.5 us (7%)
  between operations  14.1 us (4%)
  other arithmetic  5.46 us (2%)
  local copies, waits for them, and re-layouts  3.4 us (1%)
    reduce_scatter x1, waiting for transfers between devices, on_device(): lax.psum_scatter(partial_value, 'vpair', scatter_dimension=0, tiled=True)  115 us
    all_to_all x1, waiting for transfers between devices, on_device(): lax.all_to_all(departing_tiles, ('opair', 'vpair'), split_axis=0, concat_...  105 us
    pallas_call x1, Pallas kernels, place_and_contract(): pl.pallas_call(place_kernel, out_shape=(jax.ShapeDtypeStruct((owned, tile...  47.2 us
    pallas_call x1, Pallas kernels, gather_tiles(): pl.pallas_call(gather_kernel, out_shape=jax.ShapeDtypeStruct(grid_tiles.s...  11.9 us
    all_to_all x1, starting transfers between devices, on_device(): lax.all_to_all(labels, ('opair', 'vpair'), split_axis=0, concat_axis=0, t...  11.1 us
    all_to_all x1, starting transfers between devices, on_device(): lax.all_to_all(departing_tiles, ('opair', 'vpair'), split_axis=0, concat_...  10.3 us
  transfers between devices with their start and end apart: 3, of which 2 were waited for; matrix products, arithmetic and copies ran while one was open for 0% of the time, Pallas kernels for 4%

profile of v1, /device:TPU:0, one launch (start us, length us, event | category | flops | bytes accessed | tf_op | source)
XLA Modules:
  0.0 323.9 jit_solution(201380478828906832)
XLA Ops:
  7.2 0.7 fusion.11
  7.9 0.7 fusion.9
  8.5 0.1 copy.19
  8.7 0.2 fusion
  9.0 0.2 fusion.2
  9.1 0.7 compare_select_fusion
  9.8 1.4 scatter_custom_fusion
  11.3 0.6 fusion.10
  11.8 0.7 and_select_fusion.1
  12.5 0.7 and_select_fusion
  13.2 0.2 ge.17
  13.4 0.2 le.15
  13.5 0.1 copy.21
  13.7 0.7 gather_fusion
  14.4 1.0 select_select_fusion
  15.4 11.1 %all-to-all-start = ((s32[128,2,3]{2,1,0:T(2,128)}), s32[128,2,3]{2,1,0:T(2,128)S(1)}, u32[]{:S(2)}, u32[]{:S(2)}) async-start(s32[128,2,3]{2,1,0:T(2,128)} %select_select_fusion), calls=%async_computation | async-start | bytes 262144 | tf_op jit(solution)/shard_map/all_to_all | solution.py:110
  26.6 11.9 %shard_map.68 = bf16[256,128,128]{2,1,0:T(8,128)(2,1)} custom-call(s32[256]{0:T(256)} %get-tuple-element.6.src_ref, bf16[256,128,128]{2,1,0:T(8,128)(2,1)} %grid_ref.1), custom_call_target="tpu_custom_call" | custom-call | tf_op jit(solution)/shard_map/pallas_call | solution.py:32
  38.5 10.3 %all-to-all-start.1 = ((bf16[256,128,128]{2,1,0:T(8,128)(2,1)}), bf16[256,128,128]{2,1,0:T(8,128)(2,1)}, u32[]{:S(2)}, u32[]{:S(2)}) async-start(bf16[256,128,128]{2,1,0:T(8,128)(2,1)} %shard_map.68), calls=%async_computation.1 | async-start | bytes 16777216 | tf_op jit(solution)/shard_map/all_to_all | solution.py:111
  48.8 0.0 reduce-scatter.2.cloned.1.call-start
  48.9 0.1 copy.23
  49.0 0.6 reshape.57.meta_ref
  49.6 105.4 %all-to-all-done.1.inc_ref = bf16[256,128,128]{2,1,0:T(8,128)(2,1)} async-done(((bf16[256,128,128]{2,1,0:T(8,128)(2,1)}), bf16[256,128,128]{2,1,0:T(8,128)(2,1)}, u32[]{:S(2)}, u32[]{:S(2)}) %all-to-all-start.1) | async-done | bytes 8388640 | tf_op jit(solution)/shard_map/all_to_all | solution.py:111
  155.0 47.2 %shard_map.69 = (bf16[128,128,128]{2,1,0:T(8,128)(2,1)}, f32[32,128,1024]{2,1,0:T(8,128)}) custom-call(s32[768]{0:T(1024)} %reshape.57.meta_ref, bf16[256,128,128]{2,1,0:T(8,128)(2,1)} %all-to-all-done.1.inc_ref, bf16[16,128,1024]{2,1,0:T(8,128)(2,1)} %bitcast.25), custom_call_target="tpu_custom_call" | custom-call | tf_op jit(solution)/shard_map/pallas_call | solution.py:69
  202.3 114.8 %reduce-scatter.2.cloned.1.call-done = f32[128,1024]{1,0:T(8,128)} async-done(((f32[4096,1024]{1,0:T(8,128)}), f32[128,1024]{1,0:T(8,128)}) %reduce-scatter.2.cloned.1.call-update) | async-done | bytes 524304 | tf_op jit(solution)/shard_map/reduce_scatter | solution.py:117
  (12 shorter events, 0.1 us)
Async XLA Ops:
  15.4 23.1 %all-to-all-start = ((s32[128,2,3]{2,1,0:T(2,128)}), s32[128,2,3]{2,1,0:T(2,128)S(1)}, u32[]{:S(2)}, u32[]{:S(2)}) async-start(s32[128,2,3]{2,1,0:T(2,128)} %select_select_fusion), calls=%async_computation | async-start | bytes 262144 | tf_op jit(solution)/shard_map/all_to_all | solution.py:110
  38.5 116.5 %all-to-all-start.1 = ((bf16[256,128,128]{2,1,0:T(8,128)(2,1)}), bf16[256,128,128]{2,1,0:T(8,128)(2,1)}, u32[]{:S(2)}, u32[]{:S(2)}) async-start(bf16[256,128,128]{2,1,0:T(8,128)(2,1)} %shard_map.68), calls=%async_computation.1 | async-start | bytes 16777216 | tf_op jit(solution)/shard_map/all_to_all | solution.py:111
  48.8 268.3 %reduce-scatter.2.cloned.1.call-start = ((), (), s32[]{:S(2)}) async-start(), calls=%async_computation.3 | async-start | bytes 17301504 | tf_op jit(solution)/shard_map/reduce_scatter | solution.py:117
Sparse Core Ops, SparseCore 0:
  202.4 114.6 reduce-scatter.1

commit v2 on v1

--- a/solution.py
+++ b/solution.py
@@ -1,3 +1,5 @@
+import functools
+
 import jax
 import jax.numpy as jnp
 from jax import lax
@@ -6,6 +8,7 @@
 from jax.sharding import PartitionSpec as P
 
 RT_OP = 32
+CHUNKS = 2
 VMEM_LIMIT = 60 * 1024 * 1024
 
 
@@ -41,48 +44,73 @@
     )(src, grid_tiles)
 
 
-def place_kernel(meta_ref, inc_ref, int_ref, ov_ref, part_ref):
+def place_kernel(meta_ref, inc_ref, ov_ref):
     slots = inc_ref.shape[0]
-    part_ref[...] = jnp.zeros(part_ref.shape, part_ref.dtype)
 
     def body(i, carry):
         pos = meta_ref[i]
-        row = meta_ref[slots + i]
-        col = meta_ref[2 * slots + i]
 
         @pl.when(pos >= 0)
         def _():
-            tile_t = inc_ref[i].T
-            ov_ref[pos] = tile_t
-            part_ref[row] += jnp.dot(
-                tile_t, int_ref[col], preferred_element_type=jnp.float32
-            )
+            ov_ref[pos] = inc_ref[i].T
 
         return carry
 
     lax.fori_loop(0, slots, body, 0)
 
 
-def place_and_contract(meta, incoming, int_table, owned, rows):
+def place_tiles(meta, incoming, owned):
     tile_width = incoming.shape[1]
-    columns = int_table.shape[2]
     return pl.pallas_call(
         place_kernel,
-        out_shape=(
-            jax.ShapeDtypeStruct((owned, tile_width, tile_width), incoming.dtype),
-            jax.ShapeDtypeStruct((rows, tile_width, columns), jnp.float32),
-        ),
+        out_shape=jax.ShapeDtypeStruct((owned, tile_width, tile_width), incoming.dtype),
+        in_specs=[
+            pl.BlockSpec(memory_space=pltpu.SMEM),
+            pl.BlockSpec(memory_space=pltpu.VMEM),
+        ],
+        out_specs=pl.BlockSpec(memory_space=pltpu.VMEM),
+        compiler_params=pltpu.CompilerParams(vmem_limit_bytes=VMEM_LIMIT),
+    )(meta, incoming)
+
+
+def contract_kernel(kc_local, cell_ref, ov_ref, int_ref, part_ref, lhs_ref):
+    tile_width = ov_ref.shape[1]
+    zero = jnp.zeros((tile_width, tile_width), ov_ref.dtype)
+
+    def body(r, carry):
+        for kc in range(kc_local):
+            p = cell_ref[r * kc_local + kc]
+            block = pl.ds(kc * tile_width, tile_width)
+
+            @pl.when(p >= 0)
+            def _():
+                lhs_ref[:, block] = ov_ref[jnp.maximum(p, 0)]
+
+            @pl.when(p < 0)
+            def _():
+                lhs_ref[:, block] = zero
+
+        part_ref[r] = jnp.dot(lhs_ref[...], int_ref[...], preferred_element_type=jnp.float32)
+        return carry
+
+    lax.fori_loop(0, part_ref.shape[0], body, 0)
+
+
+def contract(cell, ov_tiles, int_chunk, rows, kc_local):
+    tile_width = ov_tiles.shape[1]
+    columns = int_chunk.shape[1]
+    return pl.pallas_call(
+        functools.partial(contract_kernel, kc_local),
+        out_shape=jax.ShapeDtypeStruct((rows, tile_width, columns), jnp.float32),
         in_specs=[
             pl.BlockSpec(memory_space=pltpu.SMEM),
             pl.BlockSpec(memory_space=pltpu.VMEM),
             pl.BlockSpec(memory_space=pltpu.VMEM),
         ],
-        out_specs=(
-            pl.BlockSpec(memory_space=pltpu.VMEM),
-            pl.BlockSpec(memory_space=pltpu.VMEM),
-        ),
+        out_specs=pl.BlockSpec(memory_space=pltpu.VMEM),
+        scratch_shapes=[pltpu.VMEM((tile_width, kc_local * tile_width), ov_tiles.dtype)],
         compiler_params=pltpu.CompilerParams(vmem_limit_bytes=VMEM_LIMIT),
-    )(meta, incoming, int_table)
+    )(cell, ov_tiles, int_chunk)
 
 
 def on_device(grid_tiles, tile_rows, tile_cols, tile_owner, integrals):
@@ -93,7 +121,6 @@
     owned = slot_count // 2
     capacity = slot_count // devices
     kc_local = integrals.shape[0] // tile_width
-    int_table = integrals.reshape(kc_local, tile_width, integrals.shape[1])
     live_slots = tile_owner >= 0
     target = jnp.where(live_slots, tile_owner // owned, devices)
     matches = (target[:, None] == jnp.arange(devices, dtype=jnp.int32)[None, :]).astype(jnp.int32)
@@ -111,10 +138,18 @@
     incoming = lax.all_to_all(
         departing_tiles, ("opair", "vpair"), split_axis=0, concat_axis=0, tiled=True
     )
-    meta = jnp.transpose(arrived).reshape(-1)
-    ov_tiles, partial_value = place_and_contract(meta, incoming, int_table, owned, RT_OP)
-    partial_value = partial_value.reshape(RT_OP * tile_width, int_table.shape[2])
-    cycle_sum = lax.psum_scatter(partial_value, "vpair", scatter_dimension=0, tiled=True)
+    pos = arrived[:, 0]
+    ov_tiles = place_tiles(pos, incoming, owned)
+    cell_id = jnp.where(pos >= 0, arrived[:, 1] * kc_local + arrived[:, 2], RT_OP * kc_local)
+    cell = jnp.full((RT_OP * kc_local + 1,), -1, jnp.int32).at[cell_id].set(pos)[: RT_OP * kc_local]
+    columns = integrals.shape[1]
+    width = columns // CHUNKS
+    pieces = []
+    for c in range(CHUNKS):
+        part = contract(cell, ov_tiles, integrals[:, c * width : (c + 1) * width], RT_OP, kc_local)
+        part = part.reshape(RT_OP * tile_width, width)
+        pieces.append(lax.psum_scatter(part, "vpair", scatter_dimension=0, tiled=True))
+    cycle_sum = jnp.concatenate(pieces, axis=1)
     return (ov_tiles, cycle_sum)
 
 

time: 324 us -> 397 us (1.23)
  waiting for transfers between devices: 220 us -> 260 us
  Pallas kernels: 59.2 us -> 84.8 us
  local copies, waits for them, and re-layouts: 3.4 us -> 9.57 us
    reduce_scatter x1 -> x2, waiting for transfers between devices: 115 us -> 160 us  [on_device(): lax.psum_scatter(part, 'vpair', scatter_dimension=0, tiled=True)]
    pallas_call x1 -> x3, Pallas kernels: 47.2 us -> 72.9 us  [the longest x2 56.1 us: contract(): pl.pallas_call(functools.partial(contract_kernel, kc_local), out_shape=ja...]
    all_to_all x1, waiting for transfers between devices: 105 us -> 99.2 us  [on_device(): lax.all_to_all(departing_tiles, ('opair', 'vpair'), split_axis=0, concat_...]
    slice x0 -> x3, local copies, waits for them, and re-layouts: none -> 5.18 us  [the longest x1 4.47 us: on_device(): integrals[:, c * width:(c + 1) * width]]
  transfers between devices with their start and end apart: 3 -> 4, of which waited for: 2 -> 3; matrix products, arithmetic and copies ran while one was open for 0% -> 2% of each run, Pallas kernels for 4% -> 10%
where the time goes in v2:
time: 397 us
  waiting for transfers between devices  260 us (65%)
  Pallas kernels  84.8 us (21%)
  starting transfers between devices  21.5 us (5%)
  between operations  14.1 us (4%)
  local copies, waits for them, and re-layouts  9.57 us (2%)
  other arithmetic  7.34 us (2%)
    reduce_scatter x2, waiting for transfers between devices, on_device(): lax.psum_scatter(part, 'vpair', scatter_dimension=0, tiled=True)  160 us
    all_to_all x1, waiting for transfers between devices, on_device(): lax.all_to_all(departing_tiles, ('opair', 'vpair'), split_axis=0, concat_...  99.2 us
    pallas_call x2, Pallas kernels, contract(): pl.pallas_call(functools.partial(contract_kernel, kc_local), out_shape=ja...  56.1 us
    pallas_call x1, Pallas kernels, place_tiles(): pl.pallas_call(place_kernel, out_shape=jax.ShapeDtypeStruct((owned, tile_...  16.7 us
    pallas_call x1, Pallas kernels, gather_tiles(): pl.pallas_call(gather_kernel, out_shape=jax.ShapeDtypeStruct(grid_tiles.s...  11.9 us
    all_to_all x1, starting transfers between devices, on_device(): lax.all_to_all(labels, ('opair', 'vpair'), split_axis=0, concat_axis=0, t...  11.1 us
    all_to_all x1, starting transfers between devices, on_device(): lax.all_to_all(departing_tiles, ('opair', 'vpair'), split_axis=0, concat_...  10.3 us
  transfers between devices with their start and end apart: 4, of which 3 were waited for; matrix products, arithmetic and copies ran while one was open for 2% of the time, Pallas kernels for 10%

profile of v2, /device:TPU:0, one launch (start us, length us, event | category | flops | bytes accessed | tf_op | source)
XLA Modules:
  0.0 397.0 jit_solution(17633733408558994491)
XLA Ops:
  7.2 0.7 fusion.15
  7.9 0.7 fusion.11
  8.7 0.2 fusion
  9.0 0.2 fusion.2
  9.1 0.7 compare_select_fusion.2
  9.8 1.4 scatter_custom_fusion
  11.3 0.6 fusion.14
  11.8 0.7 and_select_fusion.1
  12.5 0.7 and_select_fusion
  13.7 0.7 gather_fusion
  14.4 1.0 select_select_fusion
  15.4 11.1 %all-to-all-start = ((s32[128,2,3]{2,1,0:T(2,128)}), s32[128,2,3]{2,1,0:T(2,128)S(1)}, u32[]{:S(2)}, u32[]{:S(2)}) async-start(s32[128,2,3]{2,1,0:T(2,128)} %select_select_fusion), calls=%async_computation | async-start | bytes 262144 | tf_op jit(solution)/shard_map/all_to_all | solution.py:137
  26.6 11.9 %shard_map.68 = bf16[256,128,128]{2,1,0:T(8,128)(2,1)} custom-call(s32[256]{0:T(256)} %get-tuple-element.7.src_ref, bf16[256,128,128]{2,1,0:T(8,128)(2,1)} %grid_ref.1), custom_call_target="tpu_custom_call" | custom-call | tf_op jit(solution)/shard_map/pallas_call | solution.py:35
  38.5 10.3 %all-to-all-start.1 = ((bf16[256,128,128]{2,1,0:T(8,128)(2,1)}), bf16[256,128,128]{2,1,0:T(8,128)(2,1)}, u32[]{:S(2)}, u32[]{:S(2)}) async-start(bf16[256,128,128]{2,1,0:T(8,128)(2,1)} %shard_map.68), calls=%async_computation.1 | async-start | bytes 16777216 | tf_op jit(solution)/shard_map/all_to_all | solution.py:138
  48.8 4.5 %fusion.12 = (bf16[2048,512]{1,0:T(8,128)(2,1)}, bf16[2048,512]{1,0:T(8,128)(2,1)}) fusion(bf16[2048,1024]{1,0:T(8,128)(2,1)} %param.9), kind=kLoop, calls=%fused_computation.44 | loop fusion | bytes 8388608 | tf_op jit(solution)/shard_map/slice | solution.py:149
  53.7 1.4 scatter_custom_fusion.1
  55.1 0.6 slice.33.cell_ref
  55.7 99.2 %all-to-all-done.1.inc_ref = bf16[256,128,128]{2,1,0:T(8,128)(2,1)} async-done(((bf16[256,128,128]{2,1,0:T(8,128)(2,1)}), bf16[256,128,128]{2,1,0:T(8,128)(2,1)}, u32[]{:S(2)}, u32[]{:S(2)}) %all-to-all-start.1) | async-done | bytes 8388640 | tf_op jit(solution)/shard_map/all_to_all | solution.py:138
  155.0 16.7 %shard_map.69.ov_ref = bf16[128,128,128]{2,1,0:T(8,128)(2,1)} custom-call(s32[256]{0:T(256)} %bitcast.32, bf16[256,128,128]{2,1,0:T(8,128)(2,1)} %all-to-all-done.1.inc_ref), custom_call_target="tpu_custom_call" | custom-call | tf_op jit(solution)/shard_map/pallas_call | solution.py:64
  171.7 28.1 %shard_map.70 = f32[32,128,512]{2,1,0:T(8,128)} custom-call(s32[512]{0:T(512)} %slice.33.cell_ref, bf16[128,128,128]{2,1,0:T(8,128)(2,1)} %shard_map.69.ov_ref, bf16[2048,512]{1,0:T(8,128)(2,1)} %get-tuple-element.2.int_ref), custom_call_target="tpu_custom_call" | custom-call | tf_op jit(solution)/shard_map/pallas_call | solution.py:102
  199.8 28.1 %shard_map.71 = f32[32,128,512]{2,1,0:T(8,128)} custom-call(s32[512]{0:T(512)} %slice.33.cell_ref, bf16[128,128,128]{2,1,0:T(8,128)(2,1)} %shard_map.69.ov_ref, bf16[2048,512]{1,0:T(8,128)(2,1)} %get-tuple-element.3.int_ref), custom_call_target="tpu_custom_call" | custom-call | tf_op jit(solution)/shard_map/pallas_call | solution.py:102
  227.9 64.1 %reduce-scatter.3.cloned.1.call-done = f32[128,512]{1,0:T(8,128)} async-done(((f32[4096,512]{1,0:T(8,128)}), f32[128,512]{1,0:T(8,128)}) %reduce-scatter.3.cloned.1.call-update) | async-done | bytes 262160 | tf_op jit(solution)/shard_map/reduce_scatter | solution.py:151
  292.1 96.2 %reduce-scatter.5.cloned.1.call-done = f32[128,512]{1,0:T(8,128)} async-done(((f32[4096,512]{1,0:T(8,128)}), f32[128,512]{1,0:T(8,128)}) %reduce-scatter.5.cloned.1.call-update) | async-done | bytes 262160 | tf_op jit(solution)/shard_map/reduce_scatter | solution.py:151
  388.3 1.9 pad_maximum_fusion
  (26 shorter events, 1.2 us)
Async XLA Ops:
  15.4 23.0 %all-to-all-start = ((s32[128,2,3]{2,1,0:T(2,128)}), s32[128,2,3]{2,1,0:T(2,128)S(1)}, u32[]{:S(2)}, u32[]{:S(2)}) async-start(s32[128,2,3]{2,1,0:T(2,128)} %select_select_fusion), calls=%async_computation | async-start | bytes 262144 | tf_op jit(solution)/shard_map/all_to_all | solution.py:137
  38.5 116.5 %all-to-all-start.1 = ((bf16[256,128,128]{2,1,0:T(8,128)(2,1)}), bf16[256,128,128]{2,1,0:T(8,128)(2,1)}, u32[]{:S(2)}, u32[]{:S(2)}) async-start(bf16[256,128,128]{2,1,0:T(8,128)(2,1)} %shard_map.68), calls=%async_computation.1 | async-start | bytes 16777216 | tf_op jit(solution)/shard_map/all_to_all | solution.py:138
  48.8 243.3 %reduce-scatter.3.cloned.1.call-start = ((), (), s32[]{:S(2)}) async-start(), calls=%async_computation.4 | async-start | bytes 8650752 | tf_op jit(solution)/shard_map/reduce_scatter | solution.py:151
  53.5 101.4 %copy-start = (s32[256,1]{0,1:T(1,128)}, s32[256,1]{0,1:T(1,128)S(1)}, u32[]{:S(2)}) copy-start(s32[256,1]{0,1:T(1,128)S(1)} %copy.24) | copy-start | bytes 3076
  199.8 188.5 %reduce-scatter.5.cloned.1.call-start = ((), (), s32[]{:S(2)}) async-start(), calls=%async_computation.5 | async-start | bytes 8650752 | tf_op jit(solution)/shard_map/reduce_scatter | solution.py:151
Sparse Core Ops, SparseCore 0:
  199.9 92.1 reduce-scatter.2
  296.2 92.0 reduce-scatter.4

commit v3 on v1

--- a/solution.py
+++ b/solution.py
@@ -1,3 +1,5 @@
+import functools
+
 import jax
 import jax.numpy as jnp
 from jax import lax
@@ -41,38 +43,51 @@
     )(src, grid_tiles)
 
 
-def place_kernel(meta_ref, inc_ref, int_ref, ov_ref, part_ref):
-    slots = inc_ref.shape[0]
-    part_ref[...] = jnp.zeros(part_ref.shape, part_ref.dtype)
+def place_kernel(kc_local, pos_ref, cell_ref, inc_ref, it_ref, ov_ref, part_ref, rhs_ref):
+    slots, tile_width, _ = inc_ref.shape
+    zero = jnp.zeros((tile_width, tile_width), inc_ref.dtype)
 
-    def body(i, carry):
-        pos = meta_ref[i]
-        row = meta_ref[slots + i]
-        col = meta_ref[2 * slots + i]
+    def place(i, carry):
+        pos = pos_ref[i]
 
         @pl.when(pos >= 0)
         def _():
-            tile_t = inc_ref[i].T
-            ov_ref[pos] = tile_t
-            part_ref[row] += jnp.dot(
-                tile_t, int_ref[col], preferred_element_type=jnp.float32
-            )
+            ov_ref[jnp.maximum(pos, 0)] = inc_ref[i].T
 
         return carry
 
-    lax.fori_loop(0, slots, body, 0)
+    lax.fori_loop(0, slots, place, 0)
+
+    def row(r, carry):
+        for kc in range(kc_local):
+            s = cell_ref[r * kc_local + kc]
+            block = pl.ds(kc * tile_width, tile_width)
+
+            @pl.when(s >= 0)
+            def _():
+                rhs_ref[block, :] = inc_ref[jnp.maximum(s, 0)]
+
+            @pl.when(s < 0)
+            def _():
+                rhs_ref[block, :] = zero
+
+        part_ref[r] = jnp.dot(it_ref[...], rhs_ref[...], preferred_element_type=jnp.float32)
+        return carry
+
+    lax.fori_loop(0, part_ref.shape[0], row, 0)
 
 
-def place_and_contract(meta, incoming, int_table, owned, rows):
+def place_and_contract(pos, cell, incoming, it_all, owned, rows, kc_local):
     tile_width = incoming.shape[1]
-    columns = int_table.shape[2]
+    columns = it_all.shape[0]
     return pl.pallas_call(
-        place_kernel,
+        functools.partial(place_kernel, kc_local),
         out_shape=(
             jax.ShapeDtypeStruct((owned, tile_width, tile_width), incoming.dtype),
-            jax.ShapeDtypeStruct((rows, tile_width, columns), jnp.float32),
+            jax.ShapeDtypeStruct((rows, columns, tile_width), jnp.float32),
         ),
         in_specs=[
+            pl.BlockSpec(memory_space=pltpu.SMEM),
             pl.BlockSpec(memory_space=pltpu.SMEM),
             pl.BlockSpec(memory_space=pltpu.VMEM),
             pl.BlockSpec(memory_space=pltpu.VMEM),
@@ -81,8 +96,9 @@
             pl.BlockSpec(memory_space=pltpu.VMEM),
             pl.BlockSpec(memory_space=pltpu.VMEM),
         ),
+        scratch_shapes=[pltpu.VMEM((kc_local * tile_width, tile_width), incoming.dtype)],
         compiler_params=pltpu.CompilerParams(vmem_limit_bytes=VMEM_LIMIT),
-    )(meta, incoming, int_table)
+    )(pos, cell, incoming, it_all)
 
 
 def on_device(grid_tiles, tile_rows, tile_cols, tile_owner, integrals):
@@ -93,7 +109,6 @@
     owned = slot_count // 2
     capacity = slot_count // devices
     kc_local = integrals.shape[0] // tile_width
-    int_table = integrals.reshape(kc_local, tile_width, integrals.shape[1])
     live_slots = tile_owner >= 0
     target = jnp.where(live_slots, tile_owner // owned, devices)
     matches = (target[:, None] == jnp.arange(devices, dtype=jnp.int32)[None, :]).astype(jnp.int32)
@@ -111,10 +126,16 @@
     incoming = lax.all_to_all(
         departing_tiles, ("opair", "vpair"), split_axis=0, concat_axis=0, tiled=True
     )
-    meta = jnp.transpose(arrived).reshape(-1)
-    ov_tiles, partial_value = place_and_contract(meta, incoming, int_table, owned, RT_OP)
-    partial_value = partial_value.reshape(RT_OP * tile_width, int_table.shape[2])
-    cycle_sum = lax.psum_scatter(partial_value, "vpair", scatter_dimension=0, tiled=True)
+    pos = arrived[:, 0]
+    cell_id = jnp.where(pos >= 0, arrived[:, 1] * kc_local + arrived[:, 2], RT_OP * kc_local)
+    slot_ids = jnp.arange(slot_count, dtype=jnp.int32)
+    cell = jnp.full((RT_OP * kc_local + 1,), -1, jnp.int32).at[cell_id].set(slot_ids)[: RT_OP * kc_local]
+    it_all = jnp.transpose(integrals)
+    ov_tiles, partial_t = place_and_contract(pos, cell, incoming, it_all, owned, RT_OP, kc_local)
+    columns = integrals.shape[1]
+    partial_t = partial_t.reshape(RT_OP * columns, tile_width)
+    cycle_t = lax.psum_scatter(partial_t, "vpair", scatter_dimension=0, tiled=True)
+    cycle_sum = jnp.transpose(cycle_t)
     return (ov_tiles, cycle_sum)
 
 

time: 324 us -> 363 us (1.12)
  local copies, waits for them, and re-layouts: 3.4 us -> 29 us
  Pallas kernels: 59.2 us -> 80.6 us
  waiting for transfers between devices: 220 us -> 212 us
    pallas_call x1, Pallas kernels: 47.2 us -> 68.7 us  [place_and_contract(): pl.pallas_call(functools.partial(place_kernel, kc_local), out_shape=(jax....]
    reshape x1, local copies, waits for them, and re-layouts: 0.62 us -> 17.4 us  [on_device(): partial_t = partial_t.reshape(RT_OP * columns, tile_width)]
    all_to_all x1, waiting for transfers between devices: 105 us -> 97.2 us  [on_device(): lax.all_to_all(departing_tiles, ('opair', 'vpair'), split_axis=0, concat_...]
    unnamed x1 -> x7, local copies, waits for them, and re-layouts: 0.01 us -> 6.73 us
  transfers between devices with their start and end apart: 3 -> 3, of which waited for: 2 -> 2; matrix products, arithmetic and copies ran while one was open for 0% -> 2% of each run, Pallas kernels for 4% -> 3%
where the time goes in v3:
time: 363 us
  waiting for transfers between devices  212 us (58%)
  Pallas kernels  80.6 us (22%)
  local copies, waits for them, and re-layouts  29 us (8%)
  starting transfers between devices  21.5 us (6%)
  between operations  14.1 us (4%)
  other arithmetic  5.47 us (2%)
    reduce_scatter x1, waiting for transfers between devices, on_device(): lax.psum_scatter(partial_t, 'vpair', scatter_dimension=0, tiled=True)  115 us
    all_to_all x1, waiting for transfers between devices, on_device(): lax.all_to_all(departing_tiles, ('opair', 'vpair'), split_axis=0, concat_...  97.2 us
    pallas_call x1, Pallas kernels, place_and_contract(): pl.pallas_call(functools.partial(place_kernel, kc_local), out_shape=(jax....  68.7 us
    reshape x1, local copies, waits for them, and re-layouts, on_device(): partial_t = partial_t.reshape(RT_OP * columns, tile_width)  17.4 us
    pallas_call x1, Pallas kernels, gather_tiles(): pl.pallas_call(gather_kernel, out_shape=jax.ShapeDtypeStruct(grid_tiles.s...  11.9 us
    all_to_all x1, starting transfers between devices, on_device(): lax.all_to_all(labels, ('opair', 'vpair'), split_axis=0, concat_axis=0, t...  11.1 us
    all_to_all x1, starting transfers between devices, on_device(): lax.all_to_all(departing_tiles, ('opair', 'vpair'), split_axis=0, concat_...  10.4 us
  transfers between devices with their start and end apart: 3, of which 2 were waited for; matrix products, arithmetic and copies ran while one was open for 2% of the time, Pallas kernels for 3%

profile of v3, /device:TPU:0, one launch (start us, length us, event | category | flops | bytes accessed | tf_op | source)
XLA Modules:
  0.0 362.8 jit_solution(11926140035877010281)
XLA Ops:
  7.2 0.7 fusion.14
  7.9 0.7 fusion.11
  8.7 0.2 fusion
  9.0 0.2 fusion.2
  9.1 0.7 compare_select_fusion.2
  9.8 1.4 scatter_custom_fusion
  11.3 0.6 fusion.13
  11.8 0.7 and_select_fusion.1
  12.5 0.7 and_select_fusion
  13.2 0.2 ge.21
  13.4 0.2 le.15
  13.5 0.1 copy.27
  13.7 0.7 gather_fusion
  14.4 1.0 select_select_fusion
  15.4 11.1 %all-to-all-start = ((s32[128,2,3]{2,1,0:T(2,128)}), s32[128,2,3]{2,1,0:T(2,128)S(1)}, u32[]{:S(2)}, u32[]{:S(2)}) async-start(s32[128,2,3]{2,1,0:T(2,128)} %select_select_fusion), calls=%async_computation | async-start | bytes 262144 | tf_op jit(solution)/shard_map/all_to_all | solution.py:125
  26.6 11.9 %shard_map.68 = bf16[256,128,128]{2,1,0:T(8,128)(2,1)} custom-call(s32[256]{0:T(256)} %get-tuple-element.9.src_ref, bf16[256,128,128]{2,1,0:T(8,128)(2,1)} %grid_ref.1), custom_call_target="tpu_custom_call" | custom-call | tf_op jit(solution)/shard_map/pallas_call | solution.py:34
  38.5 10.4 %all-to-all-start.1 = ((bf16[256,128,128]{2,1,0:T(8,128)(2,1)}), bf16[256,128,128]{2,1,0:T(8,128)(2,1)}, u32[]{:S(2)}, u32[]{:S(2)}) async-start(bf16[256,128,128]{2,1,0:T(8,128)(2,1)} %shard_map.68), calls=%async_computation.1 | async-start | bytes 16777216 | tf_op jit(solution)/shard_map/all_to_all | solution.py:126
  48.9 6.5 %copy.29 = bf16[2048,1024]{0,1:T(8,128)(2,1)} copy(bf16[2048,1024]{1,0:T(8,128)(2,1)} %param.9) | data formatting | bytes 8388608 | tf_op args[4]
  55.7 1.4 scatter_custom_fusion.1
  57.2 0.6 slice.27.cell_ref
  57.7 97.2 %all-to-all-done.1.inc_ref = bf16[256,128,128]{2,1,0:T(8,128)(2,1)} async-done(((bf16[256,128,128]{2,1,0:T(8,128)(2,1)}), bf16[256,128,128]{2,1,0:T(8,128)(2,1)}, u32[]{:S(2)}, u32[]{:S(2)}) %all-to-all-start.1) | async-done | bytes 8388640 | tf_op jit(solution)/shard_map/all_to_all | solution.py:126
  155.0 68.7 %shard_map.69 = (bf16[128,128,128]{2,1,0:T(8,128)(2,1)}, f32[32,1024,128]{2,1,0:T(8,128)}) custom-call(s32[256]{0:T(256)} %bitcast.34, s32[512]{0:T(512)} %slice.27.cell_ref, bf16[256,128,128]{2,1,0:T(8,128)(2,1)} %all-to-all-done.1.inc_ref, bf16[1024,2048]{1,0:T(8,128)(2,1)} %bitcast.28), custom_call_target="tpu_custom_call" | custom-call | tf_op jit(solution)/shard_map/pallas_call | solution.py:83
  223.7 17.4 %copy.30 = f32[32768,128]{0,1:T(8,128)} copy(f32[32768,128]{1,0:T(8,128)} %bitcast.27) | data formatting | bytes 33554432 | tf_op jit(solution)/shard_map/reshape | solution.py:136
  241.2 114.8 %reduce-scatter.2.cloned.1.call-done = f32[1024,128]{0,1:T(8,128)} async-done(((f32[32768,128]{0,1:T(8,128)}), f32[1024,128]{0,1:T(8,128)}) %reduce-scatter.2.cloned.1.call-update) | async-done | bytes 524304 | tf_op jit(solution)/shard_map/reduce_scatter | solution.py:137
  (22 shorter events, 0.7 us)
Async XLA Ops:
  15.4 23.0 %all-to-all-start = ((s32[128,2,3]{2,1,0:T(2,128)}), s32[128,2,3]{2,1,0:T(2,128)S(1)}, u32[]{:S(2)}, u32[]{:S(2)}) async-start(s32[128,2,3]{2,1,0:T(2,128)} %select_select_fusion), calls=%async_computation | async-start | bytes 262144 | tf_op jit(solution)/shard_map/all_to_all | solution.py:125
  38.5 116.5 %all-to-all-start.1 = ((bf16[256,128,128]{2,1,0:T(8,128)(2,1)}), bf16[256,128,128]{2,1,0:T(8,128)(2,1)}, u32[]{:S(2)}, u32[]{:S(2)}) async-start(bf16[256,128,128]{2,1,0:T(8,128)(2,1)} %shard_map.68), calls=%async_computation.1 | async-start | bytes 16777216 | tf_op jit(solution)/shard_map/all_to_all | solution.py:126
  48.8 307.2 %reduce-scatter.2.cloned.1.call-start = ((), (), s32[]{:S(2)}) async-start(), calls=%async_computation.3 | async-start | bytes 17301504 | tf_op jit(solution)/shard_map/reduce_scatter | solution.py:137
  55.6 99.4 %copy-start = (s32[256,1]{0,1:T(1,128)}, s32[256,1]{0,1:T(1,128)S(1)}, u32[]{:S(2)}) copy-start(s32[256,1]{0,1:T(1,128)S(1)} %copy.32) | copy-start | bytes 3076
Sparse Core Ops, SparseCore 0:
  241.3 114.6 reduce-scatter.1

commit v4 on v1

--- a/solution.py
+++ b/solution.py
@@ -1,3 +1,5 @@
+import functools
+
 import jax
 import jax.numpy as jnp
 from jax import lax
@@ -6,6 +8,8 @@
 from jax.sharding import PartitionSpec as P
 
 RT_OP = 32
+QUARTERS = 4
+MESH = pl.DeviceIdType.MESH
 VMEM_LIMIT = 60 * 1024 * 1024
 
 
@@ -41,8 +45,19 @@
     )(src, grid_tiles)
 
 
-def place_kernel(meta_ref, inc_ref, int_ref, ov_ref, part_ref):
+def storage_row(q, row, ring):
+    c = row % 2
+    y = (row // 2) % ring
+    z = row // (2 * ring)
+    half = ring * ring
+    if q < 2:
+        return c * half + y * ring + z
+    return c * half + z * ring + y
+
+
+def place_kernel(quarters, ring, meta_ref, inc_ref, int_ref, ov_ref, part_ref):
     slots = inc_ref.shape[0]
+    width = part_ref.shape[3]
     part_ref[...] = jnp.zeros(part_ref.shape, part_ref.dtype)
 
     def body(i, carry):
@@ -53,24 +68,25 @@
         @pl.when(pos >= 0)
         def _():
             tile_t = inc_ref[i].T
-            ov_ref[pos] = tile_t
-            part_ref[row] += jnp.dot(
-                tile_t, int_ref[col], preferred_element_type=jnp.float32
-            )
+            ov_ref[jnp.maximum(pos, 0)] = tile_t
+            prod = jnp.dot(tile_t, int_ref[jnp.maximum(col, 0)], preferred_element_type=jnp.float32)
+            for q in range(quarters):
+                s = storage_row(q, jnp.maximum(row, 0), ring)
+                part_ref[q, s] += prod[:, q * width : (q + 1) * width]
 
         return carry
 
     lax.fori_loop(0, slots, body, 0)
 
 
-def place_and_contract(meta, incoming, int_table, owned, rows):
+def place_and_contract(meta, incoming, int_table, owned, rows, quarters, ring):
     tile_width = incoming.shape[1]
     columns = int_table.shape[2]
     return pl.pallas_call(
-        place_kernel,
+        functools.partial(place_kernel, quarters, ring),
         out_shape=(
             jax.ShapeDtypeStruct((owned, tile_width, tile_width), incoming.dtype),
-            jax.ShapeDtypeStruct((rows, tile_width, columns), jnp.float32),
+            jax.ShapeDtypeStruct((quarters, rows, tile_width, columns // quarters), jnp.float32),
         ),
         in_specs=[
             pl.BlockSpec(memory_space=pltpu.SMEM),
@@ -83,6 +99,147 @@
         ),
         compiler_params=pltpu.CompilerParams(vmem_limit_bytes=VMEM_LIMIT),
     )(meta, incoming, int_table)
+
+
+def rs_kernel(ring, part_ref, out_ref, core_buf, red, rbuf1, acc1, fin1, rbuf2, acc2,
+              core_send, core_recv, send1, recv1, send2, recv2):
+    quarters, rows, tile_width, width = part_ref.shape
+    half = rows // 2
+    steps = ring - 1
+    op = lax.axis_index("opair")
+    v = lax.axis_index("vpair")
+    c = v % 2
+    y = (v // 2) % ring
+    z = v // (2 * ring)
+
+    def dev(zz, yy, cc):
+        return (op, (zz * ring + yy) * 2 + cc)
+
+    sib = dev(z, y, 1 - c)
+    y_up = dev(z, (y + 1) % ring, c)
+    y_dn = dev(z, (y + ring - 1) % ring, c)
+    z_up = dev((z + 1) % ring, y, c)
+    z_dn = dev((z + ring - 1) % ring, y, c)
+
+    barrier = pltpu.get_barrier_semaphore()
+    for peer in (sib, y_up, y_dn, z_up, z_dn):
+        pl.semaphore_signal(barrier, inc=1, device_id=peer, device_id_type=MESH)
+    pl.semaphore_wait(barrier, 5)
+
+    core_copy = pltpu.make_async_remote_copy(
+        src_ref=part_ref.at[:, pl.ds((1 - c) * half, half)],
+        dst_ref=core_buf,
+        send_sem=core_send,
+        recv_sem=core_recv,
+        device_id=sib,
+        device_id_type=MESH,
+    )
+    core_copy.start()
+    core_copy.wait()
+
+    def core_sum(k, carry):
+        q = k // half
+        i = k % half
+        red[q, i] = part_ref[q, c * half + i] + core_buf[q, i]
+        return carry
+
+    lax.fori_loop(0, quarters * half, core_sum, 0)
+
+    def plan(q):
+        d = 1 if q % 2 == 0 else -1
+        if q < 2:
+            return d, y, z, (y_up if d > 0 else y_dn), (z_up if d > 0 else z_dn)
+        return d, z, y, (z_up if d > 0 else z_dn), (y_up if d > 0 else y_dn)
+
+    for s in range(steps):
+        copies = []
+        for q in range(quarters):
+            d, a, b, first, second = plan(q)
+            blk = (a - d * (s + 1) + 2 * ring) % ring
+            if s == 0:
+                src = red.at[q, pl.ds(blk * ring, ring)]
+            else:
+                src = acc1.at[q, s - 1]
+            cp = pltpu.make_async_remote_copy(
+                src_ref=src,
+                dst_ref=rbuf1.at[q, s],
+                send_sem=send1.at[q, s],
+                recv_sem=recv1.at[q, s],
+                device_id=first,
+                device_id_type=MESH,
+            )
+            cp.start()
+            copies.append(cp)
+        for q in range(quarters):
+            copies[q].wait()
+            d, a, b, first, second = plan(q)
+            blk = (a - d * (s + 2) + 3 * ring) % ring
+            for j in range(ring):
+                total = rbuf1[q, s, j] + red[q, blk * ring + j]
+                if s < steps - 1:
+                    acc1[q, s, j] = total
+                else:
+                    fin1[q, j] = total
+
+    for s in range(steps):
+        copies = []
+        for q in range(quarters):
+            d, a, b, first, second = plan(q)
+            blk = (b - d * (s + 1) + 2 * ring) % ring
+            if s == 0:
+                src = fin1.at[q, blk]
+            else:
+                src = acc2.at[q, s - 1]
+            cp = pltpu.make_async_remote_copy(
+                src_ref=src,
+                dst_ref=rbuf2.at[q, s],
+                send_sem=send2.at[q, s],
+                recv_sem=recv2.at[q, s],
+                device_id=second,
+                device_id_type=MESH,
+            )
+            cp.start()
+            copies.append(cp)
+        for q in range(quarters):
+            copies[q].wait()
+            d, a, b, first, second = plan(q)
+            blk = (b - d * (s + 2) + 3 * ring) % ring
+            total = rbuf2[q, s] + fin1[q, blk]
+            if s < steps - 1:
+                acc2[q, s] = total
+            else:
+                out_ref[:, q * width : (q + 1) * width] = total
+
+
+def reduce_scatter(part, ring):
+    quarters, rows, tile_width, width = part.shape
+    half = rows // 2
+    steps = ring - 1
+    f32 = jnp.float32
+    return pl.pallas_call(
+        functools.partial(rs_kernel, ring),
+        out_shape=jax.ShapeDtypeStruct((tile_width, quarters * width), f32),
+        in_specs=[pl.BlockSpec(memory_space=pltpu.VMEM)],
+        out_specs=pl.BlockSpec(memory_space=pltpu.VMEM),
+        scratch_shapes=[
+            pltpu.VMEM((quarters, half, tile_width, width), f32),
+            pltpu.VMEM((quarters, half, tile_width, width), f32),
+            pltpu.VMEM((quarters, steps, ring, tile_width, width), f32),
+            pltpu.VMEM((quarters, steps - 1, ring, tile_width, width), f32),
+            pltpu.VMEM((quarters, ring, tile_width, width), f32),
+            pltpu.VMEM((quarters, steps, tile_width, width), f32),
+            pltpu.VMEM((quarters, steps - 1, tile_width, width), f32),
+            pltpu.SemaphoreType.DMA(()),
+            pltpu.SemaphoreType.DMA(()),
+            pltpu.SemaphoreType.DMA((quarters, steps)),
+            pltpu.SemaphoreType.DMA((quarters, steps)),
+            pltpu.SemaphoreType.DMA((quarters, steps)),
+            pltpu.SemaphoreType.DMA((quarters, steps)),
+        ],
+        compiler_params=pltpu.CompilerParams(
+            collective_id=0, has_side_effects=True, vmem_limit_bytes=VMEM_LIMIT
+        ),
+    )(part)
 
 
 def on_device(grid_tiles, tile_rows, tile_cols, tile_owner, integrals):
@@ -112,9 +269,11 @@
         departing_tiles, ("opair", "vpair"), split_axis=0, concat_axis=0, tiled=True
     )
     meta = jnp.transpose(arrived).reshape(-1)
-    ov_tiles, partial_value = place_and_contract(meta, incoming, int_table, owned, RT_OP)
-    partial_value = partial_value.reshape(RT_OP * tile_width, int_table.shape[2])
-    cycle_sum = lax.psum_scatter(partial_value, "vpair", scatter_dimension=0, tiled=True)
+    ring = 4
+    ov_tiles, partial_value = place_and_contract(
+        meta, incoming, int_table, owned, RT_OP, QUARTERS, ring
+    )
+    cycle_sum = reduce_scatter(partial_value, ring)
     return (ov_tiles, cycle_sum)
 
 

time: 324 us -> 280 us (0.86)
  waiting for transfers between devices: 220 us -> 105 us
  Pallas kernels: 59.2 us -> 142 us
  between operations: 14.1 us -> 0.73 us
    reduce_scatter x1 -> x0, waiting for transfers between devices: 115 us -> none  [on_device(): lax.psum_scatter(partial_value, 'vpair', scatter_dimension=0, tiled=True)]
    pallas_call x1 -> x2, Pallas kernels: 47.2 us -> 130 us  [the longest x1 82.3 us: reduce_scatter(): pl.pallas_call(functools.partial(rs_kernel, ring), out_shape=jax.ShapeDty...]
  transfers between devices with their start and end apart: 3 -> 2, of which waited for: 2 -> 1; matrix products, arithmetic and copies ran while one was open for 0% -> 0% of each run, Pallas kernels for 4% -> 4%
where the time goes in v4:
time: 280 us
  Pallas kernels  142 us (51%)
  waiting for transfers between devices  105 us (38%)
  starting transfers between devices  21.4 us (8%)
  other arithmetic  5.46 us (2%)
  local copies, waits for them, and re-layouts  5.29 us (2%)
    all_to_all x1, waiting for transfers between devices, on_device(): lax.all_to_all(departing_tiles, ('opair', 'vpair'), split_axis=0, concat_...  105 us
    pallas_call x1, Pallas kernels, reduce_scatter(): pl.pallas_call(functools.partial(rs_kernel, ring), out_shape=jax.ShapeDty...  82.3 us
    pallas_call x1, Pallas kernels, place_and_contract(): pl.pallas_call(functools.partial(place_kernel, quarters, ring), out_shape...  47.3 us
    pallas_call x1, Pallas kernels, gather_tiles(): pl.pallas_call(gather_kernel, out_shape=jax.ShapeDtypeStruct(grid_tiles.s...  11.9 us
    all_to_all x1, starting transfers between devices, on_device(): lax.all_to_all(labels, ('opair', 'vpair'), split_axis=0, concat_axis=0, t...  11.1 us
    all_to_all x1, starting transfers between devices, on_device(): lax.all_to_all(departing_tiles, ('opair', 'vpair'), split_axis=0, concat_...  10.3 us
  transfers between devices with their start and end apart: 2, of which 1 were waited for; matrix products, arithmetic and copies ran while one was open for 0% of the time, Pallas kernels for 4%

profile of v4, /device:TPU:0, one launch (start us, length us, event | category | flops | bytes accessed | tf_op | source)
XLA Modules:
  0.0 280.0 jit_solution(8175267268247486435)
XLA Ops:
  0.6 0.7 fusion.11
  1.3 0.7 fusion.9
  2.0 0.1 copy.19
  2.1 0.2 fusion
  2.4 0.2 fusion.2
  2.6 0.7 compare_select_fusion
  3.3 1.4 scatter_custom_fusion
  4.7 0.6 fusion.10
  5.3 0.7 and_select_fusion.1
  6.0 0.7 and_select_fusion
  6.7 0.2 ge.17
  6.8 0.2 le.15
  7.0 0.1 copy.21
  7.2 0.7 gather_fusion
  7.9 1.0 select_select_fusion
  8.9 11.1 %all-to-all-start = ((s32[128,2,3]{2,1,0:T(2,128)}), s32[128,2,3]{2,1,0:T(2,128)S(1)}, u32[]{:S(2)}, u32[]{:S(2)}) async-start(s32[128,2,3]{2,1,0:T(2,128)} %select_select_fusion), calls=%async_computation | async-start | bytes 262144 | tf_op jit(solution)/shard_map/all_to_all | solution.py:267
  20.0 11.9 %shard_map.68 = bf16[256,128,128]{2,1,0:T(8,128)(2,1)} custom-call(s32[256]{0:T(256)} %get-tuple-element.6.src_ref, bf16[256,128,128]{2,1,0:T(8,128)(2,1)} %grid_ref.1), custom_call_target="tpu_custom_call" | custom-call | tf_op jit(solution)/shard_map/pallas_call | solution.py:36
  32.0 10.3 %all-to-all-start.1 = ((bf16[256,128,128]{2,1,0:T(8,128)(2,1)}), bf16[256,128,128]{2,1,0:T(8,128)(2,1)}, u32[]{:S(2)}, u32[]{:S(2)}) async-start(bf16[256,128,128]{2,1,0:T(8,128)(2,1)} %shard_map.68), calls=%async_computation.1 | async-start | bytes 16777216 | tf_op jit(solution)/shard_map/all_to_all | solution.py:268
  42.3 0.1 copy.23
  42.3 0.6 reshape.54.meta_ref
  42.9 105.5 %all-to-all-done.1.inc_ref = bf16[256,128,128]{2,1,0:T(8,128)(2,1)} async-done(((bf16[256,128,128]{2,1,0:T(8,128)(2,1)}), bf16[256,128,128]{2,1,0:T(8,128)(2,1)}, u32[]{:S(2)}, u32[]{:S(2)}) %all-to-all-start.1) | async-done | bytes 8388640 | tf_op jit(solution)/shard_map/all_to_all | solution.py:268
  148.4 47.3 %shard_map.69 = (bf16[128,128,128]{2,1,0:T(8,128)(2,1)}, f32[4,32,128,256]{3,2,1,0:T(8,128)}) custom-call(s32[768]{0:T(1024)} %reshape.54.meta_ref, bf16[256,128,128]{2,1,0:T(8,128)(2,1)} %all-to-all-done.1.inc_ref, bf16[16,128,1024]{2,1,0:T(8,128)(2,1)} %bitcast.23), custom_call_target="tpu_custom_call" | custom-call | tf_op jit(solution)/shard_map/pallas_call | solution.py:85
  195.8 82.3 %shard_map.70 = f32[128,1024]{1,0:T(8,128)} custom-call(f32[4,32,128,256]{3,2,1,0:T(8,128)} %get-tuple-element.5.part_ref), custom_call_target="tpu_custom_call" | custom-call | tf_op jit(solution)/shard_map/pallas_call | solution.py:219
  278.1 1.9 copy.25
  (11 shorter events, 0.1 us)
Async XLA Ops:
  8.9 23.1 %all-to-all-start = ((s32[128,2,3]{2,1,0:T(2,128)}), s32[128,2,3]{2,1,0:T(2,128)S(1)}, u32[]{:S(2)}, u32[]{:S(2)}) async-start(s32[128,2,3]{2,1,0:T(2,128)} %select_select_fusion), calls=%async_computation | async-start | bytes 262144 | tf_op jit(solution)/shard_map/all_to_all | solution.py:267
  32.0 116.5 %all-to-all-start.1 = ((bf16[256,128,128]{2,1,0:T(8,128)(2,1)}), bf16[256,128,128]{2,1,0:T(8,128)(2,1)}, u32[]{:S(2)}, u32[]{:S(2)}) async-start(bf16[256,128,128]{2,1,0:T(8,128)(2,1)} %shard_map.68), calls=%async_computation.1 | async-start | bytes 16777216 | tf_op jit(solution)/shard_map/all_to_all | solution.py:268

commit v5 on v4

--- a/solution.py
+++ b/solution.py
@@ -57,7 +57,7 @@
 
 def place_kernel(quarters, ring, meta_ref, inc_ref, int_ref, ov_ref, part_ref):
     slots = inc_ref.shape[0]
-    width = part_ref.shape[3]
+    width = part_ref.shape[2]
     part_ref[...] = jnp.zeros(part_ref.shape, part_ref.dtype)
 
     def body(i, carry):
@@ -67,12 +67,12 @@
 
         @pl.when(pos >= 0)
         def _():
-            tile_t = inc_ref[i].T
-            ov_ref[jnp.maximum(pos, 0)] = tile_t
-            prod = jnp.dot(tile_t, int_ref[jnp.maximum(col, 0)], preferred_element_type=jnp.float32)
+            tile = inc_ref[i]
+            ov_ref[jnp.maximum(pos, 0)] = tile.T
+            prod = jnp.dot(int_ref[jnp.maximum(col, 0)], tile, preferred_element_type=jnp.float32)
             for q in range(quarters):
                 s = storage_row(q, jnp.maximum(row, 0), ring)
-                part_ref[q, s] += prod[:, q * width : (q + 1) * width]
+                part_ref[q, s] += prod[q * width : (q + 1) * width, :]
 
         return carry
 
@@ -81,12 +81,12 @@
 
 def place_and_contract(meta, incoming, int_table, owned, rows, quarters, ring):
     tile_width = incoming.shape[1]
-    columns = int_table.shape[2]
+    columns = int_table.shape[1]
     return pl.pallas_call(
         functools.partial(place_kernel, quarters, ring),
         out_shape=(
             jax.ShapeDtypeStruct((owned, tile_width, tile_width), incoming.dtype),
-            jax.ShapeDtypeStruct((quarters, rows, tile_width, columns // quarters), jnp.float32),
+            jax.ShapeDtypeStruct((quarters, rows, columns // quarters, tile_width), jnp.float32),
         ),
         in_specs=[
             pl.BlockSpec(memory_space=pltpu.SMEM),
@@ -208,7 +208,7 @@
             if s < steps - 1:
                 acc2[q, s] = total
             else:
-                out_ref[:, q * width : (q + 1) * width] = total
+                out_ref[q] = total
 
 
 def reduce_scatter(part, ring):
@@ -218,7 +218,7 @@
     f32 = jnp.float32
     return pl.pallas_call(
         functools.partial(rs_kernel, ring),
-        out_shape=jax.ShapeDtypeStruct((tile_width, quarters * width), f32),
+        out_shape=jax.ShapeDtypeStruct((quarters, tile_width, width), f32),
         in_specs=[pl.BlockSpec(memory_space=pltpu.VMEM)],
         out_specs=pl.BlockSpec(memory_space=pltpu.VMEM),
         scratch_shapes=[
@@ -250,7 +250,7 @@
     owned = slot_count // 2
     capacity = slot_count // devices
     kc_local = integrals.shape[0] // tile_width
-    int_table = integrals.reshape(kc_local, tile_width, integrals.shape[1])
+    int_table = jnp.swapaxes(integrals.reshape(kc_local, tile_width, integrals.shape[1]), 1, 2)
     live_slots = tile_owner >= 0
     target = jnp.where(live_slots, tile_owner // owned, devices)
     matches = (target[:, None] == jnp.arange(devices, dtype=jnp.int32)[None, :]).astype(jnp.int32)
@@ -273,7 +273,8 @@
     ov_tiles, partial_value = place_and_contract(
         meta, incoming, int_table, owned, RT_OP, QUARTERS, ring
     )
-    cycle_sum = reduce_scatter(partial_value, ring)
+    cycle_t = reduce_scatter(partial_value, ring)
+    cycle_sum = jnp.transpose(cycle_t.reshape(-1, tile_width))
     return (ov_tiles, cycle_sum)
 
 

time: 280 us -> 279 us (level)
  local copies, waits for them, and re-layouts: 5.29 us -> 11.8 us
  waiting for transfers between devices: 105 us -> 99.1 us
    reshape x0 -> x2, local copies, waits for them, and re-layouts: none -> 8.41 us  [the longest x1 6.37 us: on_device(): integrals.reshape(kc_local, tile_width, integrals.shape[1])]
    all_to_all x1, waiting for transfers between devices: 105 us -> 99.1 us  [on_device(): lax.all_to_all(departing_tiles, ('opair', 'vpair'), split_axis=0, concat_...]
  transfers between devices with their start and end apart: 2 -> 2, of which waited for: 1 -> 1; matrix products, arithmetic and copies ran while one was open for 0% -> 3% of each run, Pallas kernels for 4% -> 4%
where the time goes in v5:
time: 279 us; the launch traced here: 278 us
  Pallas kernels  140 us (50%)
  waiting for transfers between devices  99.1 us (36%)
  starting transfers between devices  21.5 us (8%)
  local copies, waits for them, and re-layouts  11.8 us (4%)
  other arithmetic  5.46 us (2%)
    all_to_all x1, waiting for transfers between devices, on_device(): lax.all_to_all(departing_tiles, ('opair', 'vpair'), split_axis=0, concat_...  99.1 us
    pallas_call x1, Pallas kernels, reduce_scatter(): pl.pallas_call(functools.partial(rs_kernel, ring), out_shape=jax.ShapeDty...  82.2 us
    pallas_call x1, Pallas kernels, place_and_contract(): pl.pallas_call(functools.partial(place_kernel, quarters, ring), out_shape...  45.6 us
    pallas_call x1, Pallas kernels, gather_tiles(): pl.pallas_call(gather_kernel, out_shape=jax.ShapeDtypeStruct(grid_tiles.s...  11.9 us
    all_to_all x1, starting transfers between devices, on_device(): lax.all_to_all(labels, ('opair', 'vpair'), split_axis=0, concat_axis=0, t...  11.1 us
    all_to_all x1, starting transfers between devices, on_device(): lax.all_to_all(departing_tiles, ('opair', 'vpair'), split_axis=0, concat_...  10.4 us
    reshape x1, local copies, waits for them, and re-layouts, on_device(): integrals.reshape(kc_local, tile_width, integrals.shape[1])  6.37 us
  transfers between devices with their start and end apart: 2, of which 1 were waited for; matrix products, arithmetic and copies ran while one was open for 3% of the time, Pallas kernels for 4%

profile of v5, /device:TPU:0, one launch (start us, length us, event | category | flops | bytes accessed | tf_op | source)
XLA Modules:
  0.0 278.3 jit_solution(12515152853128980675)
XLA Ops:
  0.6 0.7 fusion.11
  1.3 0.7 fusion.9
  2.0 0.1 copy.24
  2.1 0.2 fusion
  2.4 0.2 fusion.2
  2.6 0.7 compare_select_fusion
  3.3 1.4 scatter_custom_fusion
  4.7 0.6 fusion.10
  5.3 0.7 and_select_fusion.1
  6.0 0.7 and_select_fusion
  6.7 0.2 ge.17
  6.8 0.2 le.15
  7.0 0.1 copy.26
  7.2 0.7 gather_fusion
  7.9 1.0 select_select_fusion
  8.9 11.1 %all-to-all-start = ((s32[128,2,3]{2,1,0:T(2,128)}), s32[128,2,3]{2,1,0:T(2,128)S(1)}, u32[]{:S(2)}, u32[]{:S(2)}) async-start(s32[128,2,3]{2,1,0:T(2,128)} %select_select_fusion), calls=%async_computation | async-start | bytes 262144 | tf_op jit(solution)/shard_map/all_to_all | solution.py:267
  20.0 11.9 %shard_map.68 = bf16[256,128,128]{2,1,0:T(8,128)(2,1)} custom-call(s32[256]{0:T(256)} %get-tuple-element.6.src_ref, bf16[256,128,128]{2,1,0:T(8,128)(2,1)} %grid_ref.1), custom_call_target="tpu_custom_call" | custom-call | tf_op jit(solution)/shard_map/pallas_call | solution.py:36
  31.9 10.4 %all-to-all-start.1 = ((bf16[256,128,128]{2,1,0:T(8,128)(2,1)}), bf16[256,128,128]{2,1,0:T(8,128)(2,1)}, u32[]{:S(2)}, u32[]{:S(2)}) async-start(bf16[256,128,128]{2,1,0:T(8,128)(2,1)} %shard_map.68), calls=%async_computation.1 | async-start | bytes 16777216 | tf_op jit(solution)/shard_map/all_to_all | solution.py:268
  42.3 6.4 %copy.28 = bf16[16,128,1024]{1,2,0:T(8,128)(2,1)} copy(bf16[16,128,1024]{2,1,0:T(8,128)(2,1)} %bitcast.27) | data formatting | bytes 8388608 | tf_op jit(solution)/shard_map/reshape | solution.py:253
  48.7 0.6 reshape.57.meta_ref
  49.3 99.1 %all-to-all-done.1.inc_ref = bf16[256,128,128]{2,1,0:T(8,128)(2,1)} async-done(((bf16[256,128,128]{2,1,0:T(8,128)(2,1)}), bf16[256,128,128]{2,1,0:T(8,128)(2,1)}, u32[]{:S(2)}, u32[]{:S(2)}) %all-to-all-start.1) | async-done | bytes 8388640 | tf_op jit(solution)/shard_map/all_to_all | solution.py:268
  148.4 45.6 %shard_map.69 = (bf16[128,128,128]{2,1,0:T(8,128)(2,1)}, f32[4,32,256,128]{3,2,1,0:T(8,128)}) custom-call(s32[768]{0:T(1024)} %reshape.57.meta_ref, bf16[256,128,128]{2,1,0:T(8,128)(2,1)} %all-to-all-done.1.inc_ref, bf16[16,1024,128]{2,1,0:T(8,128)(2,1)} %bitcast.26), custom_call_target="tpu_custom_call" | custom-call | tf_op jit(solution)/shard_map/pallas_call | solution.py:85
  194.0 82.2 %shard_map.70 = f32[4,256,128]{2,1,0:T(8,128)} custom-call(f32[4,32,256,128]{3,2,1,0:T(8,128)} %get-tuple-element.5.part_ref), custom_call_target="tpu_custom_call" | custom-call | tf_op jit(solution)/shard_map/pallas_call | solution.py:219
  276.2 2.0 copy.29
  (12 shorter events, 0.2 us)
Async XLA Ops:
  8.9 23.0 %all-to-all-start = ((s32[128,2,3]{2,1,0:T(2,128)}), s32[128,2,3]{2,1,0:T(2,128)S(1)}, u32[]{:S(2)}, u32[]{:S(2)}) async-start(s32[128,2,3]{2,1,0:T(2,128)} %select_select_fusion), calls=%async_computation | async-start | bytes 262144 | tf_op jit(solution)/shard_map/all_to_all | solution.py:267
  31.9 116.5 %all-to-all-start.1 = ((bf16[256,128,128]{2,1,0:T(8,128)(2,1)}), bf16[256,128,128]{2,1,0:T(8,128)(2,1)}, u32[]{:S(2)}, u32[]{:S(2)}) async-start(bf16[256,128,128]{2,1,0:T(8,128)(2,1)} %shard_map.68), calls=%async_computation.1 | async-start | bytes 16777216 | tf_op jit(solution)/shard_map/all_to_all | solution.py:268

commit v6 on v5

--- a/solution.py
+++ b/solution.py
@@ -55,41 +55,50 @@
     return c * half + z * ring + y
 
 
-def place_kernel(quarters, ring, meta_ref, inc_ref, int_ref, ov_ref, part_ref):
+def place_kernel(quarters, ring, pos_ref, order_ref, starts_ref, col_ref, inc_ref, int_ref, ov_ref, part_ref):
     slots = inc_ref.shape[0]
+    rows = part_ref.shape[1]
     width = part_ref.shape[2]
-    part_ref[...] = jnp.zeros(part_ref.shape, part_ref.dtype)
-
-    def body(i, carry):
-        pos = meta_ref[i]
-        row = meta_ref[slots + i]
-        col = meta_ref[2 * slots + i]
+
+    def place(i, carry):
+        pos = pos_ref[i]
 
         @pl.when(pos >= 0)
         def _():
-            tile = inc_ref[i]
-            ov_ref[jnp.maximum(pos, 0)] = tile.T
-            prod = jnp.dot(int_ref[jnp.maximum(col, 0)], tile, preferred_element_type=jnp.float32)
-            for q in range(quarters):
-                s = storage_row(q, jnp.maximum(row, 0), ring)
-                part_ref[q, s] += prod[q * width : (q + 1) * width, :]
+            ov_ref[jnp.maximum(pos, 0)] = inc_ref[i].T
 
         return carry
 
-    lax.fori_loop(0, slots, body, 0)
-
-
-def place_and_contract(meta, incoming, int_table, owned, rows, quarters, ring):
+    lax.fori_loop(0, slots, place, 0)
+
+    def row(r, carry):
+        lo = starts_ref[r]
+        hi = starts_ref[r + 1]
+        for q in range(quarters):
+
+            def add(t, acc):
+                i = order_ref[t]
+                block = int_ref[col_ref[i], pl.ds(q * width, width), :]
+                return acc + jnp.dot(block, inc_ref[i], preferred_element_type=jnp.float32)
+
+            acc = lax.fori_loop(lo, hi, add, jnp.zeros(part_ref.shape[2:], jnp.float32))
+            part_ref[q, storage_row(q, r, ring)] = acc
+        return carry
+
+    lax.fori_loop(0, rows, row, 0)
+
+
+def place_and_contract(pos, order, starts, col, incoming, int_table, owned, rows, quarters, ring):
     tile_width = incoming.shape[1]
     columns = int_table.shape[1]
+    smem = pl.BlockSpec(memory_space=pltpu.SMEM)
     return pl.pallas_call(
         functools.partial(place_kernel, quarters, ring),
         out_shape=(
             jax.ShapeDtypeStruct((owned, tile_width, tile_width), incoming.dtype),
             jax.ShapeDtypeStruct((quarters, rows, columns // quarters, tile_width), jnp.float32),
         ),
-        in_specs=[
-            pl.BlockSpec(memory_space=pltpu.SMEM),
+        in_specs=[smem, smem, smem, smem,
             pl.BlockSpec(memory_space=pltpu.VMEM),
             pl.BlockSpec(memory_space=pltpu.VMEM),
         ],
@@ -98,7 +107,7 @@
             pl.BlockSpec(memory_space=pltpu.VMEM),
         ),
         compiler_params=pltpu.CompilerParams(vmem_limit_bytes=VMEM_LIMIT),
-    )(meta, incoming, int_table)
+    )(pos, order, starts, col, incoming, int_table)
 
 
 def rs_kernel(ring, part_ref, out_ref, core_buf, red, rbuf1, acc1, fin1, rbuf2, acc2,
@@ -268,10 +277,19 @@
     incoming = lax.all_to_all(
         departing_tiles, ("opair", "vpair"), split_axis=0, concat_axis=0, tiled=True
     )
-    meta = jnp.transpose(arrived).reshape(-1)
     ring = 4
+    pos = arrived[:, 0]
+    valid = pos >= 0
+    key = jnp.where(valid, arrived[:, 1], RT_OP)
+    slot_ids = jnp.arange(slot_count, dtype=jnp.int32)
+    before = (key[None, :] < key[:, None]) | ((key[None, :] == key[:, None]) & (slot_ids[None, :] < slot_ids[:, None]))
+    rank = jnp.sum(before.astype(jnp.int32), axis=1)
+    order = jnp.zeros((slot_count,), jnp.int32).at[rank].set(slot_ids)
+    row_ids = jnp.arange(RT_OP + 1, dtype=jnp.int32)
+    starts = jnp.sum((key[None, :] < row_ids[:, None]).astype(jnp.int32), axis=1)
+    col = jnp.maximum(arrived[:, 2], 0)
     ov_tiles, partial_value = place_and_contract(
-        meta, incoming, int_table, owned, RT_OP, QUARTERS, ring
+        pos, order, starts, col, incoming, int_table, owned, RT_OP, QUARTERS, ring
     )
     cycle_t = reduce_scatter(partial_value, ring)
     cycle_sum = jnp.transpose(cycle_t.reshape(-1, tile_width))

time: 279 us -> 337 us (1.21)
  Pallas kernels: 140 us -> 198 us
    pallas_call x1, Pallas kernels: 45.6 us -> 104 us  [place_and_contract(): pl.pallas_call(functools.partial(place_kernel, quarters, ring), out_shape...]
where the time goes in v6:
time: 337 us; the launch traced here: 336 us
  Pallas kernels  198 us (59%)
  waiting for transfers between devices  95.9 us (28%)
  starting transfers between devices  21.4 us (6%)
  local copies, waits for them, and re-layouts  13.9 us (4%)
  other arithmetic  6.51 us (2%)
    pallas_call x1, Pallas kernels, place_and_contract(): pl.pallas_call(functools.partial(place_kernel, quarters, ring), out_shape...  104 us
    all_to_all x1, waiting for transfers between devices, on_device(): lax.all_to_all(departing_tiles, ('opair', 'vpair'), split_axis=0, concat_...  95.9 us
    pallas_call x1, Pallas kernels, reduce_scatter(): pl.pallas_call(functools.partial(rs_kernel, ring), out_shape=jax.ShapeDty...  82.2 us
    pallas_call x1, Pallas kernels, gather_tiles(): pl.pallas_call(gather_kernel, out_shape=jax.ShapeDtypeStruct(grid_tiles.s...  12 us
    all_to_all x1, starting transfers between devices, on_device(): lax.all_to_all(labels, ('opair', 'vpair'), split_axis=0, concat_axis=0, t...  11.1 us
    all_to_all x1, starting transfers between devices, on_device(): lax.all_to_all(departing_tiles, ('opair', 'vpair'), split_axis=0, concat_...  10.3 us
  transfers between devices with their start and end apart: 2, of which 1 were waited for; matrix products, arithmetic and copies ran while one was open for 3% of the time, Pallas kernels for 4%

profile of v6, /device:TPU:0, one launch (start us, length us, event | category | flops | bytes accessed | tf_op | source)
XLA Modules:
  0.0 336.3 jit_solution(8692526407836209370)
XLA Ops:
  0.6 0.7 fusion.15
  1.3 0.7 fusion.11
  2.1 0.2 fusion.2
  2.4 0.2 fusion.4
  2.6 0.7 compare_select_fusion.2
  3.3 1.4 scatter_custom_fusion
  4.7 0.6 fusion.14
  5.3 0.7 and_select_fusion.1
  6.0 0.7 and_select_fusion
  6.8 0.2 le.15
  7.2 0.7 gather_fusion
  7.9 1.0 select_select_fusion
  8.9 11.1 %all-to-all-start = ((s32[128,2,3]{2,1,0:T(2,128)}), s32[128,2,3]{2,1,0:T(2,128)S(1)}, u32[]{:S(2)}, u32[]{:S(2)}) async-start(s32[128,2,3]{2,1,0:T(2,128)} %select_select_fusion), calls=%async_computation | async-start | bytes 262144 | tf_op jit(solution)/shard_map/all_to_all | solution.py:276
  20.0 12.0 %shard_map.68 = bf16[256,128,128]{2,1,0:T(8,128)(2,1)} custom-call(s32[256]{0:T(256)} %get-tuple-element.9.src_ref, bf16[256,128,128]{2,1,0:T(8,128)(2,1)} %grid_ref.1), custom_call_target="tpu_custom_call" | custom-call | tf_op jit(solution)/shard_map/pallas_call | solution.py:36
  32.0 10.3 %all-to-all-start.1 = ((bf16[256,128,128]{2,1,0:T(8,128)(2,1)}), bf16[256,128,128]{2,1,0:T(8,128)(2,1)}, u32[]{:S(2)}, u32[]{:S(2)}) async-start(bf16[256,128,128]{2,1,0:T(8,128)(2,1)} %shard_map.68), calls=%async_computation.1 | async-start | bytes 16777216 | tf_op jit(solution)/shard_map/all_to_all | solution.py:277
  42.3 6.4 %copy.34 = bf16[16,128,1024]{1,2,0:T(8,128)(2,1)} copy(bf16[16,128,1024]{2,1,0:T(8,128)(2,1)} %bitcast.33) | data formatting | bytes 8388608 | tf_op jit(solution)/shard_map/reshape | solution.py:262
  48.8 0.7 copy.40
  49.6 0.2 convert_reduce_fusion
  49.8 2.0 scatter_custom_fusion.1.order_ref
  51.8 0.7 convert_reduce_fusion.1.starts_ref
  52.5 95.9 %all-to-all-done.1.inc_ref = bf16[256,128,128]{2,1,0:T(8,128)(2,1)} async-done(((bf16[256,128,128]{2,1,0:T(8,128)(2,1)}), bf16[256,128,128]{2,1,0:T(8,128)(2,1)}, u32[]{:S(2)}, u32[]{:S(2)}) %all-to-all-start.1) | async-done | bytes 8388640 | tf_op jit(solution)/shard_map/all_to_all | solution.py:277
  148.5 103.6 %shard_map.69 = (bf16[128,128,128]{2,1,0:T(8,128)(2,1)}, f32[4,32,256,128]{3,2,1,0:T(8,128)}) custom-call(s32[256]{0:T(256)} %bitcast.41, s32[256]{0:T(256)} %scatter_custom_fusion.1.order_ref, s32[33]{0:T(128)} %convert_reduce_fusion.1.starts_ref, s32[256]{0:T(256)} %bitcast.44, bf16[256,128,128]{2,1,0:T(8,128)(2,1)} %all-to-all-done.1.inc_ref, ...), custom_call_target="tpu_custom_call" | custom-call | tf_op jit(solution)/shard_map/pallas_call | solution.py:95
  252.0 82.2 %shard_map.70 = f32[4,256,128]{2,1,0:T(8,128)} custom-call(f32[4,32,256,128]{3,2,1,0:T(8,128)} %get-tuple-element.5.part_ref), custom_call_target="tpu_custom_call" | custom-call | tf_op jit(solution)/shard_map/pallas_call | solution.py:228
  334.3 2.0 copy.35
  (23 shorter events, 0.8 us)
Async XLA Ops:
  8.9 23.1 %all-to-all-start = ((s32[128,2,3]{2,1,0:T(2,128)}), s32[128,2,3]{2,1,0:T(2,128)S(1)}, u32[]{:S(2)}, u32[]{:S(2)}) async-start(s32[128,2,3]{2,1,0:T(2,128)} %select_select_fusion), calls=%async_computation | async-start | bytes 262144 | tf_op jit(solution)/shard_map/all_to_all | solution.py:276
  32.0 116.5 %all-to-all-start.1 = ((bf16[256,128,128]{2,1,0:T(8,128)(2,1)}), bf16[256,128,128]{2,1,0:T(8,128)(2,1)}, u32[]{:S(2)}, u32[]{:S(2)}) async-start(bf16[256,128,128]{2,1,0:T(8,128)(2,1)} %shard_map.68), calls=%async_computation.1 | async-start | bytes 16777216 | tf_op jit(solution)/shard_map/all_to_all | solution.py:277
  49.6 98.8 %copy-start = (s32[256,1]{0,1:T(1,128)}, s32[256,1]{0,1:T(1,128)S(1)}, u32[]{:S(2)}) copy-start(s32[256,1]{0,1:T(1,128)S(1)} %copy.37) | copy-start | bytes 3076

commit v7 on v5

--- a/solution.py
+++ b/solution.py
@@ -262,12 +262,23 @@
         .set(jnp.arange(slot_count, dtype=jnp.int32))[: devices * capacity]
     )
     departing_tiles = gather_tiles(src, grid_tiles)
-    label_rows = jnp.stack([tile_owner % owned, tile_rows % RT_OP, tile_cols % kc_local], axis=1)
-    labels = jnp.where((src >= 0)[:, None], jnp.take(label_rows, jnp.maximum(src, 0), axis=0), -1)
-    arrived = lax.all_to_all(labels, ("opair", "vpair"), split_axis=0, concat_axis=0, tiled=True)
+    everything = lax.all_gather(
+        jnp.stack([tile_owner, tile_rows, tile_cols]), ("opair", "vpair"), axis=0, tiled=False
+    )
     incoming = lax.all_to_all(
         departing_tiles, ("opair", "vpair"), split_axis=0, concat_axis=0, tiled=True
     )
+    me = lax.axis_index("opair") * vp_count + lax.axis_index("vpair")
+    g_owner = everything[:, 0]
+    mine = (g_owner >= 0) & (g_owner // owned == me)
+    mine_i = mine.astype(jnp.int32)
+    rank = jnp.cumsum(mine_i, axis=1) - mine_i
+    source = jnp.arange(devices, dtype=jnp.int32)[:, None]
+    landing = jnp.where(mine, source * capacity + rank, slot_count).reshape(-1)
+    fields = jnp.stack(
+        [g_owner % owned, everything[:, 1] % RT_OP, everything[:, 2] % kc_local], axis=-1
+    ).reshape(-1, 3)
+    arrived = jnp.full((slot_count + 1, 3), -1, jnp.int32).at[landing].set(fields)[:slot_count]
     meta = jnp.transpose(arrived).reshape(-1)
     ring = 4
     ov_tiles, partial_value = place_and_contract(

time: 279 us -> 387 us (1.39)
  blocking collectives: 0 us -> 132 us
  waiting for transfers between devices: 99.1 us -> 0.01 us
  local copies, waits for them, and re-layouts: 11.8 us -> 101 us
  starting transfers between devices: 21.5 us -> 11.6 us
  Pallas kernels: 140 us -> 135 us
    all_gather x0 -> x1, blocking collectives: none -> 132 us  [on_device(): lax.all_gather(jnp.stack([tile_owner, tile_rows, tile_cols]), ('opair', '...]
    all_to_all x1, waiting for transfers between devices: 99.1 us -> 0.01 us  [on_device(): lax.all_to_all(departing_tiles, ('opair', 'vpair'), split_axis=0, concat_...]
    scatter x0 -> x1, local copies, waits for them, and re-layouts: none -> 80.6 us  [on_device(): jnp.full((slot_count + 1, 3), -1, jnp.int32).at[landing].set(fields)]
    all_to_all x1 -> x0, starting transfers between devices: 11.1 us -> none  [on_device(): lax.all_to_all(labels, ('opair', 'vpair'), split_axis=0, concat_axis=0, t...]
    another operation x4 -> x7, local copies, waits for them, and re-layouts: 0.15 us -> 8.71 us  [the longest x1 8.57 us: on_device(): jnp.stack([g_owner % owned, everything[:, 1] % RT_OP, everything[:, 2] %...]
    pallas_call x1, Pallas kernels: 82.2 us -> 77.7 us  [reduce_scatter(): pl.pallas_call(functools.partial(rs_kernel, ring), out_shape=jax.ShapeDty...]
  transfers between devices with their start and end apart: 2 -> 1, of which waited for: 1 -> 0; matrix products, arithmetic and copies ran while one was open for 3% -> 26% of each run, Pallas kernels for 4% -> 0%
where the time goes in v7:
time: 387 us; the launch traced here: 386 us
  Pallas kernels  135 us (35%)
  blocking collectives  132 us (34%)
  local copies, waits for them, and re-layouts  101 us (26%)
  starting transfers between devices  11.6 us (3%)
  other arithmetic  5.07 us (1%)
    all_gather x1, blocking collectives, on_device(): lax.all_gather(jnp.stack([tile_owner, tile_rows, tile_cols]), ('opair', '...  132 us
    scatter x1, local copies, waits for them, and re-layouts, on_device(): jnp.full((slot_count + 1, 3), -1, jnp.int32).at[landing].set(fields)  80.6 us
    pallas_call x1, Pallas kernels, reduce_scatter(): pl.pallas_call(functools.partial(rs_kernel, ring), out_shape=jax.ShapeDty...  77.7 us
    pallas_call x1, Pallas kernels, place_and_contract(): pl.pallas_call(functools.partial(place_kernel, quarters, ring), out_shape...  45.4 us
    pallas_call x1, Pallas kernels, gather_tiles(): pl.pallas_call(gather_kernel, out_shape=jax.ShapeDtypeStruct(grid_tiles.s...  12 us
    all_to_all x1, starting transfers between devices, on_device(): lax.all_to_all(departing_tiles, ('opair', 'vpair'), split_axis=0, concat_...  11.6 us
    another operation x1, local copies, waits for them, and re-layouts, on_device(): jnp.stack([g_owner % owned, everything[:, 1] % RT_OP, everything[:, 2] %...  8.57 us
  transfers between devices with their start and end apart: 1, of which 0 were waited for; matrix products, arithmetic and copies ran while one was open for 26% of the time, Pallas kernels for 0%

profile of v7, /device:TPU:0, one launch (start us, length us, event | category | flops | bytes accessed | tf_op | source)
XLA Modules:
  0.0 385.8 jit_solution(14615414985119444938)
XLA Ops:
  0.6 0.7 fusion.18
  1.3 0.7 fusion.14
  2.1 0.2 fusion.2
  2.4 0.2 fusion.6
  2.6 0.7 compare_select_fusion.8
  3.3 1.4 scatter_custom_fusion.1
  4.7 0.6 slice.35.src_ref
  5.3 12.0 %shard_map.68 = bf16[256,128,128]{2,1,0:T(8,128)(2,1)} custom-call(s32[256]{0:T(256)} %slice.35.src_ref, bf16[256,128,128]{2,1,0:T(8,128)(2,1)} %grid_ref.1), custom_call_target="tpu_custom_call" | custom-call | tf_op jit(solution)/shard_map/pallas_call | solution.py:36
  17.3 11.6 %all-to-all-start = ((bf16[256,128,128]{2,1,0:T(8,128)(2,1)}), bf16[256,128,128]{2,1,0:T(8,128)(2,1)}, u32[]{:S(2)}, u32[]{:S(2)}) async-start(bf16[256,128,128]{2,1,0:T(8,128)(2,1)} %shard_map.68), calls=%async_computation | async-start | bytes 16777216 | tf_op jit(solution)/shard_map/all_to_all | solution.py:268
  29.0 0.1 copy.38
  29.2 131.9 %all-gather.1 = s32[128,3,256]{2,1,0:T(4,128)S(1)} all-gather(s32[1,3,256]{2,1,0:T(4,128)S(1)} %add_bitcast_fusion), channel_id=2, replica_groups=mesh['opair'=4,'vpair'=32] {'opair','vpair'}, dimensions={0}, use_global_device_ids=true | all-gather | bytes 396288 | tf_op jit(solution)/shard_map/all_gather | solution.py:265
  161.1 0.3 fusion.17
  161.6 0.1 fusion.7
  161.8 0.1 copy.29
  161.9 6.4 %copy.34 = bf16[16,128,1024]{1,2,0:T(8,128)(2,1)} copy(bf16[16,128,1024]{2,1,0:T(8,128)(2,1)} %bitcast.45) | data formatting | bytes 8388608 | tf_op jit(solution)/shard_map/reshape | solution.py:253
  168.3 1.2 and_select_fusion.2
  169.5 0.7 and_select_fusion
  170.3 0.3 pad_add_fusion
  170.6 8.6 %copy.30 = s32[32768,3]{1,0:T(8,128)} copy(s32[32768,3]{0,1:T(4,128)S(1)} %pad_add_fusion) | data formatting | bytes 786432 | tf_op jit(solution)/shard_map/stack | solution.py:278
  179.2 80.6 %scatter_custom_fusion = s32[257,3]{1,0:T(8,128)S(1)} fusion(s32[32768]{0:T(1024)S(1)} %bitcast.58, s32[32768,3]{1,0:T(8,128)} %copy.30, s32[]{:T(128)} %constant.73.clone.1), kind=kCustom, calls=%fused_computation.37 | custom fusion | bytes 3596 | tf_op jit(solution)/shard_map/scatter | solution.py:281
  259.9 0.6 reshape.331.meta_ref
  260.6 45.4 %shard_map.69 = (bf16[128,128,128]{2,1,0:T(8,128)(2,1)}, f32[4,32,256,128]{3,2,1,0:T(8,128)}) custom-call(s32[768]{0:T(1024)} %reshape.331.meta_ref, bf16[256,128,128]{2,1,0:T(8,128)(2,1)} %all-to-all-done.inc_ref, bf16[16,1024,128]{2,1,0:T(8,128)(2,1)} %bitcast.44), custom_call_target="tpu_custom_call" | custom-call | tf_op jit(solution)/shard_map/pallas_call | solution.py:85
  306.0 77.7 %shard_map.70 = f32[4,256,128]{2,1,0:T(8,128)} custom-call(f32[4,32,256,128]{3,2,1,0:T(8,128)} %get-tuple-element.5.part_ref), custom_call_target="tpu_custom_call" | custom-call | tf_op jit(solution)/shard_map/pallas_call | solution.py:219
  383.8 2.0 copy.35
  (27 shorter events, 0.6 us)
Async XLA Ops:
  5.3 23.9 %copy-start = (s32[256]{0:T(256)S(1)}, s32[256]{0:T(256)}, u32[]{:S(2)}) copy-start(s32[256]{0:T(256)} %param.8) | copy-start | bytes 3076
  5.3 23.9 %copy-start.1 = (s32[256]{0:T(256)S(1)}, s32[256]{0:T(256)}, u32[]{:S(2)}) copy-start(s32[256]{0:T(256)} %param.7) | copy-start | bytes 3076
  5.3 23.9 %copy-start.2 = (s32[256]{0:T(256)S(1)}, s32[256]{0:T(256)}, u32[]{:S(2)}) copy-start(s32[256]{0:T(256)} %param.6) | copy-start | bytes 3076
  17.3 243.3 %all-to-all-start = ((bf16[256,128,128]{2,1,0:T(8,128)(2,1)}), bf16[256,128,128]{2,1,0:T(8,128)(2,1)}, u32[]{:S(2)}, u32[]{:S(2)}) async-start(bf16[256,128,128]{2,1,0:T(8,128)(2,1)} %shard_map.68), calls=%async_computation | async-start | bytes 16777216 | tf_op jit(solution)/shard_map/all_to_all | solution.py:268

commit v8 on v7

--- a/solution.py
+++ b/solution.py
@@ -273,12 +273,14 @@
     mine = (g_owner >= 0) & (g_owner // owned == me)
     mine_i = mine.astype(jnp.int32)
     rank = jnp.cumsum(mine_i, axis=1) - mine_i
-    source = jnp.arange(devices, dtype=jnp.int32)[:, None]
-    landing = jnp.where(mine, source * capacity + rank, slot_count).reshape(-1)
-    fields = jnp.stack(
-        [g_owner % owned, everything[:, 1] % RT_OP, everything[:, 2] % kc_local], axis=-1
-    ).reshape(-1, 3)
-    arrived = jnp.full((slot_count + 1, 3), -1, jnp.int32).at[landing].set(fields)[:slot_count]
+    fields = jnp.stack([g_owner % owned, everything[:, 1] % RT_OP, everything[:, 2] % kc_local], axis=-1)
+    picked = []
+    for k in range(capacity):
+        chosen = mine & (rank == k)
+        found = jnp.any(chosen, axis=1)
+        value = jnp.sum(jnp.where(chosen[:, :, None], fields, 0), axis=1)
+        picked.append(jnp.where(found[:, None], value, -1))
+    arrived = jnp.stack(picked, axis=1).reshape(slot_count, 3)
     meta = jnp.transpose(arrived).reshape(-1)
     ring = 4
     ov_tiles, partial_value = place_and_contract(

time: 387 us -> 298 us (0.77)
  local copies, waits for them, and re-layouts: 101 us -> 12 us
    scatter x1 -> x0, local copies, waits for them, and re-layouts: 80.6 us -> none  [on_device(): jnp.full((slot_count + 1, 3), -1, jnp.int32).at[landing].set(fields)]
    another operation x7, local copies, waits for them, and re-layouts: 8.71 us -> 0.18 us  [the longest x1 0.14 us: on_device(): arrived = jnp.stack(picked, axis=1).reshape(slot_count, 3)]
  transfers between devices with their start and end apart: 1 -> 1, of which waited for: 0 -> 0; matrix products, arithmetic and copies ran while one was open for 26% -> 3% of each run, Pallas kernels for 0% -> 0%
where the time goes in v8:
time: 298 us; the launch traced here: 296 us
  Pallas kernels  136 us (46%)
  blocking collectives  132 us (44%)
  local copies, waits for them, and re-layouts  12 us (4%)
  starting transfers between devices  11.7 us (4%)
  other arithmetic  3.26 us (1%)
    all_gather x1, blocking collectives, on_device(): lax.all_gather(jnp.stack([tile_owner, tile_rows, tile_cols]), ('opair', '...  132 us
    pallas_call x1, Pallas kernels, reduce_scatter(): pl.pallas_call(functools.partial(rs_kernel, ring), out_shape=jax.ShapeDty...  78.6 us
    pallas_call x1, Pallas kernels, place_and_contract(): pl.pallas_call(functools.partial(place_kernel, quarters, ring), out_shape...  45.5 us
    pallas_call x1, Pallas kernels, gather_tiles(): pl.pallas_call(gather_kernel, out_shape=jax.ShapeDtypeStruct(grid_tiles.s...  11.9 us
    all_to_all x1, starting transfers between devices, on_device(): lax.all_to_all(departing_tiles, ('opair', 'vpair'), split_axis=0, concat_...  11.7 us
    reshape x1, local copies, waits for them, and re-layouts, on_device(): integrals.reshape(kc_local, tile_width, integrals.shape[1])  6.36 us
  transfers between devices with their start and end apart: 1, of which 0 were waited for; matrix products, arithmetic and copies ran while one was open for 3% of the time, Pallas kernels for 0%

profile of v8, /device:TPU:0, one launch (start us, length us, event | category | flops | bytes accessed | tf_op | source)
XLA Modules:
  0.0 296.0 jit_solution(7696166896175125284)
XLA Ops:
  0.6 0.7 fusion.25
  1.3 0.7 fusion.18
  2.0 0.1 copy.33
  2.1 0.2 fusion.7
  2.4 0.2 fusion.9
  2.6 0.7 compare_select_fusion
  3.3 1.4 scatter_custom_fusion
  4.7 0.6 slice.31.src_ref
  5.3 11.9 %shard_map.68 = bf16[256,128,128]{2,1,0:T(8,128)(2,1)} custom-call(s32[256]{0:T(256)} %slice.31.src_ref, bf16[256,128,128]{2,1,0:T(8,128)(2,1)} %grid_ref.1), custom_call_target="tpu_custom_call" | custom-call | tf_op jit(solution)/shard_map/pallas_call | solution.py:36
  17.2 11.7 %all-to-all-start = ((bf16[256,128,128]{2,1,0:T(8,128)(2,1)}), bf16[256,128,128]{2,1,0:T(8,128)(2,1)}, u32[]{:S(2)}, u32[]{:S(2)}) async-start(bf16[256,128,128]{2,1,0:T(8,128)(2,1)} %shard_map.68), calls=%async_computation | async-start | bytes 16777216 | tf_op jit(solution)/shard_map/all_to_all | solution.py:268
  29.0 132.2 %all-gather.1 = s32[128,3,256]{2,1,0:T(4,128)S(1)} all-gather(s32[1,3,256]{2,1,0:T(4,128)S(1)} %add_bitcast_fusion), channel_id=2, replica_groups=mesh['opair'=4,'vpair'=32] {'opair','vpair'}, dimensions={0}, use_global_device_ids=true | all-gather | bytes 396288 | tf_op jit(solution)/shard_map/all_gather | solution.py:265
  161.1 0.3 fusion.24
  161.4 0.1 copy.39
  161.6 0.1 fusion.11
  161.9 0.1 copy.40
  162.0 0.1 copy.41
  162.1 0.2 fusion.21
  162.6 0.1 copy.32
  162.7 0.2 reshape.323
  162.9 0.6 reshape.324.meta_ref
  163.5 6.4 %copy.35 = bf16[16,128,1024]{1,2,0:T(8,128)(2,1)} copy(bf16[16,128,1024]{2,1,0:T(8,128)(2,1)} %bitcast.81) | data formatting | bytes 8388608 | tf_op jit(solution)/shard_map/reshape | solution.py:253
  169.8 45.5 %shard_map.69 = (bf16[128,128,128]{2,1,0:T(8,128)(2,1)}, f32[4,32,256,128]{3,2,1,0:T(8,128)}) custom-call(s32[768]{0:T(1024)} %reshape.324.meta_ref, bf16[256,128,128]{2,1,0:T(8,128)(2,1)} %all-to-all-done.inc_ref, bf16[16,1024,128]{2,1,0:T(8,128)(2,1)} %bitcast.80), custom_call_target="tpu_custom_call" | custom-call | tf_op jit(solution)/shard_map/pallas_call | solution.py:85
  215.4 78.6 %shard_map.70 = f32[4,256,128]{2,1,0:T(8,128)} custom-call(f32[4,32,256,128]{3,2,1,0:T(8,128)} %get-tuple-element.5.part_ref), custom_call_target="tpu_custom_call" | custom-call | tf_op jit(solution)/shard_map/pallas_call | solution.py:219
  293.9 2.0 copy.36
  (29 shorter events, 0.6 us)
Async XLA Ops:
  17.2 11.7 %copy-start = (s32[256]{0:T(256)S(1)}, s32[256]{0:T(256)}, u32[]{:S(2)}) copy-start(s32[256]{0:T(256)} %param.8) | copy-start | bytes 3076
  17.2 11.8 %copy-start.1 = (s32[256]{0:T(256)S(1)}, s32[256]{0:T(256)}, u32[]{:S(2)}) copy-start(s32[256]{0:T(256)} %param.7) | copy-start | bytes 3076
  17.2 11.8 %copy-start.2 = (s32[256]{0:T(256)S(1)}, s32[256]{0:T(256)}, u32[]{:S(2)}) copy-start(s32[256]{0:T(256)} %param.6) | copy-start | bytes 3076
  17.2 152.6 %all-to-all-start = ((bf16[256,128,128]{2,1,0:T(8,128)(2,1)}), bf16[256,128,128]{2,1,0:T(8,128)(2,1)}, u32[]{:S(2)}, u32[]{:S(2)}) async-start(bf16[256,128,128]{2,1,0:T(8,128)(2,1)} %shard_map.68), calls=%async_computation | async-start | bytes 16777216 | tf_op jit(solution)/shard_map/all_to_all | solution.py:268

commit v9 on v5

--- a/solution.py
+++ b/solution.py
@@ -55,23 +55,30 @@
     return c * half + z * ring + y
 
 
-def place_kernel(quarters, ring, meta_ref, inc_ref, int_ref, ov_ref, part_ref):
+def place_kernel(quarters, ring, with_ov, meta_ref, inc_ref, int_ref, *outs):
+    part_ref = outs[-1]
     slots = inc_ref.shape[0]
+    half = part_ref.shape[1]
     width = part_ref.shape[2]
+    want = meta_ref[3 * slots]
     part_ref[...] = jnp.zeros(part_ref.shape, part_ref.dtype)
 
     def body(i, carry):
         pos = meta_ref[i]
-        row = meta_ref[slots + i]
-        col = meta_ref[2 * slots + i]
-
-        @pl.when(pos >= 0)
+        row = jnp.maximum(meta_ref[slots + i], 0)
+        col = jnp.maximum(meta_ref[2 * slots + i], 0)
+
+        if with_ov:
+
+            @pl.when(pos >= 0)
+            def _():
+                outs[0][jnp.maximum(pos, 0)] = inc_ref[i].T
+
+        @pl.when((pos >= 0) & (row % 2 == want))
         def _():
-            tile = inc_ref[i]
-            ov_ref[jnp.maximum(pos, 0)] = tile.T
-            prod = jnp.dot(int_ref[jnp.maximum(col, 0)], tile, preferred_element_type=jnp.float32)
+            prod = jnp.dot(int_ref[col], inc_ref[i], preferred_element_type=jnp.float32)
             for q in range(quarters):
-                s = storage_row(q, jnp.maximum(row, 0), ring)
+                s = storage_row(q, row, ring) - want * half
                 part_ref[q, s] += prod[q * width : (q + 1) * width, :]
 
         return carry
@@ -79,32 +86,34 @@
     lax.fori_loop(0, slots, body, 0)
 
 
-def place_and_contract(meta, incoming, int_table, owned, rows, quarters, ring):
+def place_and_contract(meta, incoming, int_table, owned, rows, quarters, ring, with_ov):
     tile_width = incoming.shape[1]
     columns = int_table.shape[1]
+    part_shape = jax.ShapeDtypeStruct((quarters, rows // 2, columns // quarters, tile_width), jnp.float32)
+    vmem = pl.BlockSpec(memory_space=pltpu.VMEM)
+    if with_ov:
+        out_shape = (jax.ShapeDtypeStruct((owned, tile_width, tile_width), incoming.dtype), part_shape)
+        out_specs = (vmem, vmem)
+    else:
+        out_shape = (part_shape,)
+        out_specs = (vmem,)
     return pl.pallas_call(
-        functools.partial(place_kernel, quarters, ring),
-        out_shape=(
-            jax.ShapeDtypeStruct((owned, tile_width, tile_width), incoming.dtype),
-            jax.ShapeDtypeStruct((quarters, rows, columns // quarters, tile_width), jnp.float32),
+        functools.partial(place_kernel, quarters, ring, with_ov),
+        out_shape=out_shape,
+        in_specs=[pl.BlockSpec(memory_space=pltpu.SMEM), vmem, vmem],
+        out_specs=out_specs,
+        compiler_params=pltpu.CompilerParams(vmem_limit_bytes=VMEM_LIMIT),
+        cost_estimate=pl.CostEstimate(
+            flops=2 * tile_width * tile_width * columns * owned // 2,
+            bytes_accessed=incoming.size * 2 + int_table.size * 2 + part_shape.size * 4,
+            transcendentals=0,
         ),
-        in_specs=[
-            pl.BlockSpec(memory_space=pltpu.SMEM),
-            pl.BlockSpec(memory_space=pltpu.VMEM),
-            pl.BlockSpec(memory_space=pltpu.VMEM),
-        ],
-        out_specs=(
-            pl.BlockSpec(memory_space=pltpu.VMEM),
-            pl.BlockSpec(memory_space=pltpu.VMEM),
-        ),
-        compiler_params=pltpu.CompilerParams(vmem_limit_bytes=VMEM_LIMIT),
     )(meta, incoming, int_table)
 
 
-def rs_kernel(ring, part_ref, out_ref, core_buf, red, rbuf1, acc1, fin1, rbuf2, acc2,
-              core_send, core_recv, send1, recv1, send2, recv2):
-    quarters, rows, tile_width, width = part_ref.shape
-    half = rows // 2
+def rs_kernel(ring, part_ref, core_buf, out_ref, red, rbuf1, acc1, fin1, rbuf2, acc2,
+              send1, recv1, send2, recv2):
+    quarters, half, tile_width, width = part_ref.shape
     steps = ring - 1
     op = lax.axis_index("opair")
     v = lax.axis_index("vpair")
@@ -115,35 +124,23 @@
     def dev(zz, yy, cc):
         return (op, (zz * ring + yy) * 2 + cc)
 
-    sib = dev(z, y, 1 - c)
     y_up = dev(z, (y + 1) % ring, c)
     y_dn = dev(z, (y + ring - 1) % ring, c)
     z_up = dev((z + 1) % ring, y, c)
     z_dn = dev((z + ring - 1) % ring, y, c)
 
     barrier = pltpu.get_barrier_semaphore()
-    for peer in (sib, y_up, y_dn, z_up, z_dn):
+    for peer in (y_up, y_dn, z_up, z_dn):
         pl.semaphore_signal(barrier, inc=1, device_id=peer, device_id_type=MESH)
-    pl.semaphore_wait(barrier, 5)
-
-    core_copy = pltpu.make_async_remote_copy(
-        src_ref=part_ref.at[:, pl.ds((1 - c) * half, half)],
-        dst_ref=core_buf,
-        send_sem=core_send,
-        recv_sem=core_recv,
-        device_id=sib,
-        device_id_type=MESH,
-    )
-    core_copy.start()
-    core_copy.wait()
 
     def core_sum(k, carry):
         q = k // half
         i = k % half
-        red[q, i] = part_ref[q, c * half + i] + core_buf[q, i]
+        red[q, i] = part_ref[q, i] + core_buf[q, i]
         return carry
 
     lax.fori_loop(0, quarters * half, core_sum, 0)
+    pl.semaphore_wait(barrier, 4)
 
     def plan(q):
         d = 1 if q % 2 == 0 else -1
@@ -211,26 +208,23 @@
                 out_ref[q] = total
 
 
-def reduce_scatter(part, ring):
-    quarters, rows, tile_width, width = part.shape
-    half = rows // 2
+def reduce_scatter(part, core_part, ring):
+    quarters, half, tile_width, width = part.shape
     steps = ring - 1
     f32 = jnp.float32
+    vmem = pl.BlockSpec(memory_space=pltpu.VMEM)
     return pl.pallas_call(
         functools.partial(rs_kernel, ring),
         out_shape=jax.ShapeDtypeStruct((quarters, tile_width, width), f32),
-        in_specs=[pl.BlockSpec(memory_space=pltpu.VMEM)],
-        out_specs=pl.BlockSpec(memory_space=pltpu.VMEM),
+        in_specs=[vmem, vmem],
+        out_specs=vmem,
         scratch_shapes=[
-            pltpu.VMEM((quarters, half, tile_width, width), f32),
             pltpu.VMEM((quarters, half, tile_width, width), f32),
             pltpu.VMEM((quarters, steps, ring, tile_width, width), f32),
             pltpu.VMEM((quarters, steps - 1, ring, tile_width, width), f32),
             pltpu.VMEM((quarters, ring, tile_width, width), f32),
             pltpu.VMEM((quarters, steps, tile_width, width), f32),
             pltpu.VMEM((quarters, steps - 1, tile_width, width), f32),
-            pltpu.SemaphoreType.DMA(()),
-            pltpu.SemaphoreType.DMA(()),
             pltpu.SemaphoreType.DMA((quarters, steps)),
             pltpu.SemaphoreType.DMA((quarters, steps)),
             pltpu.SemaphoreType.DMA((quarters, steps)),
@@ -239,7 +233,7 @@
         compiler_params=pltpu.CompilerParams(
             collective_id=0, has_side_effects=True, vmem_limit_bytes=VMEM_LIMIT
         ),
-    )(part)
+    )(part, core_part)
 
 
 def on_device(grid_tiles, tile_rows, tile_cols, tile_owner, integrals):
@@ -268,12 +262,20 @@
     incoming = lax.all_to_all(
         departing_tiles, ("opair", "vpair"), split_axis=0, concat_axis=0, tiled=True
     )
-    meta = jnp.transpose(arrived).reshape(-1)
     ring = 4
-    ov_tiles, partial_value = place_and_contract(
-        meta, incoming, int_table, owned, RT_OP, QUARTERS, ring
-    )
-    cycle_t = reduce_scatter(partial_value, ring)
+    side = lax.axis_index("vpair") % 2
+    flat = jnp.transpose(arrived).reshape(-1)
+    meta_sib = jnp.concatenate([flat, (1 - side)[None].astype(jnp.int32)])
+    meta_own = jnp.concatenate([flat, side[None].astype(jnp.int32)])
+    ov_tiles, part_sib = place_and_contract(
+        meta_sib, incoming, int_table, owned, RT_OP, QUARTERS, ring, True
+    )
+    pairs = [(v, v ^ 1) for v in range(vp_count)]
+    core_part = lax.ppermute(part_sib, "vpair", perm=pairs)
+    (part_own,) = place_and_contract(
+        meta_own, incoming, int_table, owned, RT_OP, QUARTERS, ring, False
+    )
+    cycle_t = reduce_scatter(part_own, core_part, ring)
     cycle_sum = jnp.transpose(cycle_t.reshape(-1, tile_width))
     return (ov_tiles, cycle_sum)
 

time: 279 us -> 281 us (level)
    pallas_call x1 -> x2, Pallas kernels: 45.6 us -> 64.6 us  [place_and_contract(): pl.pallas_call(functools.partial(place_kernel, quarters, ring, with_ov),...]
    pallas_call x1, Pallas kernels: 82.2 us -> 64.9 us  [reduce_scatter(): pl.pallas_call(functools.partial(rs_kernel, ring), out_shape=jax.ShapeDty...]
  transfers between devices with their start and end apart: 2 -> 3, of which waited for: 1 -> 1; matrix products, arithmetic and copies ran while one was open for 3% -> 3% of each run, Pallas kernels for 4% -> 14%
where the time goes in v9:
time: 281 us; the launch traced here: 280 us
  Pallas kernels  141 us (50%)
  waiting for transfers between devices  99 us (35%)
  starting transfers between devices  21.6 us (8%)
  local copies, waits for them, and re-layouts  11.3 us (4%)
  other arithmetic  6.08 us (2%)
    all_to_all x1, waiting for transfers between devices, on_device(): lax.all_to_all(departing_tiles, ('opair', 'vpair'), split_axis=0, concat_...  99 us
    pallas_call x1, Pallas kernels, reduce_scatter(): pl.pallas_call(functools.partial(rs_kernel, ring), out_shape=jax.ShapeDty...  64.9 us
    pallas_call x2, Pallas kernels, place_and_contract(): pl.pallas_call(functools.partial(place_kernel, quarters, ring, with_ov),...  64.6 us
    pallas_call x1, Pallas kernels, gather_tiles(): pl.pallas_call(gather_kernel, out_shape=jax.ShapeDtypeStruct(grid_tiles.s...  11.9 us
    all_to_all x1, starting transfers between devices, on_device(): lax.all_to_all(labels, ('opair', 'vpair'), split_axis=0, concat_axis=0, t...  11.1 us
    all_to_all x1, starting transfers between devices, on_device(): lax.all_to_all(departing_tiles, ('opair', 'vpair'), split_axis=0, concat_...  10.4 us
    reshape x1, local copies, waits for them, and re-layouts, on_device(): integrals.reshape(kc_local, tile_width, integrals.shape[1])  6.42 us
  transfers between devices with their start and end apart: 3, of which 1 were waited for; matrix products, arithmetic and copies ran while one was open for 3% of the time, Pallas kernels for 14%

profile of v9, /device:TPU:0, one launch (start us, length us, event | category | flops | bytes accessed | tf_op | source)
XLA Modules:
  0.0 280.0 jit_solution(16617107600035281045)
XLA Ops:
  0.6 0.7 fusion.11
  1.3 0.7 fusion.9
  2.1 0.2 fusion
  2.4 0.2 fusion.2
  2.6 0.7 compare_select_fusion
  3.3 1.4 scatter_custom_fusion
  4.7 0.6 fusion.10
  5.3 0.7 and_select_fusion.1
  6.0 0.7 and_select_fusion
  6.7 0.2 ge.17
  6.8 0.2 le.15
  7.0 0.1 copy.26
  7.2 0.7 gather_fusion
  7.9 1.0 select_select_fusion
  8.9 11.1 %all-to-all-start = ((s32[128,2,3]{2,1,0:T(2,128)}), s32[128,2,3]{2,1,0:T(2,128)S(1)}, u32[]{:S(2)}, u32[]{:S(2)}) async-start(s32[128,2,3]{2,1,0:T(2,128)} %select_select_fusion), calls=%async_computation | async-start | bytes 262144 | tf_op jit(solution)/shard_map/all_to_all | solution.py:261
  20.0 11.9 %shard_map.68 = bf16[256,128,128]{2,1,0:T(8,128)(2,1)} custom-call(s32[256]{0:T(256)} %get-tuple-element.8.src_ref, bf16[256,128,128]{2,1,0:T(8,128)(2,1)} %grid_ref.1), custom_call_target="tpu_custom_call" | custom-call | tf_op jit(solution)/shard_map/pallas_call | solution.py:36
  31.9 10.4 %all-to-all-start.1 = ((bf16[256,128,128]{2,1,0:T(8,128)(2,1)}), bf16[256,128,128]{2,1,0:T(8,128)(2,1)}, u32[]{:S(2)}, u32[]{:S(2)}) async-start(bf16[256,128,128]{2,1,0:T(8,128)(2,1)} %shard_map.68), calls=%async_computation.1 | async-start | bytes 16777216 | tf_op jit(solution)/shard_map/all_to_all | solution.py:262
  42.3 6.4 %copy.28 = bf16[16,128,1024]{1,2,0:T(8,128)(2,1)} copy(bf16[16,128,1024]{2,1,0:T(8,128)(2,1)} %bitcast.30) | data formatting | bytes 8388608 | tf_op jit(solution)/shard_map/reshape | solution.py:247
  48.8 0.6 pad_add_fusion.2
  49.4 99.0 %all-to-all-done.1.inc_ref = bf16[256,128,128]{2,1,0:T(8,128)(2,1)} async-done(((bf16[256,128,128]{2,1,0:T(8,128)(2,1)}), bf16[256,128,128]{2,1,0:T(8,128)(2,1)}, u32[]{:S(2)}, u32[]{:S(2)}) %all-to-all-start.1) | async-done | bytes 8388640 | tf_op jit(solution)/shard_map/all_to_all | solution.py:262
  148.4 36.8 %shard_map.69 = (bf16[128,128,128]{2,1,0:T(8,128)(2,1)}, f32[4,16,256,128]{3,2,1,0:T(8,128)}) custom-call(s32[769]{0:T(1024)} %get-tuple-element.7.meta_ref, bf16[256,128,128]{2,1,0:T(8,128)(2,1)} %all-to-all-done.1.inc_ref, bf16[16,1024,128]{2,1,0:T(8,128)(2,1)} %bitcast.28), custom_call_target="tpu_custom_call" | custom-call | flops 2147483648 | bytes 20971520 | tf_op jit(solution)/shard_map/pallas_call | solution.py:100
  185.4 27.7 %shard_map.70.part_ref = f32[4,16,256,128]{3,2,1,0:T(8,128)} custom-call(s32[769]{0:T(1024)} %get-tuple-element.6.meta_ref, bf16[256,128,128]{2,1,0:T(8,128)(2,1)} %all-to-all-done.1.inc_ref, bf16[16,1024,128]{2,1,0:T(8,128)(2,1)} %bitcast.29), custom_call_target="tpu_custom_call" | custom-call | flops 2147483648 | bytes 20971520 | tf_op jit(solution)/shard_map/pallas_call | solution.py:100
  213.1 64.9 %shard_map.71 = f32[4,256,128]{2,1,0:T(8,128)} custom-call(f32[4,16,256,128]{3,2,1,0:T(8,128)} %shard_map.70.part_ref, f32[4,16,256,128]{3,2,1,0:T(8,128)} %collective-permute-done.core_buf), custom_call_target="tpu_custom_call" | custom-call | tf_op jit(solution)/shard_map/pallas_call | solution.py:216
  278.0 2.0 copy.29
  (16 shorter events, 0.4 us)
Async XLA Ops:
  8.9 23.0 %all-to-all-start = ((s32[128,2,3]{2,1,0:T(2,128)}), s32[128,2,3]{2,1,0:T(2,128)S(1)}, u32[]{:S(2)}, u32[]{:S(2)}) async-start(s32[128,2,3]{2,1,0:T(2,128)} %select_select_fusion), calls=%async_computation | async-start | bytes 262144 | tf_op jit(solution)/shard_map/all_to_all | solution.py:261
  31.9 116.6 %all-to-all-start.1 = ((bf16[256,128,128]{2,1,0:T(8,128)(2,1)}), bf16[256,128,128]{2,1,0:T(8,128)(2,1)}, u32[]{:S(2)}, u32[]{:S(2)}) async-start(bf16[256,128,128]{2,1,0:T(8,128)(2,1)} %shard_map.68), calls=%async_computation.1 | async-start | bytes 16777216 | tf_op jit(solution)/shard_map/all_to_all | solution.py:262
  185.3 27.8 %collective-permute-start = (f32[4,16,256,128]{3,2,1,0:T(8,128)}, f32[4,16,256,128]{3,2,1,0:T(8,128)}, u32[]{:S(2)}, u32[]{:S(2)}) collective-permute-start(f32[4,16,256,128]{3,2,1,0:T(8,128)} %get-tuple-element.5), channel_id=1, source_target_pairs={{0,1},{1,0},{2,3},{3,2},{4,5},{5,4},{6,7},{7,6},{8,9},{9,8},{10,11... | collective-permute-start | bytes 25165832 | tf_op jit(solution)/shard_map/ppermute | solution.py:274

commit v10 on v5

--- a/solution.py
+++ b/solution.py
@@ -13,35 +13,80 @@
 VMEM_LIMIT = 60 * 1024 * 1024
 
 
-def gather_kernel(src_ref, grid_ref, out_ref):
-    zero = jnp.zeros(out_ref.shape[1:], out_ref.dtype)
-
-    def body(j, carry):
-        s = src_ref[j]
-
-        @pl.when(s >= 0)
-        def _():
-            out_ref[j] = grid_ref[jnp.maximum(s, 0)]
-
-        @pl.when(s < 0)
-        def _():
-            out_ref[j] = zero
-
-        return carry
-
-    lax.fori_loop(0, out_ref.shape[0], body, 0)
-
-
-def gather_tiles(src, grid_tiles):
+def exchange_kernel(devices, vp_count, capacity, src_ref, grid_ref, recv_ref, send_buf,
+                    send_sems, recv_sems, local_sem):
+    op = lax.axis_index("opair")
+    me = op * vp_count + lax.axis_index("vpair")
+
+    def peer(k):
+        d = (me + k) % devices
+        return d, (d // vp_count, d % vp_count)
+
+    barrier = pltpu.get_barrier_semaphore()
+
+    def greet(k, carry):
+        _, where = peer(k)
+        pl.semaphore_signal(barrier, inc=1, device_id=where, device_id_type=MESH)
+        return carry
+
+    lax.fori_loop(1, devices, greet, 0)
+
+    def gather(j, carry):
+        send_buf[j] = grid_ref[jnp.maximum(src_ref[j], 0)]
+        return carry
+
+    lax.fori_loop(0, send_buf.shape[0], gather, 0)
+    pl.semaphore_wait(barrier, devices - 1)
+
+    def copy_to(k):
+        d, where = peer(k)
+        return pltpu.make_async_remote_copy(
+            src_ref=send_buf.at[pl.ds(d * capacity, capacity)],
+            dst_ref=recv_ref.at[pl.ds(me * capacity, capacity)],
+            send_sem=send_sems.at[k],
+            recv_sem=recv_sems.at[k],
+            device_id=where,
+            device_id_type=MESH,
+        )
+
+    def start(k, carry):
+        copy_to(k).start()
+        return carry
+
+    lax.fori_loop(1, devices, start, 0)
+    local = pltpu.make_async_copy(
+        send_buf.at[pl.ds(me * capacity, capacity)],
+        recv_ref.at[pl.ds(me * capacity, capacity)],
+        local_sem,
+    )
+    local.start()
+
+    def finish(k, carry):
+        copy_to(k).wait()
+        return carry
+
+    lax.fori_loop(1, devices, finish, 0)
+    local.wait()
+
+
+def exchange(src, grid_tiles, devices, vp_count, capacity):
     return pl.pallas_call(
-        gather_kernel,
+        functools.partial(exchange_kernel, devices, vp_count, capacity),
         out_shape=jax.ShapeDtypeStruct(grid_tiles.shape, grid_tiles.dtype),
         in_specs=[
             pl.BlockSpec(memory_space=pltpu.SMEM),
             pl.BlockSpec(memory_space=pltpu.VMEM),
         ],
         out_specs=pl.BlockSpec(memory_space=pltpu.VMEM),
-        compiler_params=pltpu.CompilerParams(vmem_limit_bytes=VMEM_LIMIT),
+        scratch_shapes=[
+            pltpu.VMEM(grid_tiles.shape, grid_tiles.dtype),
+            pltpu.SemaphoreType.DMA((devices,)),
+            pltpu.SemaphoreType.DMA((devices,)),
+            pltpu.SemaphoreType.DMA(()),
+        ],
+        compiler_params=pltpu.CompilerParams(
+            collective_id=1, has_side_effects=True, vmem_limit_bytes=VMEM_LIMIT
+        ),
     )(src, grid_tiles)
 
 
@@ -261,13 +306,10 @@
         .at[placing]
         .set(jnp.arange(slot_count, dtype=jnp.int32))[: devices * capacity]
     )
-    departing_tiles = gather_tiles(src, grid_tiles)
     label_rows = jnp.stack([tile_owner % owned, tile_rows % RT_OP, tile_cols % kc_local], axis=1)
     labels = jnp.where((src >= 0)[:, None], jnp.take(label_rows, jnp.maximum(src, 0), axis=0), -1)
     arrived = lax.all_to_all(labels, ("opair", "vpair"), split_axis=0, concat_axis=0, tiled=True)
-    incoming = lax.all_to_all(
-        departing_tiles, ("opair", "vpair"), split_axis=0, concat_axis=0, tiled=True
-    )
+    incoming = exchange(src, grid_tiles, devices, vp_count, capacity)
     meta = jnp.transpose(arrived).reshape(-1)
     ring = 4
     ov_tiles, partial_value = place_and_contract(

time: 279 us -> 368 us (1.32)
  Pallas kernels: 140 us -> 337 us
  waiting for transfers between devices: 99.1 us -> 0.01 us
  starting transfers between devices: 21.5 us -> 11.1 us
    pallas_call x1, Pallas kernels: 11.9 us -> 169 us  [exchange(): pl.pallas_call(functools.partial(exchange_kernel, devices, vp_count, capa...]
    all_to_all x1 -> x0, waiting for transfers between devices: 99.1 us -> none  [on_device(): lax.all_to_all(departing_tiles, ('opair', 'vpair'), split_axis=0, concat_...]
    pallas_call x1, Pallas kernels: 82.2 us -> 123 us  [reduce_scatter(): pl.pallas_call(functools.partial(rs_kernel, ring), out_shape=jax.ShapeDty...]
    all_to_all x1 -> x0, starting transfers between devices: 10.4 us -> none  [on_device(): lax.all_to_all(departing_tiles, ('opair', 'vpair'), split_axis=0, concat_...]
  transfers between devices with their start and end apart: 2 -> 1, of which waited for: 1 -> 0; matrix products, arithmetic and copies ran while one was open for 3% -> 2% of each run, Pallas kernels for 4% -> 46%
where the time goes in v10:
time: 368 us; the launch traced here: 366 us
  Pallas kernels  337 us (92%)
  local copies, waits for them, and re-layouts  11.8 us (3%)
  starting transfers between devices  11.1 us (3%)
  other arithmetic  5.46 us (1%)
    pallas_call x1, Pallas kernels, exchange(): pl.pallas_call(functools.partial(exchange_kernel, devices, vp_count, capa...  169 us
    pallas_call x1, Pallas kernels, reduce_scatter(): pl.pallas_call(functools.partial(rs_kernel, ring), out_shape=jax.ShapeDty...  123 us
    pallas_call x1, Pallas kernels, place_and_contract(): pl.pallas_call(functools.partial(place_kernel, quarters, ring), out_shape...  45.5 us
    all_to_all x1, starting transfers between devices, on_device(): lax.all_to_all(labels, ('opair', 'vpair'), split_axis=0, concat_axis=0, t...  11.1 us
  transfers between devices with their start and end apart: 1, of which 0 were waited for; matrix products, arithmetic and copies ran while one was open for 2% of the time, Pallas kernels for 46%

profile of v10, /device:TPU:0, one launch (start us, length us, event | category | flops | bytes accessed | tf_op | source)
XLA Modules:
  0.0 366.0 jit_solution(14269690135513659388)
XLA Ops:
  0.6 0.7 fusion.11
  1.3 0.7 fusion.9
  2.0 0.1 copy.24
  2.1 0.2 fusion
  2.4 0.2 fusion.2
  2.6 0.7 compare_select_fusion
  3.3 1.4 scatter_custom_fusion
  4.7 0.6 fusion.10
  5.3 0.7 and_select_fusion.1
  6.0 0.7 and_select_fusion
  6.7 0.2 ge.17
  6.8 0.2 le.15
  7.0 0.1 copy.26
  7.2 0.7 gather_fusion
  7.9 1.0 select_select_fusion
  8.9 11.1 %all-to-all-start = ((s32[128,2,3]{2,1,0:T(2,128)}), s32[128,2,3]{2,1,0:T(2,128)S(1)}, u32[]{:S(2)}, u32[]{:S(2)}) async-start(s32[128,2,3]{2,1,0:T(2,128)} %select_select_fusion), calls=%async_computation | async-start | bytes 262144 | tf_op jit(solution)/shard_map/all_to_all | solution.py:311
  20.0 6.4 %copy.28 = bf16[16,128,1024]{1,2,0:T(8,128)(2,1)} copy(bf16[16,128,1024]{2,1,0:T(8,128)(2,1)} %bitcast.27) | data formatting | bytes 8388608 | tf_op jit(solution)/shard_map/reshape | solution.py:298
  26.4 168.7 %shard_map.68.inc_ref = bf16[256,128,128]{2,1,0:T(8,128)(2,1)} custom-call(s32[256]{0:T(256)} %get-tuple-element.6.src_ref, bf16[256,128,128]{2,1,0:T(8,128)(2,1)} %grid_ref.1), custom_call_target="tpu_custom_call" | custom-call | tf_op jit(solution)/shard_map/pallas_call | solution.py:73
  195.1 0.0 all-to-all-done
  195.1 0.1 copy.30
  195.2 0.6 reshape.57.meta_ref
  195.8 45.5 %shard_map.69 = (bf16[128,128,128]{2,1,0:T(8,128)(2,1)}, f32[4,32,256,128]{3,2,1,0:T(8,128)}) custom-call(s32[768]{0:T(1024)} %reshape.57.meta_ref, bf16[256,128,128]{2,1,0:T(8,128)(2,1)} %shard_map.68.inc_ref, bf16[16,1024,128]{2,1,0:T(8,128)(2,1)} %bitcast.26), custom_call_target="tpu_custom_call" | custom-call | tf_op jit(solution)/shard_map/pallas_call | solution.py:130
  241.3 122.7 %shard_map.70 = f32[4,256,128]{2,1,0:T(8,128)} custom-call(f32[4,32,256,128]{3,2,1,0:T(8,128)} %get-tuple-element.5.part_ref), custom_call_target="tpu_custom_call" | custom-call | tf_op jit(solution)/shard_map/pallas_call | solution.py:264
  364.0 2.0 copy.29
  (10 shorter events, 0.1 us)
Async XLA Ops:
  8.9 186.2 %all-to-all-start = ((s32[128,2,3]{2,1,0:T(2,128)}), s32[128,2,3]{2,1,0:T(2,128)S(1)}, u32[]{:S(2)}, u32[]{:S(2)}) async-start(s32[128,2,3]{2,1,0:T(2,128)} %select_select_fusion), calls=%async_computation | async-start | bytes 262144 | tf_op jit(solution)/shard_map/all_to_all | solution.py:311

commit v11 on v5

--- a/solution.py
+++ b/solution.py
@@ -69,10 +69,10 @@
         def _():
             tile = inc_ref[i]
             ov_ref[jnp.maximum(pos, 0)] = tile.T
-            prod = jnp.dot(int_ref[jnp.maximum(col, 0)], tile, preferred_element_type=jnp.float32)
             for q in range(quarters):
                 s = storage_row(q, jnp.maximum(row, 0), ring)
-                part_ref[q, s] += prod[q * width : (q + 1) * width, :]
+                block = int_ref[jnp.maximum(col, 0), pl.ds(q * width, width), :]
+                part_ref[q, s] += jnp.dot(block, tile, preferred_element_type=jnp.float32)
 
         return carry
 

time: 279 us -> 276 us (0.989)
  Pallas kernels: 140 us -> 137 us
    pallas_call x1, Pallas kernels: 45.6 us -> 42.7 us  [place_and_contract(): pl.pallas_call(functools.partial(place_kernel, quarters, ring), out_shape...]
where the time goes in v11:
time: 276 us
  Pallas kernels  137 us (50%)
  waiting for transfers between devices  99.1 us (36%)
  starting transfers between devices  21.5 us (8%)
  local copies, waits for them, and re-layouts  11.8 us (4%)
  other arithmetic  5.46 us (2%)
    all_to_all x1, waiting for transfers between devices, on_device(): lax.all_to_all(departing_tiles, ('opair', 'vpair'), split_axis=0, concat_...  99.1 us
    pallas_call x1, Pallas kernels, reduce_scatter(): pl.pallas_call(functools.partial(rs_kernel, ring), out_shape=jax.ShapeDty...  82.3 us
    pallas_call x1, Pallas kernels, place_and_contract(): pl.pallas_call(functools.partial(place_kernel, quarters, ring), out_shape...  42.7 us
    pallas_call x1, Pallas kernels, gather_tiles(): pl.pallas_call(gather_kernel, out_shape=jax.ShapeDtypeStruct(grid_tiles.s...  11.9 us
    all_to_all x1, starting transfers between devices, on_device(): lax.all_to_all(labels, ('opair', 'vpair'), split_axis=0, concat_axis=0, t...  11.1 us
    all_to_all x1, starting transfers between devices, on_device(): lax.all_to_all(departing_tiles, ('opair', 'vpair'), split_axis=0, concat_...  10.3 us
    reshape x1, local copies, waits for them, and re-layouts, on_device(): integrals.reshape(kc_local, tile_width, integrals.shape[1])  6.37 us
  transfers between devices with their start and end apart: 2, of which 1 were waited for; matrix products, arithmetic and copies ran while one was open for 3% of the time, Pallas kernels for 4%

profile of v11, /device:TPU:0, one launch (start us, length us, event | category | flops | bytes accessed | tf_op | source)
XLA Modules:
  0.0 275.5 jit_solution(1155127384345186461)
XLA Ops:
  0.6 0.7 fusion.11
  1.3 0.7 fusion.9
  2.0 0.1 copy.24
  2.1 0.2 fusion
  2.4 0.2 fusion.2
  2.6 0.7 compare_select_fusion
  3.3 1.4 scatter_custom_fusion
  4.7 0.6 fusion.10
  5.3 0.7 and_select_fusion.1
  6.0 0.7 and_select_fusion
  6.7 0.2 ge.17
  6.8 0.2 le.15
  7.0 0.1 copy.26
  7.2 0.7 gather_fusion
  7.9 1.0 select_select_fusion
  8.9 11.1 %all-to-all-start = ((s32[128,2,3]{2,1,0:T(2,128)}), s32[128,2,3]{2,1,0:T(2,128)S(1)}, u32[]{:S(2)}, u32[]{:S(2)}) async-start(s32[128,2,3]{2,1,0:T(2,128)} %select_select_fusion), calls=%async_computation | async-start | bytes 262144 | tf_op jit(solution)/shard_map/all_to_all | solution.py:267
  20.0 11.9 %shard_map.68 = bf16[256,128,128]{2,1,0:T(8,128)(2,1)} custom-call(s32[256]{0:T(256)} %get-tuple-element.6.src_ref, bf16[256,128,128]{2,1,0:T(8,128)(2,1)} %grid_ref.1), custom_call_target="tpu_custom_call" | custom-call | tf_op jit(solution)/shard_map/pallas_call | solution.py:36
  32.0 10.3 %all-to-all-start.1 = ((bf16[256,128,128]{2,1,0:T(8,128)(2,1)}), bf16[256,128,128]{2,1,0:T(8,128)(2,1)}, u32[]{:S(2)}, u32[]{:S(2)}) async-start(bf16[256,128,128]{2,1,0:T(8,128)(2,1)} %shard_map.68), calls=%async_computation.1 | async-start | bytes 16777216 | tf_op jit(solution)/shard_map/all_to_all | solution.py:268
  42.3 6.4 %copy.28 = bf16[16,128,1024]{1,2,0:T(8,128)(2,1)} copy(bf16[16,128,1024]{2,1,0:T(8,128)(2,1)} %bitcast.27) | data formatting | bytes 8388608 | tf_op jit(solution)/shard_map/reshape | solution.py:253
  48.8 0.6 reshape.57.meta_ref
  49.4 99.1 %all-to-all-done.1.inc_ref = bf16[256,128,128]{2,1,0:T(8,128)(2,1)} async-done(((bf16[256,128,128]{2,1,0:T(8,128)(2,1)}), bf16[256,128,128]{2,1,0:T(8,128)(2,1)}, u32[]{:S(2)}, u32[]{:S(2)}) %all-to-all-start.1) | async-done | bytes 8388640 | tf_op jit(solution)/shard_map/all_to_all | solution.py:268
  148.5 42.7 %shard_map.69 = (bf16[128,128,128]{2,1,0:T(8,128)(2,1)}, f32[4,32,256,128]{3,2,1,0:T(8,128)}) custom-call(s32[768]{0:T(1024)} %reshape.57.meta_ref, bf16[256,128,128]{2,1,0:T(8,128)(2,1)} %all-to-all-done.1.inc_ref, bf16[16,1024,128]{2,1,0:T(8,128)(2,1)} %bitcast.26), custom_call_target="tpu_custom_call" | custom-call | tf_op jit(solution)/shard_map/pallas_call | solution.py:85
  191.1 82.3 %shard_map.70 = f32[4,256,128]{2,1,0:T(8,128)} custom-call(f32[4,32,256,128]{3,2,1,0:T(8,128)} %get-tuple-element.5.part_ref), custom_call_target="tpu_custom_call" | custom-call | tf_op jit(solution)/shard_map/pallas_call | solution.py:219
  273.5 2.0 copy.29
  (12 shorter events, 0.2 us)
Async XLA Ops:
  8.9 23.1 %all-to-all-start = ((s32[128,2,3]{2,1,0:T(2,128)}), s32[128,2,3]{2,1,0:T(2,128)S(1)}, u32[]{:S(2)}, u32[]{:S(2)}) async-start(s32[128,2,3]{2,1,0:T(2,128)} %select_select_fusion), calls=%async_computation | async-start | bytes 262144 | tf_op jit(solution)/shard_map/all_to_all | solution.py:267
  32.0 116.5 %all-to-all-start.1 = ((bf16[256,128,128]{2,1,0:T(8,128)(2,1)}), bf16[256,128,128]{2,1,0:T(8,128)(2,1)}, u32[]{:S(2)}, u32[]{:S(2)}) async-start(bf16[256,128,128]{2,1,0:T(8,128)(2,1)} %shard_map.68), calls=%async_computation.1 | async-start | bytes 16777216 | tf_op jit(solution)/shard_map/all_to_all | solution.py:268

commit v12 on v11

--- a/solution.py
+++ b/solution.py
@@ -126,52 +126,69 @@
         pl.semaphore_signal(barrier, inc=1, device_id=peer, device_id_type=MESH)
     pl.semaphore_wait(barrier, 5)
 
-    core_copy = pltpu.make_async_remote_copy(
-        src_ref=part_ref.at[:, pl.ds((1 - c) * half, half)],
-        dst_ref=core_buf,
-        send_sem=core_send,
-        recv_sem=core_recv,
-        device_id=sib,
-        device_id_type=MESH,
-    )
-    core_copy.start()
-    core_copy.wait()
-
-    def core_sum(k, carry):
-        q = k // half
-        i = k % half
-        red[q, i] = part_ref[q, c * half + i] + core_buf[q, i]
-        return carry
-
-    lax.fori_loop(0, quarters * half, core_sum, 0)
-
     def plan(q):
         d = 1 if q % 2 == 0 else -1
         if q < 2:
             return d, y, z, (y_up if d > 0 else y_dn), (z_up if d > 0 else z_dn)
         return d, z, y, (z_up if d > 0 else z_dn), (y_up if d > 0 else y_dn)
 
+    def core_copy(q):
+        return pltpu.make_async_remote_copy(
+            src_ref=part_ref.at[q, pl.ds((1 - c) * half, half)],
+            dst_ref=core_buf.at[q],
+            send_sem=core_send.at[q],
+            recv_sem=core_recv.at[q],
+            device_id=sib,
+            device_id_type=MESH,
+        )
+
+    def first_copy(q, s):
+        d, a, b, first, second = plan(q)
+        if s == 0:
+            blk = (a - d + 2 * ring) % ring
+            src = red.at[q, pl.ds(blk * ring, ring)]
+        else:
+            src = acc1.at[q, s - 1]
+        return pltpu.make_async_remote_copy(
+            src_ref=src,
+            dst_ref=rbuf1.at[q, s],
+            send_sem=send1.at[q, s],
+            recv_sem=recv1.at[q, s],
+            device_id=first,
+            device_id_type=MESH,
+        )
+
+    def second_copy(q, s):
+        d, a, b, first, second = plan(q)
+        if s == 0:
+            src = fin1.at[q, (b - d + 2 * ring) % ring]
+        else:
+            src = acc2.at[q, s - 1]
+        return pltpu.make_async_remote_copy(
+            src_ref=src,
+            dst_ref=rbuf2.at[q, s],
+            send_sem=send2.at[q, s],
+            recv_sem=recv2.at[q, s],
+            device_id=second,
+            device_id_type=MESH,
+        )
+
+    for q in range(quarters):
+        core_copy(q).start()
+
+    for q in range(quarters):
+        core_copy(q).wait()
+
+        def core_sum(i, carry):
+            red[q, i] = part_ref[q, c * half + i] + core_buf[q, i]
+            return carry
+
+        lax.fori_loop(0, half, core_sum, 0)
+        first_copy(q, 0).start()
+
     for s in range(steps):
-        copies = []
         for q in range(quarters):
-            d, a, b, first, second = plan(q)
-            blk = (a - d * (s + 1) + 2 * ring) % ring
-            if s == 0:
-                src = red.at[q, pl.ds(blk * ring, ring)]
-            else:
-                src = acc1.at[q, s - 1]
-            cp = pltpu.make_async_remote_copy(
-                src_ref=src,
-                dst_ref=rbuf1.at[q, s],
-                send_sem=send1.at[q, s],
-                recv_sem=recv1.at[q, s],
-                device_id=first,
-                device_id_type=MESH,
-            )
-            cp.start()
-            copies.append(cp)
-        for q in range(quarters):
-            copies[q].wait()
+            first_copy(q, s).wait()
             d, a, b, first, second = plan(q)
             blk = (a - d * (s + 2) + 3 * ring) % ring
             for j in range(ring):
@@ -180,33 +197,20 @@
                     acc1[q, s, j] = total
                 else:
                     fin1[q, j] = total
+            if s < steps - 1:
+                first_copy(q, s + 1).start()
+            else:
+                second_copy(q, 0).start()
 
     for s in range(steps):
-        copies = []
         for q in range(quarters):
-            d, a, b, first, second = plan(q)
-            blk = (b - d * (s + 1) + 2 * ring) % ring
-            if s == 0:
-                src = fin1.at[q, blk]
-            else:
-                src = acc2.at[q, s - 1]
-            cp = pltpu.make_async_remote_copy(
-                src_ref=src,
-                dst_ref=rbuf2.at[q, s],
-                send_sem=send2.at[q, s],
-                recv_sem=recv2.at[q, s],
-                device_id=second,
-                device_id_type=MESH,
-            )
-            cp.start()
-            copies.append(cp)
-        for q in range(quarters):
-            copies[q].wait()
+            second_copy(q, s).wait()
             d, a, b, first, second = plan(q)
             blk = (b - d * (s + 2) + 3 * ring) % ring
             total = rbuf2[q, s] + fin1[q, blk]
             if s < steps - 1:
                 acc2[q, s] = total
+                second_copy(q, s + 1).start()
             else:
                 out_ref[q] = total
 
@@ -229,8 +233,8 @@
             pltpu.VMEM((quarters, ring, tile_width, width), f32),
             pltpu.VMEM((quarters, steps, tile_width, width), f32),
             pltpu.VMEM((quarters, steps - 1, tile_width, width), f32),
-            pltpu.SemaphoreType.DMA(()),
-            pltpu.SemaphoreType.DMA(()),
+            pltpu.SemaphoreType.DMA((quarters,)),
+            pltpu.SemaphoreType.DMA((quarters,)),
             pltpu.SemaphoreType.DMA((quarters, steps)),
             pltpu.SemaphoreType.DMA((quarters, steps)),
             pltpu.SemaphoreType.DMA((quarters, steps)),

time: 276 us -> 271 us (0.982)
  Pallas kernels: 137 us -> 132 us
    pallas_call x1, Pallas kernels: 82.3 us -> 77 us  [reduce_scatter(): pl.pallas_call(functools.partial(rs_kernel, ring), out_shape=jax.ShapeDty...]
where the time goes in v12:
time: 271 us; the launch traced here: 270 us
  Pallas kernels  132 us (49%)
  waiting for transfers between devices  99.1 us (37%)
  starting transfers between devices  21.5 us (8%)
  local copies, waits for them, and re-layouts  11.8 us (4%)
  other arithmetic  5.46 us (2%)
    all_to_all x1, waiting for transfers between devices, on_device(): lax.all_to_all(departing_tiles, ('opair', 'vpair'), split_axis=0, concat_...  99.1 us
    pallas_call x1, Pallas kernels, reduce_scatter(): pl.pallas_call(functools.partial(rs_kernel, ring), out_shape=jax.ShapeDty...  77 us
    pallas_call x1, Pallas kernels, place_and_contract(): pl.pallas_call(functools.partial(place_kernel, quarters, ring), out_shape...  42.7 us
    pallas_call x1, Pallas kernels, gather_tiles(): pl.pallas_call(gather_kernel, out_shape=jax.ShapeDtypeStruct(grid_tiles.s...  11.9 us
    all_to_all x1, starting transfers between devices, on_device(): lax.all_to_all(labels, ('opair', 'vpair'), split_axis=0, concat_axis=0, t...  11.1 us
    all_to_all x1, starting transfers between devices, on_device(): lax.all_to_all(departing_tiles, ('opair', 'vpair'), split_axis=0, concat_...  10.3 us
    reshape x1, local copies, waits for them, and re-layouts, on_device(): integrals.reshape(kc_local, tile_width, integrals.shape[1])  6.37 us
  transfers between devices with their start and end apart: 2, of which 1 were waited for; matrix products, arithmetic and copies ran while one was open for 3% of the time, Pallas kernels for 4%

profile of v12, /device:TPU:0, one launch (start us, length us, event | category | flops | bytes accessed | tf_op | source)
XLA Modules:
  0.0 270.1 jit_solution(1039911870234841899)
XLA Ops:
  0.6 0.7 fusion.11
  1.3 0.7 fusion.9
  2.0 0.1 copy.24
  2.1 0.2 fusion
  2.4 0.2 fusion.2
  2.6 0.7 compare_select_fusion
  3.3 1.4 scatter_custom_fusion
  4.7 0.6 fusion.10
  5.3 0.7 and_select_fusion.1
  6.0 0.7 and_select_fusion
  6.7 0.2 ge.17
  6.8 0.2 le.15
  7.0 0.1 copy.26
  7.2 0.7 gather_fusion
  7.9 1.0 select_select_fusion
  8.9 11.1 %all-to-all-start = ((s32[128,2,3]{2,1,0:T(2,128)}), s32[128,2,3]{2,1,0:T(2,128)S(1)}, u32[]{:S(2)}, u32[]{:S(2)}) async-start(s32[128,2,3]{2,1,0:T(2,128)} %select_select_fusion), calls=%async_computation | async-start | bytes 262144 | tf_op jit(solution)/shard_map/all_to_all | solution.py:271
  20.0 11.9 %shard_map.68 = bf16[256,128,128]{2,1,0:T(8,128)(2,1)} custom-call(s32[256]{0:T(256)} %get-tuple-element.6.src_ref, bf16[256,128,128]{2,1,0:T(8,128)(2,1)} %grid_ref.1), custom_call_target="tpu_custom_call" | custom-call | tf_op jit(solution)/shard_map/pallas_call | solution.py:36
  32.0 10.3 %all-to-all-start.1 = ((bf16[256,128,128]{2,1,0:T(8,128)(2,1)}), bf16[256,128,128]{2,1,0:T(8,128)(2,1)}, u32[]{:S(2)}, u32[]{:S(2)}) async-start(bf16[256,128,128]{2,1,0:T(8,128)(2,1)} %shard_map.68), calls=%async_computation.1 | async-start | bytes 16777216 | tf_op jit(solution)/shard_map/all_to_all | solution.py:272
  42.3 6.4 %copy.28 = bf16[16,128,1024]{1,2,0:T(8,128)(2,1)} copy(bf16[16,128,1024]{2,1,0:T(8,128)(2,1)} %bitcast.27) | data formatting | bytes 8388608 | tf_op jit(solution)/shard_map/reshape | solution.py:257
  48.7 0.6 reshape.57.meta_ref
  49.3 99.1 %all-to-all-done.1.inc_ref = bf16[256,128,128]{2,1,0:T(8,128)(2,1)} async-done(((bf16[256,128,128]{2,1,0:T(8,128)(2,1)}), bf16[256,128,128]{2,1,0:T(8,128)(2,1)}, u32[]{:S(2)}, u32[]{:S(2)}) %all-to-all-start.1) | async-done | bytes 8388640 | tf_op jit(solution)/shard_map/all_to_all | solution.py:272
  148.5 42.7 %shard_map.69 = (bf16[128,128,128]{2,1,0:T(8,128)(2,1)}, f32[4,32,256,128]{3,2,1,0:T(8,128)}) custom-call(s32[768]{0:T(1024)} %reshape.57.meta_ref, bf16[256,128,128]{2,1,0:T(8,128)(2,1)} %all-to-all-done.1.inc_ref, bf16[16,1024,128]{2,1,0:T(8,128)(2,1)} %bitcast.26), custom_call_target="tpu_custom_call" | custom-call | tf_op jit(solution)/shard_map/pallas_call | solution.py:85
  191.1 77.0 %shard_map.70 = f32[4,256,128]{2,1,0:T(8,128)} custom-call(f32[4,32,256,128]{3,2,1,0:T(8,128)} %get-tuple-element.5.part_ref), custom_call_target="tpu_custom_call" | custom-call | tf_op jit(solution)/shard_map/pallas_call | solution.py:223
  268.1 2.0 copy.29
  (12 shorter events, 0.2 us)
Async XLA Ops:
  8.9 23.1 %all-to-all-start = ((s32[128,2,3]{2,1,0:T(2,128)}), s32[128,2,3]{2,1,0:T(2,128)S(1)}, u32[]{:S(2)}, u32[]{:S(2)}) async-start(s32[128,2,3]{2,1,0:T(2,128)} %select_select_fusion), calls=%async_computation | async-start | bytes 262144 | tf_op jit(solution)/shard_map/all_to_all | solution.py:271
  32.0 116.5 %all-to-all-start.1 = ((bf16[256,128,128]{2,1,0:T(8,128)(2,1)}), bf16[256,128,128]{2,1,0:T(8,128)(2,1)}, u32[]{:S(2)}, u32[]{:S(2)}) async-start(bf16[256,128,128]{2,1,0:T(8,128)(2,1)} %shard_map.68), calls=%async_computation.1 | async-start | bytes 16777216 | tf_op jit(solution)/shard_map/all_to_all | solution.py:272

commit v13 on v12

--- a/solution.py
+++ b/solution.py
@@ -58,7 +58,18 @@
 def place_kernel(quarters, ring, meta_ref, inc_ref, int_ref, ov_ref, part_ref):
     slots = inc_ref.shape[0]
     width = part_ref.shape[2]
-    part_ref[...] = jnp.zeros(part_ref.shape, part_ref.dtype)
+    rows = part_ref.shape[1]
+    zero = jnp.zeros(part_ref.shape[2:], part_ref.dtype)
+
+    def clear(r, carry):
+        @pl.when(meta_ref[4 * slots + r] > 0)
+        def _():
+            for q in range(quarters):
+                part_ref[q, storage_row(q, r, ring)] = zero
+
+        return carry
+
+    lax.fori_loop(0, rows, clear, 0)
 
     def body(i, carry):
         pos = meta_ref[i]
@@ -69,10 +80,19 @@
         def _():
             tile = inc_ref[i]
             ov_ref[jnp.maximum(pos, 0)] = tile.T
+            first = meta_ref[3 * slots + i] > 0
             for q in range(quarters):
                 s = storage_row(q, jnp.maximum(row, 0), ring)
                 block = int_ref[jnp.maximum(col, 0), pl.ds(q * width, width), :]
-                part_ref[q, s] += jnp.dot(block, tile, preferred_element_type=jnp.float32)
+                prod = jnp.dot(block, tile, preferred_element_type=jnp.float32)
+
+                @pl.when(first)
+                def _():
+                    part_ref[q, s] = prod
+
+                @pl.when(jnp.logical_not(first))
+                def _():
+                    part_ref[q, s] += prod
 
         return carry
 
@@ -272,7 +292,14 @@
     incoming = lax.all_to_all(
         departing_tiles, ("opair", "vpair"), split_axis=0, concat_axis=0, tiled=True
     )
-    meta = jnp.transpose(arrived).reshape(-1)
+    valid = arrived[:, 0] >= 0
+    row_in = arrived[:, 1]
+    slot_ids = jnp.arange(slot_count, dtype=jnp.int32)
+    earlier_same = (row_in[None, :] == row_in[:, None]) & valid[None, :] & (slot_ids[None, :] < slot_ids[:, None])
+    first = (valid & ~jnp.any(earlier_same, axis=1)).astype(jnp.int32)
+    row_ids = jnp.arange(RT_OP, dtype=jnp.int32)
+    empty = (~jnp.any((row_in[None, :] == row_ids[:, None]) & valid[None, :], axis=1)).astype(jnp.int32)
+    meta = jnp.concatenate([jnp.transpose(arrived).reshape(-1), first, empty])
     ring = 4
     ov_tiles, partial_value = place_and_contract(
         meta, incoming, int_table, owned, RT_OP, QUARTERS, ring

time: 271 us -> 330 us (1.22)
  Pallas kernels: 132 us -> 191 us
    pallas_call x1, Pallas kernels: 42.7 us -> 102 us  [place_and_contract(): pl.pallas_call(functools.partial(place_kernel, quarters, ring), out_shape...]
  transfers between devices with their start and end apart: 2 -> 2, of which waited for: 1 -> 1; matrix products, arithmetic and copies ran while one was open for 3% -> 2% of each run, Pallas kernels for 4% -> 4%
where the time goes in v13:
time: 330 us
  Pallas kernels  191 us (58%)
  waiting for transfers between devices  98.7 us (30%)
  starting transfers between devices  21.4 us (6%)
  local copies, waits for them, and re-layouts  11.2 us (3%)
  other arithmetic  6.41 us (2%)
    pallas_call x1, Pallas kernels, place_and_contract(): pl.pallas_call(functools.partial(place_kernel, quarters, ring), out_shape...  102 us
    all_to_all x1, waiting for transfers between devices, on_device(): lax.all_to_all(departing_tiles, ('opair', 'vpair'), split_axis=0, concat_...  98.7 us
    pallas_call x1, Pallas kernels, reduce_scatter(): pl.pallas_call(functools.partial(rs_kernel, ring), out_shape=jax.ShapeDty...  77.1 us
    pallas_call x1, Pallas kernels, gather_tiles(): pl.pallas_call(gather_kernel, out_shape=jax.ShapeDtypeStruct(grid_tiles.s...  12 us
    all_to_all x1, starting transfers between devices, on_device(): lax.all_to_all(labels, ('opair', 'vpair'), split_axis=0, concat_axis=0, t...  11.1 us
    all_to_all x1, starting transfers between devices, on_device(): lax.all_to_all(departing_tiles, ('opair', 'vpair'), split_axis=0, concat_...  10.3 us
  transfers between devices with their start and end apart: 2, of which 1 were waited for; matrix products, arithmetic and copies ran while one was open for 2% of the time, Pallas kernels for 4%

profile of v13, /device:TPU:0, one launch (start us, length us, event | category | flops | bytes accessed | tf_op | source)
XLA Modules:
  0.0 329.8 jit_solution(17664877510192126748)
XLA Ops:
  0.6 0.7 fusion.15
  1.3 0.7 fusion.13
  2.1 0.2 fusion.2
  2.4 0.2 fusion.4
  2.6 0.7 compare_select_fusion
  3.3 1.4 scatter_custom_fusion
  4.7 0.6 fusion.14
  5.3 0.7 and_select_fusion.1
  6.0 0.7 and_select_fusion
  6.7 0.2 ge.27
  6.8 0.2 le.15
  7.0 0.1 copy.32
  7.2 0.7 gather_fusion
  7.9 1.0 select_select_fusion
  8.9 11.1 %all-to-all-start = ((s32[128,2,3]{2,1,0:T(2,128)}), s32[128,2,3]{2,1,0:T(2,128)S(1)}, u32[]{:S(2)}, u32[]{:S(2)}) async-start(s32[128,2,3]{2,1,0:T(2,128)} %select_select_fusion), calls=%async_computation | async-start | bytes 262144 | tf_op jit(solution)/shard_map/all_to_all | solution.py:291
  20.0 12.0 %shard_map.68 = bf16[256,128,128]{2,1,0:T(8,128)(2,1)} custom-call(s32[256]{0:T(256)} %get-tuple-element.6.src_ref, bf16[256,128,128]{2,1,0:T(8,128)(2,1)} %grid_ref.1), custom_call_target="tpu_custom_call" | custom-call | tf_op jit(solution)/shard_map/pallas_call | solution.py:36
  32.0 10.3 %all-to-all-start.1 = ((bf16[256,128,128]{2,1,0:T(8,128)(2,1)}), bf16[256,128,128]{2,1,0:T(8,128)(2,1)}, u32[]{:S(2)}, u32[]{:S(2)}) async-start(bf16[256,128,128]{2,1,0:T(8,128)(2,1)} %shard_map.68), calls=%async_computation.1 | async-start | bytes 16777216 | tf_op jit(solution)/shard_map/all_to_all | solution.py:292
  42.3 6.4 %copy.34 = bf16[16,128,1024]{1,2,0:T(8,128)(2,1)} copy(bf16[16,128,1024]{2,1,0:T(8,128)(2,1)} %bitcast.28) | data formatting | bytes 8388608 | tf_op jit(solution)/shard_map/reshape | solution.py:277
  48.9 0.2 fusion.1
  49.1 0.6 pad_add_fusion.meta_ref
  49.7 98.7 %all-to-all-done.1.inc_ref = bf16[256,128,128]{2,1,0:T(8,128)(2,1)} async-done(((bf16[256,128,128]{2,1,0:T(8,128)(2,1)}), bf16[256,128,128]{2,1,0:T(8,128)(2,1)}, u32[]{:S(2)}, u32[]{:S(2)}) %all-to-all-start.1) | async-done | bytes 8388640 | tf_op jit(solution)/shard_map/all_to_all | solution.py:292
  148.5 102.2 %shard_map.69 = (bf16[128,128,128]{2,1,0:T(8,128)(2,1)}, f32[4,32,256,128]{3,2,1,0:T(8,128)}) custom-call(s32[1056]{0:T(1024)} %pad_add_fusion.meta_ref, bf16[256,128,128]{2,1,0:T(8,128)(2,1)} %all-to-all-done.1.inc_ref, bf16[16,1024,128]{2,1,0:T(8,128)(2,1)} %bitcast.27), custom_call_target="tpu_custom_call" | custom-call | tf_op jit(solution)/shard_map/pallas_call | solution.py:105
  250.7 77.1 %shard_map.70 = f32[4,256,128]{2,1,0:T(8,128)} custom-call(f32[4,32,256,128]{3,2,1,0:T(8,128)} %get-tuple-element.5.part_ref), custom_call_target="tpu_custom_call" | custom-call | tf_op jit(solution)/shard_map/pallas_call | solution.py:243
  327.8 2.0 copy.35
  (19 shorter events, 0.5 us)
Async XLA Ops:
  8.9 23.1 %all-to-all-start = ((s32[128,2,3]{2,1,0:T(2,128)}), s32[128,2,3]{2,1,0:T(2,128)S(1)}, u32[]{:S(2)}, u32[]{:S(2)}) async-start(s32[128,2,3]{2,1,0:T(2,128)} %select_select_fusion), calls=%async_computation | async-start | bytes 262144 | tf_op jit(solution)/shard_map/all_to_all | solution.py:291
  32.0 116.4 %all-to-all-start.1 = ((bf16[256,128,128]{2,1,0:T(8,128)(2,1)}), bf16[256,128,128]{2,1,0:T(8,128)(2,1)}, u32[]{:S(2)}, u32[]{:S(2)}) async-start(bf16[256,128,128]{2,1,0:T(8,128)(2,1)} %shard_map.68), calls=%async_computation.1 | async-start | bytes 16777216 | tf_op jit(solution)/shard_map/all_to_all | solution.py:292

commit v14 on v12

--- a/solution.py
+++ b/solution.py
@@ -8,7 +8,7 @@
 from jax.sharding import PartitionSpec as P
 
 RT_OP = 32
-QUARTERS = 4
+QUARTERS = 8
 MESH = pl.DeviceIdType.MESH
 VMEM_LIMIT = 60 * 1024 * 1024
 
@@ -50,7 +50,7 @@
     y = (row // 2) % ring
     z = row // (2 * ring)
     half = ring * ring
-    if q < 2:
+    if q < QUARTERS // 2:
         return c * half + y * ring + z
     return c * half + z * ring + y
 
@@ -69,10 +69,13 @@
         def _():
             tile = inc_ref[i]
             ov_ref[jnp.maximum(pos, 0)] = tile.T
-            for q in range(quarters):
-                s = storage_row(q, jnp.maximum(row, 0), ring)
-                block = int_ref[jnp.maximum(col, 0), pl.ds(q * width, width), :]
-                part_ref[q, s] += jnp.dot(block, tile, preferred_element_type=jnp.float32)
+            for q in range(quarters // 2):
+                block = int_ref[jnp.maximum(col, 0), pl.ds(2 * q * width, 2 * width), :]
+                prod = jnp.dot(block, tile, preferred_element_type=jnp.float32)
+                for h in range(2):
+                    k = 2 * q + h
+                    s = storage_row(k, jnp.maximum(row, 0), ring)
+                    part_ref[k, s] += prod[h * width : (h + 1) * width, :]
 
         return carry
 
@@ -128,7 +131,7 @@
 
     def plan(q):
         d = 1 if q % 2 == 0 else -1
-        if q < 2:
+        if q < quarters // 2:
             return d, y, z, (y_up if d > 0 else y_dn), (z_up if d > 0 else z_dn)
         return d, z, y, (z_up if d > 0 else z_dn), (y_up if d > 0 else y_dn)
 

time: 271 us -> 261 us (0.963)
  Pallas kernels: 132 us -> 122 us
    pallas_call x1, Pallas kernels: 77 us -> 67.4 us  [reduce_scatter(): pl.pallas_call(functools.partial(rs_kernel, ring), out_shape=jax.ShapeDty...]
  transfers between devices with their start and end apart: 2 -> 2, of which waited for: 1 -> 1; matrix products, arithmetic and copies ran while one was open for 3% -> 3% of each run, Pallas kernels for 4% -> 5%
where the time goes in v14:
time: 261 us
  Pallas kernels  122 us (47%)
  waiting for transfers between devices  99.1 us (38%)
  starting transfers between devices  21.5 us (8%)
  local copies, waits for them, and re-layouts  11.8 us (5%)
  other arithmetic  5.46 us (2%)
    all_to_all x1, waiting for transfers between devices, on_device(): lax.all_to_all(departing_tiles, ('opair', 'vpair'), split_axis=0, concat_...  99.1 us
    pallas_call x1, Pallas kernels, reduce_scatter(): pl.pallas_call(functools.partial(rs_kernel, ring), out_shape=jax.ShapeDty...  67.4 us
    pallas_call x1, Pallas kernels, place_and_contract(): pl.pallas_call(functools.partial(place_kernel, quarters, ring), out_shape...  42.7 us
    pallas_call x1, Pallas kernels, gather_tiles(): pl.pallas_call(gather_kernel, out_shape=jax.ShapeDtypeStruct(grid_tiles.s...  11.9 us
    all_to_all x1, starting transfers between devices, on_device(): lax.all_to_all(labels, ('opair', 'vpair'), split_axis=0, concat_axis=0, t...  11.1 us
    all_to_all x1, starting transfers between devices, on_device(): lax.all_to_all(departing_tiles, ('opair', 'vpair'), split_axis=0, concat_...  10.3 us
    reshape x1, local copies, waits for them, and re-layouts, on_device(): integrals.reshape(kc_local, tile_width, integrals.shape[1])  6.37 us
  transfers between devices with their start and end apart: 2, of which 1 were waited for; matrix products, arithmetic and copies ran while one was open for 3% of the time, Pallas kernels for 5%

profile of v14, /device:TPU:0, one launch (start us, length us, event | category | flops | bytes accessed | tf_op | source)
XLA Modules:
  0.0 260.6 jit_solution(166679069218165647)
XLA Ops:
  0.6 0.7 fusion.11
  1.3 0.7 fusion.9
  2.0 0.1 copy.24
  2.1 0.2 fusion
  2.4 0.2 fusion.2
  2.6 0.7 compare_select_fusion
  3.3 1.4 scatter_custom_fusion
  4.7 0.6 fusion.10
  5.3 0.7 and_select_fusion.1
  6.0 0.7 and_select_fusion
  6.7 0.2 ge.17
  6.8 0.2 le.15
  7.0 0.1 copy.26
  7.2 0.7 gather_fusion
  7.9 1.0 select_select_fusion
  8.9 11.1 %all-to-all-start = ((s32[128,2,3]{2,1,0:T(2,128)}), s32[128,2,3]{2,1,0:T(2,128)S(1)}, u32[]{:S(2)}, u32[]{:S(2)}) async-start(s32[128,2,3]{2,1,0:T(2,128)} %select_select_fusion), calls=%async_computation | async-start | bytes 262144 | tf_op jit(solution)/shard_map/all_to_all | solution.py:274
  20.0 11.9 %shard_map.68 = bf16[256,128,128]{2,1,0:T(8,128)(2,1)} custom-call(s32[256]{0:T(256)} %get-tuple-element.6.src_ref, bf16[256,128,128]{2,1,0:T(8,128)(2,1)} %grid_ref.1), custom_call_target="tpu_custom_call" | custom-call | tf_op jit(solution)/shard_map/pallas_call | solution.py:36
  32.0 10.3 %all-to-all-start.1 = ((bf16[256,128,128]{2,1,0:T(8,128)(2,1)}), bf16[256,128,128]{2,1,0:T(8,128)(2,1)}, u32[]{:S(2)}, u32[]{:S(2)}) async-start(bf16[256,128,128]{2,1,0:T(8,128)(2,1)} %shard_map.68), calls=%async_computation.1 | async-start | bytes 16777216 | tf_op jit(solution)/shard_map/all_to_all | solution.py:275
  42.3 6.4 %copy.28 = bf16[16,128,1024]{1,2,0:T(8,128)(2,1)} copy(bf16[16,128,1024]{2,1,0:T(8,128)(2,1)} %bitcast.27) | data formatting | bytes 8388608 | tf_op jit(solution)/shard_map/reshape | solution.py:260
  48.8 0.6 reshape.57.meta_ref
  49.4 99.1 %all-to-all-done.1.inc_ref = bf16[256,128,128]{2,1,0:T(8,128)(2,1)} async-done(((bf16[256,128,128]{2,1,0:T(8,128)(2,1)}), bf16[256,128,128]{2,1,0:T(8,128)(2,1)}, u32[]{:S(2)}, u32[]{:S(2)}) %all-to-all-start.1) | async-done | bytes 8388640 | tf_op jit(solution)/shard_map/all_to_all | solution.py:275
  148.5 42.7 %shard_map.69 = (bf16[128,128,128]{2,1,0:T(8,128)(2,1)}, f32[8,32,128,128]{3,2,1,0:T(8,128)}) custom-call(s32[768]{0:T(1024)} %reshape.57.meta_ref, bf16[256,128,128]{2,1,0:T(8,128)(2,1)} %all-to-all-done.1.inc_ref, bf16[16,1024,128]{2,1,0:T(8,128)(2,1)} %bitcast.26), custom_call_target="tpu_custom_call" | custom-call | tf_op jit(solution)/shard_map/pallas_call | solution.py:88
  191.2 67.4 %shard_map.70 = f32[8,128,128]{2,1,0:T(8,128)} custom-call(f32[8,32,128,128]{3,2,1,0:T(8,128)} %get-tuple-element.5.part_ref), custom_call_target="tpu_custom_call" | custom-call | tf_op jit(solution)/shard_map/pallas_call | solution.py:226
  258.5 2.0 copy.29
  (12 shorter events, 0.2 us)
Async XLA Ops:
  8.9 23.1 %all-to-all-start = ((s32[128,2,3]{2,1,0:T(2,128)}), s32[128,2,3]{2,1,0:T(2,128)S(1)}, u32[]{:S(2)}, u32[]{:S(2)}) async-start(s32[128,2,3]{2,1,0:T(2,128)} %select_select_fusion), calls=%async_computation | async-start | bytes 262144 | tf_op jit(solution)/shard_map/all_to_all | solution.py:274
  32.0 116.5 %all-to-all-start.1 = ((bf16[256,128,128]{2,1,0:T(8,128)(2,1)}), bf16[256,128,128]{2,1,0:T(8,128)(2,1)}, u32[]{:S(2)}, u32[]{:S(2)}) async-start(bf16[256,128,128]{2,1,0:T(8,128)(2,1)} %shard_map.68), calls=%async_computation.1 | async-start | bytes 16777216 | tf_op jit(solution)/shard_map/all_to_all | solution.py:275

commit v15 on v14

--- a/solution.py
+++ b/solution.py
@@ -8,7 +8,7 @@
 from jax.sharding import PartitionSpec as P
 
 RT_OP = 32
-QUARTERS = 8
+QUARTERS = 16
 MESH = pl.DeviceIdType.MESH
 VMEM_LIMIT = 60 * 1024 * 1024
 
@@ -69,11 +69,12 @@
         def _():
             tile = inc_ref[i]
             ov_ref[jnp.maximum(pos, 0)] = tile.T
-            for q in range(quarters // 2):
-                block = int_ref[jnp.maximum(col, 0), pl.ds(2 * q * width, 2 * width), :]
+            per = quarters // 4
+            for q in range(4):
+                block = int_ref[jnp.maximum(col, 0), pl.ds(q * per * width, per * width), :]
                 prod = jnp.dot(block, tile, preferred_element_type=jnp.float32)
-                for h in range(2):
-                    k = 2 * q + h
+                for h in range(per):
+                    k = per * q + h
                     s = storage_row(k, jnp.maximum(row, 0), ring)
                     part_ref[k, s] += prod[h * width : (h + 1) * width, :]
 

time: 261 us -> 261 us (level)
  no operation moved by 1% of the time
where the time goes in v15:
time: 261 us; the launch traced here: 260 us
  Pallas kernels  122 us (47%)
  waiting for transfers between devices  99.1 us (38%)
  starting transfers between devices  21.4 us (8%)
  local copies, waits for them, and re-layouts  11.8 us (5%)
  other arithmetic  5.46 us (2%)
    all_to_all x1, waiting for transfers between devices, on_device(): lax.all_to_all(departing_tiles, ('opair', 'vpair'), split_axis=0, concat_...  99.1 us
    pallas_call x1, Pallas kernels, reduce_scatter(): pl.pallas_call(functools.partial(rs_kernel, ring), out_shape=jax.ShapeDty...  67.1 us
    pallas_call x1, Pallas kernels, place_and_contract(): pl.pallas_call(functools.partial(place_kernel, quarters, ring), out_shape...  42.7 us
    pallas_call x1, Pallas kernels, gather_tiles(): pl.pallas_call(gather_kernel, out_shape=jax.ShapeDtypeStruct(grid_tiles.s...  12 us
    all_to_all x1, starting transfers between devices, on_device(): lax.all_to_all(labels, ('opair', 'vpair'), split_axis=0, concat_axis=0, t...  11.1 us
    all_to_all x1, starting transfers between devices, on_device(): lax.all_to_all(departing_tiles, ('opair', 'vpair'), split_axis=0, concat_...  10.3 us
    reshape x1, local copies, waits for them, and re-layouts, on_device(): integrals.reshape(kc_local, tile_width, integrals.shape[1])  6.37 us
  transfers between devices with their start and end apart: 2, of which 1 were waited for; matrix products, arithmetic and copies ran while one was open for 3% of the time, Pallas kernels for 5%

profile of v15, /device:TPU:0, one launch (start us, length us, event | category | flops | bytes accessed | tf_op | source)
XLA Modules:
  0.0 260.3 jit_solution(6717602765045514957)
XLA Ops:
  0.6 0.7 fusion.11
  1.3 0.7 fusion.9
  2.0 0.1 copy.24
  2.1 0.2 fusion
  2.4 0.2 fusion.2
  2.6 0.7 compare_select_fusion
  3.3 1.4 scatter_custom_fusion
  4.7 0.6 fusion.10
  5.3 0.7 and_select_fusion.1
  6.0 0.7 and_select_fusion
  6.7 0.2 ge.17
  6.8 0.2 le.15
  7.0 0.1 copy.26
  7.2 0.7 gather_fusion
  7.9 1.0 select_select_fusion
  8.9 11.1 %all-to-all-start = ((s32[128,2,3]{2,1,0:T(2,128)}), s32[128,2,3]{2,1,0:T(2,128)S(1)}, u32[]{:S(2)}, u32[]{:S(2)}) async-start(s32[128,2,3]{2,1,0:T(2,128)} %select_select_fusion), calls=%async_computation | async-start | bytes 262144 | tf_op jit(solution)/shard_map/all_to_all | solution.py:275
  20.0 12.0 %shard_map.68 = bf16[256,128,128]{2,1,0:T(8,128)(2,1)} custom-call(s32[256]{0:T(256)} %get-tuple-element.6.src_ref, bf16[256,128,128]{2,1,0:T(8,128)(2,1)} %grid_ref.1), custom_call_target="tpu_custom_call" | custom-call | tf_op jit(solution)/shard_map/pallas_call | solution.py:36
  32.0 10.3 %all-to-all-start.1 = ((bf16[256,128,128]{2,1,0:T(8,128)(2,1)}), bf16[256,128,128]{2,1,0:T(8,128)(2,1)}, u32[]{:S(2)}, u32[]{:S(2)}) async-start(bf16[256,128,128]{2,1,0:T(8,128)(2,1)} %shard_map.68), calls=%async_computation.1 | async-start | bytes 16777216 | tf_op jit(solution)/shard_map/all_to_all | solution.py:276
  42.3 6.4 %copy.28 = bf16[16,128,1024]{1,2,0:T(8,128)(2,1)} copy(bf16[16,128,1024]{2,1,0:T(8,128)(2,1)} %bitcast.27) | data formatting | bytes 8388608 | tf_op jit(solution)/shard_map/reshape | solution.py:261
  48.8 0.6 reshape.57.meta_ref
  49.4 99.1 %all-to-all-done.1.inc_ref = bf16[256,128,128]{2,1,0:T(8,128)(2,1)} async-done(((bf16[256,128,128]{2,1,0:T(8,128)(2,1)}), bf16[256,128,128]{2,1,0:T(8,128)(2,1)}, u32[]{:S(2)}, u32[]{:S(2)}) %all-to-all-start.1) | async-done | bytes 8388640 | tf_op jit(solution)/shard_map/all_to_all | solution.py:276
  148.5 42.7 %shard_map.69 = (bf16[128,128,128]{2,1,0:T(8,128)(2,1)}, f32[16,32,64,128]{3,2,1,0:T(8,128)}) custom-call(s32[768]{0:T(1024)} %reshape.57.meta_ref, bf16[256,128,128]{2,1,0:T(8,128)(2,1)} %all-to-all-done.1.inc_ref, bf16[16,1024,128]{2,1,0:T(8,128)(2,1)} %bitcast.26), custom_call_target="tpu_custom_call" | custom-call | tf_op jit(solution)/shard_map/pallas_call | solution.py:89
  191.2 67.1 %shard_map.70 = f32[16,64,128]{2,1,0:T(8,128)} custom-call(f32[16,32,64,128]{3,2,1,0:T(8,128)} %get-tuple-element.5.part_ref), custom_call_target="tpu_custom_call" | custom-call | tf_op jit(solution)/shard_map/pallas_call | solution.py:227
  258.2 2.0 copy.29
  (12 shorter events, 0.2 us)
Async XLA Ops:
  8.9 23.1 %all-to-all-start = ((s32[128,2,3]{2,1,0:T(2,128)}), s32[128,2,3]{2,1,0:T(2,128)S(1)}, u32[]{:S(2)}, u32[]{:S(2)}) async-start(s32[128,2,3]{2,1,0:T(2,128)} %select_select_fusion), calls=%async_computation | async-start | bytes 262144 | tf_op jit(solution)/shard_map/all_to_all | solution.py:275
  32.0 116.5 %all-to-all-start.1 = ((bf16[256,128,128]{2,1,0:T(8,128)(2,1)}), bf16[256,128,128]{2,1,0:T(8,128)(2,1)}, u32[]{:S(2)}, u32[]{:S(2)}) async-start(bf16[256,128,128]{2,1,0:T(8,128)(2,1)} %shard_map.68), calls=%async_computation.1 | async-start | bytes 16777216 | tf_op jit(solution)/shard_map/all_to_all | solution.py:276

commit v16 on v14

--- a/solution.py
+++ b/solution.py
@@ -13,23 +13,24 @@
 VMEM_LIMIT = 60 * 1024 * 1024
 
 
-def gather_kernel(src_ref, grid_ref, out_ref):
-    zero = jnp.zeros(out_ref.shape[1:], out_ref.dtype)
-
-    def body(j, carry):
-        s = src_ref[j]
-
-        @pl.when(s >= 0)
-        def _():
-            out_ref[j] = grid_ref[jnp.maximum(s, 0)]
-
-        @pl.when(s < 0)
-        def _():
-            out_ref[j] = zero
-
+def gather_kernel(src_ref, grid_ref, out_ref, sems):
+    slots = out_ref.shape[0]
+
+    def copy(j):
+        return pltpu.make_async_copy(
+            grid_ref.at[jnp.maximum(src_ref[j], 0)], out_ref.at[j], sems.at[j]
+        )
+
+    def start(j, carry):
+        copy(j).start()
         return carry
 
-    lax.fori_loop(0, out_ref.shape[0], body, 0)
+    def finish(j, carry):
+        copy(j).wait()
+        return carry
+
+    lax.fori_loop(0, slots, start, 0)
+    lax.fori_loop(0, slots, finish, 0)
 
 
 def gather_tiles(src, grid_tiles):
@@ -38,9 +39,10 @@
         out_shape=jax.ShapeDtypeStruct(grid_tiles.shape, grid_tiles.dtype),
         in_specs=[
             pl.BlockSpec(memory_space=pltpu.SMEM),
-            pl.BlockSpec(memory_space=pltpu.VMEM),
+            pl.BlockSpec(memory_space=pl.ANY),
         ],
         out_specs=pl.BlockSpec(memory_space=pltpu.VMEM),
+        scratch_shapes=[pltpu.SemaphoreType.DMA((grid_tiles.shape[0],))],
         compiler_params=pltpu.CompilerParams(vmem_limit_bytes=VMEM_LIMIT),
     )(src, grid_tiles)
 

time: 261 us -> 265 us (1.015)
  starting transfers between devices: 21.5 us -> 24.7 us
    all_to_all x1, starting transfers between devices: 10.3 us -> 13.6 us  [on_device(): lax.all_to_all(departing_tiles, ('opair', 'vpair'), split_axis=0, concat_...]
where the time goes in v16:
time: 265 us; the launch traced here: 264 us
  Pallas kernels  123 us (46%)
  waiting for transfers between devices  99.1 us (37%)
  starting transfers between devices  24.7 us (9%)
  local copies, waits for them, and re-layouts  11.8 us (4%)
  other arithmetic  5.46 us (2%)
    all_to_all x1, waiting for transfers between devices, on_device(): lax.all_to_all(departing_tiles, ('opair', 'vpair'), split_axis=0, concat_...  99.1 us
    pallas_call x1, Pallas kernels, reduce_scatter(): pl.pallas_call(functools.partial(rs_kernel, ring), out_shape=jax.ShapeDty...  67.4 us
    pallas_call x1, Pallas kernels, place_and_contract(): pl.pallas_call(functools.partial(place_kernel, quarters, ring), out_shape...  42.7 us
    all_to_all x1, starting transfers between devices, on_device(): lax.all_to_all(departing_tiles, ('opair', 'vpair'), split_axis=0, concat_...  13.6 us
    pallas_call x1, Pallas kernels, gather_tiles(): pl.pallas_call(gather_kernel, out_shape=jax.ShapeDtypeStruct(grid_tiles.s...  12.5 us
    all_to_all x1, starting transfers between devices, on_device(): lax.all_to_all(labels, ('opair', 'vpair'), split_axis=0, concat_axis=0, t...  11.1 us
    reshape x1, local copies, waits for them, and re-layouts, on_device(): integrals.reshape(kc_local, tile_width, integrals.shape[1])  6.37 us
  transfers between devices with their start and end apart: 2, of which 1 were waited for; matrix products, arithmetic and copies ran while one was open for 3% of the time, Pallas kernels for 5%

profile of v16, /device:TPU:0, one launch (start us, length us, event | category | flops | bytes accessed | tf_op | source)
XLA Modules:
  0.0 264.4 jit_solution(11811573231558931326)
XLA Ops:
  0.6 0.7 fusion.11
  1.3 0.7 fusion.9
  2.0 0.1 copy.24
  2.1 0.2 fusion
  2.4 0.2 fusion.2
  2.6 0.7 compare_select_fusion
  3.3 1.4 scatter_custom_fusion
  4.7 0.6 fusion.10
  5.3 0.7 and_select_fusion.1
  6.0 0.7 and_select_fusion
  6.7 0.2 ge.17
  6.8 0.2 le.15
  7.0 0.1 copy.26
  7.2 0.7 gather_fusion
  7.9 1.0 select_select_fusion
  8.9 11.1 %all-to-all-start = ((s32[128,2,3]{2,1,0:T(2,128)}), s32[128,2,3]{2,1,0:T(2,128)S(1)}, u32[]{:S(2)}, u32[]{:S(2)}) async-start(s32[128,2,3]{2,1,0:T(2,128)} %select_select_fusion), calls=%async_computation | async-start | bytes 262144 | tf_op jit(solution)/shard_map/all_to_all | solution.py:276
  20.0 12.5 %shard_map.68 = bf16[256,128,128]{2,1,0:T(8,128)(2,1)} custom-call(s32[256]{0:T(256)} %get-tuple-element.6.src_ref, bf16[256,128,128]{2,1,0:T(8,128)(2,1)} %grid_ref.1), custom_call_target="tpu_custom_call" | custom-call | tf_op jit(solution)/shard_map/pallas_call | solution.py:37
  32.5 13.6 %all-to-all-start.1 = ((bf16[256,128,128]{2,1,0:T(8,128)(2,1)}), bf16[256,128,128]{2,1,0:T(8,128)(2,1)}, u32[]{:S(2)}, u32[]{:S(2)}) async-start(bf16[256,128,128]{2,1,0:T(8,128)(2,1)} %shard_map.68), calls=%async_computation.1 | async-start | bytes 16777216 | tf_op jit(solution)/shard_map/all_to_all | solution.py:277
  46.1 6.4 %copy.28 = bf16[16,128,1024]{1,2,0:T(8,128)(2,1)} copy(bf16[16,128,1024]{2,1,0:T(8,128)(2,1)} %bitcast.27) | data formatting | bytes 8388608 | tf_op jit(solution)/shard_map/reshape | solution.py:262
  52.6 0.6 reshape.57.meta_ref
  53.2 99.1 %all-to-all-done.1.inc_ref = bf16[256,128,128]{2,1,0:T(8,128)(2,1)} async-done(((bf16[256,128,128]{2,1,0:T(8,128)(2,1)}), bf16[256,128,128]{2,1,0:T(8,128)(2,1)}, u32[]{:S(2)}, u32[]{:S(2)}) %all-to-all-start.1) | async-done | bytes 8388640 | tf_op jit(solution)/shard_map/all_to_all | solution.py:277
  152.3 42.7 %shard_map.69 = (bf16[128,128,128]{2,1,0:T(8,128)(2,1)}, f32[8,32,128,128]{3,2,1,0:T(8,128)}) custom-call(s32[768]{0:T(1024)} %reshape.57.meta_ref, bf16[256,128,128]{2,1,0:T(8,128)(2,1)} %all-to-all-done.1.inc_ref, bf16[16,1024,128]{2,1,0:T(8,128)(2,1)} %bitcast.26), custom_call_target="tpu_custom_call" | custom-call | tf_op jit(solution)/shard_map/pallas_call | solution.py:90
  195.0 67.4 %shard_map.70 = f32[8,128,128]{2,1,0:T(8,128)} custom-call(f32[8,32,128,128]{3,2,1,0:T(8,128)} %get-tuple-element.5.part_ref), custom_call_target="tpu_custom_call" | custom-call | tf_op jit(solution)/shard_map/pallas_call | solution.py:228
  262.4 2.0 copy.29
  (12 shorter events, 0.2 us)
Async XLA Ops:
  8.9 23.6 %all-to-all-start = ((s32[128,2,3]{2,1,0:T(2,128)}), s32[128,2,3]{2,1,0:T(2,128)S(1)}, u32[]{:S(2)}, u32[]{:S(2)}) async-start(s32[128,2,3]{2,1,0:T(2,128)} %select_select_fusion), calls=%async_computation | async-start | bytes 262144 | tf_op jit(solution)/shard_map/all_to_all | solution.py:276
  32.5 119.8 %all-to-all-start.1 = ((bf16[256,128,128]{2,1,0:T(8,128)(2,1)}), bf16[256,128,128]{2,1,0:T(8,128)(2,1)}, u32[]{:S(2)}, u32[]{:S(2)}) async-start(bf16[256,128,128]{2,1,0:T(8,128)(2,1)} %shard_map.68), calls=%async_computation.1 | async-start | bytes 16777216 | tf_op jit(solution)/shard_map/all_to_all | solution.py:277

commit v17 on v14

--- a/solution.py
+++ b/solution.py
@@ -176,11 +176,14 @@
             device_id_type=MESH,
         )
 
-    for q in range(quarters):
+    ahead = 2
+    for q in range(ahead):
         core_copy(q).start()
 
     for q in range(quarters):
         core_copy(q).wait()
+        if q + ahead < quarters:
+            core_copy(q + ahead).start()
 
         def core_sum(i, carry):
             red[q, i] = part_ref[q, c * half + i] + core_buf[q, i]

time: 261 us -> 261 us (level)
  no operation moved by 1% of the time
where the time goes in v17:
time: 261 us
  Pallas kernels  122 us (47%)
  waiting for transfers between devices  99.1 us (38%)
  starting transfers between devices  21.5 us (8%)
  local copies, waits for them, and re-layouts  11.8 us (5%)
  other arithmetic  5.46 us (2%)
    all_to_all x1, waiting for transfers between devices, on_device(): lax.all_to_all(departing_tiles, ('opair', 'vpair'), split_axis=0, concat_...  99.1 us
    pallas_call x1, Pallas kernels, reduce_scatter(): pl.pallas_call(functools.partial(rs_kernel, ring), out_shape=jax.ShapeDty...  67.4 us
    pallas_call x1, Pallas kernels, place_and_contract(): pl.pallas_call(functools.partial(place_kernel, quarters, ring), out_shape...  42.7 us
    pallas_call x1, Pallas kernels, gather_tiles(): pl.pallas_call(gather_kernel, out_shape=jax.ShapeDtypeStruct(grid_tiles.s...  11.9 us
    all_to_all x1, starting transfers between devices, on_device(): lax.all_to_all(labels, ('opair', 'vpair'), split_axis=0, concat_axis=0, t...  11.1 us
    all_to_all x1, starting transfers between devices, on_device(): lax.all_to_all(departing_tiles, ('opair', 'vpair'), split_axis=0, concat_...  10.4 us
    reshape x1, local copies, waits for them, and re-layouts, on_device(): integrals.reshape(kc_local, tile_width, integrals.shape[1])  6.37 us
  transfers between devices with their start and end apart: 2, of which 1 were waited for; matrix products, arithmetic and copies ran while one was open for 3% of the time, Pallas kernels for 5%

profile of v17, /device:TPU:0, one launch (start us, length us, event | category | flops | bytes accessed | tf_op | source)
XLA Modules:
  0.0 260.6 jit_solution(16784276612891313109)
XLA Ops:
  0.6 0.7 fusion.11
  1.3 0.7 fusion.9
  2.0 0.1 copy.24
  2.1 0.2 fusion
  2.4 0.2 fusion.2
  2.6 0.7 compare_select_fusion
  3.3 1.4 scatter_custom_fusion
  4.7 0.6 fusion.10
  5.3 0.7 and_select_fusion.1
  6.0 0.7 and_select_fusion
  6.7 0.2 ge.17
  6.8 0.2 le.15
  7.0 0.1 copy.26
  7.2 0.7 gather_fusion
  7.9 1.0 select_select_fusion
  8.9 11.1 %all-to-all-start = ((s32[128,2,3]{2,1,0:T(2,128)}), s32[128,2,3]{2,1,0:T(2,128)S(1)}, u32[]{:S(2)}, u32[]{:S(2)}) async-start(s32[128,2,3]{2,1,0:T(2,128)} %select_select_fusion), calls=%async_computation | async-start | bytes 262144 | tf_op jit(solution)/shard_map/all_to_all | solution.py:277
  20.0 11.9 %shard_map.68 = bf16[256,128,128]{2,1,0:T(8,128)(2,1)} custom-call(s32[256]{0:T(256)} %get-tuple-element.6.src_ref, bf16[256,128,128]{2,1,0:T(8,128)(2,1)} %grid_ref.1), custom_call_target="tpu_custom_call" | custom-call | tf_op jit(solution)/shard_map/pallas_call | solution.py:36
  32.0 10.4 %all-to-all-start.1 = ((bf16[256,128,128]{2,1,0:T(8,128)(2,1)}), bf16[256,128,128]{2,1,0:T(8,128)(2,1)}, u32[]{:S(2)}, u32[]{:S(2)}) async-start(bf16[256,128,128]{2,1,0:T(8,128)(2,1)} %shard_map.68), calls=%async_computation.1 | async-start | bytes 16777216 | tf_op jit(solution)/shard_map/all_to_all | solution.py:278
  42.3 6.4 %copy.28 = bf16[16,128,1024]{1,2,0:T(8,128)(2,1)} copy(bf16[16,128,1024]{2,1,0:T(8,128)(2,1)} %bitcast.27) | data formatting | bytes 8388608 | tf_op jit(solution)/shard_map/reshape | solution.py:263
  48.8 0.6 reshape.57.meta_ref
  49.4 99.1 %all-to-all-done.1.inc_ref = bf16[256,128,128]{2,1,0:T(8,128)(2,1)} async-done(((bf16[256,128,128]{2,1,0:T(8,128)(2,1)}), bf16[256,128,128]{2,1,0:T(8,128)(2,1)}, u32[]{:S(2)}, u32[]{:S(2)}) %all-to-all-start.1) | async-done | bytes 8388640 | tf_op jit(solution)/shard_map/all_to_all | solution.py:278
  148.5 42.7 %shard_map.69 = (bf16[128,128,128]{2,1,0:T(8,128)(2,1)}, f32[8,32,128,128]{3,2,1,0:T(8,128)}) custom-call(s32[768]{0:T(1024)} %reshape.57.meta_ref, bf16[256,128,128]{2,1,0:T(8,128)(2,1)} %all-to-all-done.1.inc_ref, bf16[16,1024,128]{2,1,0:T(8,128)(2,1)} %bitcast.26), custom_call_target="tpu_custom_call" | custom-call | tf_op jit(solution)/shard_map/pallas_call | solution.py:88
  191.2 67.4 %shard_map.70 = f32[8,128,128]{2,1,0:T(8,128)} custom-call(f32[8,32,128,128]{3,2,1,0:T(8,128)} %get-tuple-element.5.part_ref), custom_call_target="tpu_custom_call" | custom-call | tf_op jit(solution)/shard_map/pallas_call | solution.py:229
  258.6 2.0 copy.29
  (12 shorter events, 0.2 us)
Async XLA Ops:
  8.9 23.1 %all-to-all-start = ((s32[128,2,3]{2,1,0:T(2,128)}), s32[128,2,3]{2,1,0:T(2,128)S(1)}, u32[]{:S(2)}, u32[]{:S(2)}) async-start(s32[128,2,3]{2,1,0:T(2,128)} %select_select_fusion), calls=%async_computation | async-start | bytes 262144 | tf_op jit(solution)/shard_map/all_to_all | solution.py:277
  32.0 116.5 %all-to-all-start.1 = ((bf16[256,128,128]{2,1,0:T(8,128)(2,1)}), bf16[256,128,128]{2,1,0:T(8,128)(2,1)}, u32[]{:S(2)}, u32[]{:S(2)}) async-start(bf16[256,128,128]{2,1,0:T(8,128)(2,1)} %shard_map.68), calls=%async_computation.1 | async-start | bytes 16777216 | tf_op jit(solution)/shard_map/all_to_all | solution.py:278

commit v18 on v17

--- a/solution.py
+++ b/solution.py
@@ -218,7 +218,7 @@
                 acc2[q, s] = total
                 second_copy(q, s + 1).start()
             else:
-                out_ref[q] = total
+                out_ref[:, q * tile_width : (q + 1) * tile_width] = total.T
 
 
 def reduce_scatter(part, ring):
@@ -228,7 +228,7 @@
     f32 = jnp.float32
     return pl.pallas_call(
         functools.partial(rs_kernel, ring),
-        out_shape=jax.ShapeDtypeStruct((quarters, tile_width, width), f32),
+        out_shape=jax.ShapeDtypeStruct((width, quarters * tile_width), f32),
         in_specs=[pl.BlockSpec(memory_space=pltpu.VMEM)],
         out_specs=pl.BlockSpec(memory_space=pltpu.VMEM),
         scratch_shapes=[
@@ -284,7 +284,7 @@
         meta, incoming, int_table, owned, RT_OP, QUARTERS, ring
     )
     cycle_t = reduce_scatter(partial_value, ring)
-    cycle_sum = jnp.transpose(cycle_t.reshape(-1, tile_width))
+    cycle_sum = cycle_t
     return (ov_tiles, cycle_sum)
 
 

time: 261 us -> 262 us (level)
  no operation moved by 1% of the time
where the time goes in v18:
time: 262 us; the launch traced here: 261 us
  Pallas kernels  122 us (47%)
  waiting for transfers between devices  99.1 us (38%)
  starting transfers between devices  21.5 us (8%)
  local copies, waits for them, and re-layouts  11.7 us (4%)
  other arithmetic  5.46 us (2%)
    all_to_all x1, waiting for transfers between devices, on_device(): lax.all_to_all(departing_tiles, ('opair', 'vpair'), split_axis=0, concat_...  99.1 us
    pallas_call x1, Pallas kernels, reduce_scatter(): pl.pallas_call(functools.partial(rs_kernel, ring), out_shape=jax.ShapeDty...  67.6 us
    pallas_call x1, Pallas kernels, place_and_contract(): pl.pallas_call(functools.partial(place_kernel, quarters, ring), out_shape...  42.7 us
    pallas_call x1, Pallas kernels, gather_tiles(): pl.pallas_call(gather_kernel, out_shape=jax.ShapeDtypeStruct(grid_tiles.s...  11.9 us
    all_to_all x1, starting transfers between devices, on_device(): lax.all_to_all(labels, ('opair', 'vpair'), split_axis=0, concat_axis=0, t...  11.1 us
    all_to_all x1, starting transfers between devices, on_device(): lax.all_to_all(departing_tiles, ('opair', 'vpair'), split_axis=0, concat_...  10.4 us
    reshape x1, local copies, waits for them, and re-layouts, on_device(): integrals.reshape(kc_local, tile_width, integrals.shape[1])  6.37 us
  transfers between devices with their start and end apart: 2, of which 1 were waited for; matrix products, arithmetic and copies ran while one was open for 3% of the time, Pallas kernels for 5%

profile of v18, /device:TPU:0, one launch (start us, length us, event | category | flops | bytes accessed | tf_op | source)
XLA Modules:
  0.0 260.6 jit_solution(8824093823062693238)
XLA Ops:
  0.6 0.7 fusion.11
  1.3 0.7 fusion.9
  2.0 0.1 copy.21
  2.1 0.2 fusion
  2.4 0.2 fusion.2
  2.6 0.7 compare_select_fusion
  3.3 1.4 scatter_custom_fusion
  4.7 0.6 fusion.10
  5.3 0.7 and_select_fusion.1
  6.0 0.7 and_select_fusion
  6.7 0.2 ge.17
  6.8 0.2 le.15
  7.0 0.1 copy.23
  7.2 0.7 gather_fusion
  7.9 1.0 select_select_fusion
  8.9 11.1 %all-to-all-start = ((s32[128,2,3]{2,1,0:T(2,128)}), s32[128,2,3]{2,1,0:T(2,128)S(1)}, u32[]{:S(2)}, u32[]{:S(2)}) async-start(s32[128,2,3]{2,1,0:T(2,128)} %select_select_fusion), calls=%async_computation | async-start | bytes 262144 | tf_op jit(solution)/shard_map/all_to_all | solution.py:277
  20.0 11.9 %shard_map.68 = bf16[256,128,128]{2,1,0:T(8,128)(2,1)} custom-call(s32[256]{0:T(256)} %get-tuple-element.6.src_ref, bf16[256,128,128]{2,1,0:T(8,128)(2,1)} %grid_ref.1), custom_call_target="tpu_custom_call" | custom-call | tf_op jit(solution)/shard_map/pallas_call | solution.py:36
  32.0 10.4 %all-to-all-start.1 = ((bf16[256,128,128]{2,1,0:T(8,128)(2,1)}), bf16[256,128,128]{2,1,0:T(8,128)(2,1)}, u32[]{:S(2)}, u32[]{:S(2)}) async-start(bf16[256,128,128]{2,1,0:T(8,128)(2,1)} %shard_map.68), calls=%async_computation.1 | async-start | bytes 16777216 | tf_op jit(solution)/shard_map/all_to_all | solution.py:278
  42.3 6.4 %copy.25 = bf16[16,128,1024]{1,2,0:T(8,128)(2,1)} copy(bf16[16,128,1024]{2,1,0:T(8,128)(2,1)} %bitcast.25) | data formatting | bytes 8388608 | tf_op jit(solution)/shard_map/reshape | solution.py:263
  48.8 0.6 reshape.54.meta_ref
  49.4 99.1 %all-to-all-done.1.inc_ref = bf16[256,128,128]{2,1,0:T(8,128)(2,1)} async-done(((bf16[256,128,128]{2,1,0:T(8,128)(2,1)}), bf16[256,128,128]{2,1,0:T(8,128)(2,1)}, u32[]{:S(2)}, u32[]{:S(2)}) %all-to-all-start.1) | async-done | bytes 8388640 | tf_op jit(solution)/shard_map/all_to_all | solution.py:278
  148.5 42.7 %shard_map.69 = (bf16[128,128,128]{2,1,0:T(8,128)(2,1)}, f32[8,32,128,128]{3,2,1,0:T(8,128)}) custom-call(s32[768]{0:T(1024)} %reshape.54.meta_ref, bf16[256,128,128]{2,1,0:T(8,128)(2,1)} %all-to-all-done.1.inc_ref, bf16[16,1024,128]{2,1,0:T(8,128)(2,1)} %bitcast.24), custom_call_target="tpu_custom_call" | custom-call | tf_op jit(solution)/shard_map/pallas_call | solution.py:88
  191.2 67.6 %shard_map.70 = f32[128,1024]{1,0:T(8,128)} custom-call(f32[8,32,128,128]{3,2,1,0:T(8,128)} %get-tuple-element.5.part_ref), custom_call_target="tpu_custom_call" | custom-call | tf_op jit(solution)/shard_map/pallas_call | solution.py:229
  258.7 1.9 copy.28
  (12 shorter events, 0.2 us)
Async XLA Ops:
  8.9 23.1 %all-to-all-start = ((s32[128,2,3]{2,1,0:T(2,128)}), s32[128,2,3]{2,1,0:T(2,128)S(1)}, u32[]{:S(2)}, u32[]{:S(2)}) async-start(s32[128,2,3]{2,1,0:T(2,128)} %select_select_fusion), calls=%async_computation | async-start | bytes 262144 | tf_op jit(solution)/shard_map/all_to_all | solution.py:277
  32.0 116.5 %all-to-all-start.1 = ((bf16[256,128,128]{2,1,0:T(8,128)(2,1)}), bf16[256,128,128]{2,1,0:T(8,128)(2,1)}, u32[]{:S(2)}, u32[]{:S(2)}) async-start(bf16[256,128,128]{2,1,0:T(8,128)(2,1)} %shard_map.68), calls=%async_computation.1 | async-start | bytes 16777216 | tf_op jit(solution)/shard_map/all_to_all | solution.py:278

commit v19 on v17

--- a/solution.py
+++ b/solution.py
@@ -58,7 +58,18 @@
 def place_kernel(quarters, ring, meta_ref, inc_ref, int_ref, ov_ref, part_ref):
     slots = inc_ref.shape[0]
     width = part_ref.shape[2]
-    part_ref[...] = jnp.zeros(part_ref.shape, part_ref.dtype)
+    rows = part_ref.shape[1]
+    zero = jnp.zeros(part_ref.shape[2:], part_ref.dtype)
+
+    def clear(r, carry):
+        @pl.when(meta_ref[4 * slots + r] > 0)
+        def _():
+            for q in range(quarters):
+                part_ref[q, storage_row(q, r, ring)] = zero
+
+        return carry
+
+    lax.fori_loop(0, rows, clear, 0)
 
     def body(i, carry):
         pos = meta_ref[i]
@@ -68,6 +79,7 @@
         @pl.when(pos >= 0)
         def _():
             tile = inc_ref[i]
+            first = meta_ref[3 * slots + i] > 0
             ov_ref[jnp.maximum(pos, 0)] = tile.T
             for q in range(quarters // 2):
                 block = int_ref[jnp.maximum(col, 0), pl.ds(2 * q * width, 2 * width), :]
@@ -75,7 +87,8 @@
                 for h in range(2):
                     k = 2 * q + h
                     s = storage_row(k, jnp.maximum(row, 0), ring)
-                    part_ref[k, s] += prod[h * width : (h + 1) * width, :]
+                    piece = prod[h * width : (h + 1) * width, :]
+                    part_ref[k, s] = jnp.where(first, piece, part_ref[k, s] + piece)
 
         return carry
 
@@ -278,7 +291,14 @@
     incoming = lax.all_to_all(
         departing_tiles, ("opair", "vpair"), split_axis=0, concat_axis=0, tiled=True
     )
-    meta = jnp.transpose(arrived).reshape(-1)
+    valid = arrived[:, 0] >= 0
+    row_in = arrived[:, 1]
+    slot_ids = jnp.arange(slot_count, dtype=jnp.int32)
+    earlier_same = (row_in[None, :] == row_in[:, None]) & valid[None, :] & (slot_ids[None, :] < slot_ids[:, None])
+    first = (valid & ~jnp.any(earlier_same, axis=1)).astype(jnp.int32)
+    row_ids = jnp.arange(RT_OP, dtype=jnp.int32)
+    empty = (~jnp.any((row_in[None, :] == row_ids[:, None]) & valid[None, :], axis=1)).astype(jnp.int32)
+    meta = jnp.concatenate([jnp.transpose(arrived).reshape(-1), first, empty])
     ring = 4
     ov_tiles, partial_value = place_and_contract(
         meta, incoming, int_table, owned, RT_OP, QUARTERS, ring

time: 261 us -> 261 us (level)
  no operation moved by 1% of the time
where the time goes in v19:
time: 261 us; the launch traced here: 260 us
  Pallas kernels  122 us (47%)
  waiting for transfers between devices  98.7 us (38%)
  starting transfers between devices  21.5 us (8%)
  local copies, waits for them, and re-layouts  11.2 us (4%)
  other arithmetic  6.41 us (2%)
    all_to_all x1, waiting for transfers between devices, on_device(): lax.all_to_all(departing_tiles, ('opair', 'vpair'), split_axis=0, concat_...  98.7 us
    pallas_call x1, Pallas kernels, reduce_scatter(): pl.pallas_call(functools.partial(rs_kernel, ring), out_shape=jax.ShapeDty...  67.4 us
    pallas_call x1, Pallas kernels, place_and_contract(): pl.pallas_call(functools.partial(place_kernel, quarters, ring), out_shape...  42.5 us
    pallas_call x1, Pallas kernels, gather_tiles(): pl.pallas_call(gather_kernel, out_shape=jax.ShapeDtypeStruct(grid_tiles.s...  11.9 us
    all_to_all x1, starting transfers between devices, on_device(): lax.all_to_all(labels, ('opair', 'vpair'), split_axis=0, concat_axis=0, t...  11.1 us
    all_to_all x1, starting transfers between devices, on_device(): lax.all_to_all(departing_tiles, ('opair', 'vpair'), split_axis=0, concat_...  10.4 us
    reshape x1, local copies, waits for them, and re-layouts, on_device(): integrals.reshape(kc_local, tile_width, integrals.shape[1])  6.37 us
  transfers between devices with their start and end apart: 2, of which 1 were waited for; matrix products, arithmetic and copies ran while one was open for 3% of the time, Pallas kernels for 5%

profile of v19, /device:TPU:0, one launch (start us, length us, event | category | flops | bytes accessed | tf_op | source)
XLA Modules:
  0.0 260.4 jit_solution(8506190242522854102)
XLA Ops:
  0.6 0.7 fusion.15
  1.3 0.7 fusion.13
  2.1 0.2 fusion.2
  2.4 0.2 fusion.4
  2.6 0.7 compare_select_fusion
  3.3 1.4 scatter_custom_fusion
  4.7 0.6 fusion.14
  5.3 0.7 and_select_fusion.1
  6.0 0.7 and_select_fusion
  6.7 0.2 ge.27
  6.8 0.2 le.15
  7.0 0.1 copy.32
  7.2 0.7 gather_fusion
  7.9 1.0 select_select_fusion
  8.9 11.1 %all-to-all-start = ((s32[128,2,3]{2,1,0:T(2,128)}), s32[128,2,3]{2,1,0:T(2,128)S(1)}, u32[]{:S(2)}, u32[]{:S(2)}) async-start(s32[128,2,3]{2,1,0:T(2,128)} %select_select_fusion), calls=%async_computation | async-start | bytes 262144 | tf_op jit(solution)/shard_map/all_to_all | solution.py:290
  20.0 11.9 %shard_map.68 = bf16[256,128,128]{2,1,0:T(8,128)(2,1)} custom-call(s32[256]{0:T(256)} %get-tuple-element.6.src_ref, bf16[256,128,128]{2,1,0:T(8,128)(2,1)} %grid_ref.1), custom_call_target="tpu_custom_call" | custom-call | tf_op jit(solution)/shard_map/pallas_call | solution.py:36
  31.9 10.4 %all-to-all-start.1 = ((bf16[256,128,128]{2,1,0:T(8,128)(2,1)}), bf16[256,128,128]{2,1,0:T(8,128)(2,1)}, u32[]{:S(2)}, u32[]{:S(2)}) async-start(bf16[256,128,128]{2,1,0:T(8,128)(2,1)} %shard_map.68), calls=%async_computation.1 | async-start | bytes 16777216 | tf_op jit(solution)/shard_map/all_to_all | solution.py:291
  42.3 6.4 %copy.34 = bf16[16,128,1024]{1,2,0:T(8,128)(2,1)} copy(bf16[16,128,1024]{2,1,0:T(8,128)(2,1)} %bitcast.28) | data formatting | bytes 8388608 | tf_op jit(solution)/shard_map/reshape | solution.py:276
  48.9 0.2 fusion.1
  49.2 0.6 pad_add_fusion.meta_ref
  49.8 98.7 %all-to-all-done.1.inc_ref = bf16[256,128,128]{2,1,0:T(8,128)(2,1)} async-done(((bf16[256,128,128]{2,1,0:T(8,128)(2,1)}), bf16[256,128,128]{2,1,0:T(8,128)(2,1)}, u32[]{:S(2)}, u32[]{:S(2)}) %all-to-all-start.1) | async-done | bytes 8388640 | tf_op jit(solution)/shard_map/all_to_all | solution.py:291
  148.5 42.5 %shard_map.69 = (bf16[128,128,128]{2,1,0:T(8,128)(2,1)}, f32[8,32,128,128]{3,2,1,0:T(8,128)}) custom-call(s32[1056]{0:T(1024)} %pad_add_fusion.meta_ref, bf16[256,128,128]{2,1,0:T(8,128)(2,1)} %all-to-all-done.1.inc_ref, bf16[16,1024,128]{2,1,0:T(8,128)(2,1)} %bitcast.27), custom_call_target="tpu_custom_call" | custom-call | tf_op jit(solution)/shard_map/pallas_call | solution.py:101
  191.0 67.4 %shard_map.70 = f32[8,128,128]{2,1,0:T(8,128)} custom-call(f32[8,32,128,128]{3,2,1,0:T(8,128)} %get-tuple-element.5.part_ref), custom_call_target="tpu_custom_call" | custom-call | tf_op jit(solution)/shard_map/pallas_call | solution.py:242
  258.4 2.0 copy.35
  (19 shorter events, 0.5 us)
Async XLA Ops:
  8.9 23.1 %all-to-all-start = ((s32[128,2,3]{2,1,0:T(2,128)}), s32[128,2,3]{2,1,0:T(2,128)S(1)}, u32[]{:S(2)}, u32[]{:S(2)}) async-start(s32[128,2,3]{2,1,0:T(2,128)} %select_select_fusion), calls=%async_computation | async-start | bytes 262144 | tf_op jit(solution)/shard_map/all_to_all | solution.py:290
  31.9 116.6 %all-to-all-start.1 = ((bf16[256,128,128]{2,1,0:T(8,128)(2,1)}), bf16[256,128,128]{2,1,0:T(8,128)(2,1)}, u32[]{:S(2)}, u32[]{:S(2)}) async-start(bf16[256,128,128]{2,1,0:T(8,128)(2,1)} %shard_map.68), calls=%async_computation.1 | async-start | bytes 16777216 | tf_op jit(solution)/shard_map/all_to_all | solution.py:291

commit v20 on v17

--- a/solution.py
+++ b/solution.py
@@ -69,13 +69,10 @@
         def _():
             tile = inc_ref[i]
             ov_ref[jnp.maximum(pos, 0)] = tile.T
-            for q in range(quarters // 2):
-                block = int_ref[jnp.maximum(col, 0), pl.ds(2 * q * width, 2 * width), :]
-                prod = jnp.dot(block, tile, preferred_element_type=jnp.float32)
-                for h in range(2):
-                    k = 2 * q + h
-                    s = storage_row(k, jnp.maximum(row, 0), ring)
-                    part_ref[k, s] += prod[h * width : (h + 1) * width, :]
+            for k in range(quarters):
+                block = int_ref[jnp.maximum(col, 0), pl.ds(k * width, width), :]
+                s = storage_row(k, jnp.maximum(row, 0), ring)
+                part_ref[k, s] += jnp.dot(block, tile, preferred_element_type=jnp.float32)
 
         return carry
 

time: 261 us -> 262 us (level)
  no operation moved by 1% of the time
where the time goes in v20:
time: 262 us; the launch traced here: 261 us
  Pallas kernels  122 us (47%)
  waiting for transfers between devices  99.1 us (38%)
  starting transfers between devices  21.4 us (8%)
  local copies, waits for them, and re-layouts  11.8 us (5%)
  other arithmetic  5.46 us (2%)
    all_to_all x1, waiting for transfers between devices, on_device(): lax.all_to_all(departing_tiles, ('opair', 'vpair'), split_axis=0, concat_...  99.1 us
    pallas_call x1, Pallas kernels, reduce_scatter(): pl.pallas_call(functools.partial(rs_kernel, ring), out_shape=jax.ShapeDty...  67.4 us
    pallas_call x1, Pallas kernels, place_and_contract(): pl.pallas_call(functools.partial(place_kernel, quarters, ring), out_shape...  43.2 us
    pallas_call x1, Pallas kernels, gather_tiles(): pl.pallas_call(gather_kernel, out_shape=jax.ShapeDtypeStruct(grid_tiles.s...  11.9 us
    all_to_all x1, starting transfers between devices, on_device(): lax.all_to_all(labels, ('opair', 'vpair'), split_axis=0, concat_axis=0, t...  11.1 us
    all_to_all x1, starting transfers between devices, on_device(): lax.all_to_all(departing_tiles, ('opair', 'vpair'), split_axis=0, concat_...  10.3 us
    reshape x1, local copies, waits for them, and re-layouts, on_device(): integrals.reshape(kc_local, tile_width, integrals.shape[1])  6.37 us
  transfers between devices with their start and end apart: 2, of which 1 were waited for; matrix products, arithmetic and copies ran while one was open for 3% of the time, Pallas kernels for 5%

profile of v20, /device:TPU:0, one launch (start us, length us, event | category | flops | bytes accessed | tf_op | source)
XLA Modules:
  0.0 261.0 jit_solution(16019150401014128342)
XLA Ops:
  0.6 0.7 fusion.11
  1.3 0.7 fusion.9
  2.0 0.1 copy.24
  2.1 0.2 fusion
  2.4 0.2 fusion.2
  2.6 0.7 compare_select_fusion
  3.3 1.4 scatter_custom_fusion
  4.7 0.6 fusion.10
  5.3 0.7 and_select_fusion.1
  6.0 0.7 and_select_fusion
  6.7 0.2 ge.17
  6.8 0.2 le.15
  7.0 0.1 copy.26
  7.2 0.7 gather_fusion
  7.9 1.0 select_select_fusion
  8.9 11.1 %all-to-all-start = ((s32[128,2,3]{2,1,0:T(2,128)}), s32[128,2,3]{2,1,0:T(2,128)S(1)}, u32[]{:S(2)}, u32[]{:S(2)}) async-start(s32[128,2,3]{2,1,0:T(2,128)} %select_select_fusion), calls=%async_computation | async-start | bytes 262144 | tf_op jit(solution)/shard_map/all_to_all | solution.py:274
  20.0 11.9 %shard_map.68 = bf16[256,128,128]{2,1,0:T(8,128)(2,1)} custom-call(s32[256]{0:T(256)} %get-tuple-element.6.src_ref, bf16[256,128,128]{2,1,0:T(8,128)(2,1)} %grid_ref.1), custom_call_target="tpu_custom_call" | custom-call | tf_op jit(solution)/shard_map/pallas_call | solution.py:36
  31.9 10.3 %all-to-all-start.1 = ((bf16[256,128,128]{2,1,0:T(8,128)(2,1)}), bf16[256,128,128]{2,1,0:T(8,128)(2,1)}, u32[]{:S(2)}, u32[]{:S(2)}) async-start(bf16[256,128,128]{2,1,0:T(8,128)(2,1)} %shard_map.68), calls=%async_computation.1 | async-start | bytes 16777216 | tf_op jit(solution)/shard_map/all_to_all | solution.py:275
  42.3 6.4 %copy.28 = bf16[16,128,1024]{1,2,0:T(8,128)(2,1)} copy(bf16[16,128,1024]{2,1,0:T(8,128)(2,1)} %bitcast.27) | data formatting | bytes 8388608 | tf_op jit(solution)/shard_map/reshape | solution.py:260
  48.7 0.6 reshape.57.meta_ref
  49.3 99.1 %all-to-all-done.1.inc_ref = bf16[256,128,128]{2,1,0:T(8,128)(2,1)} async-done(((bf16[256,128,128]{2,1,0:T(8,128)(2,1)}), bf16[256,128,128]{2,1,0:T(8,128)(2,1)}, u32[]{:S(2)}, u32[]{:S(2)}) %all-to-all-start.1) | async-done | bytes 8388640 | tf_op jit(solution)/shard_map/all_to_all | solution.py:275
  148.4 43.2 %shard_map.69 = (bf16[128,128,128]{2,1,0:T(8,128)(2,1)}, f32[8,32,128,128]{3,2,1,0:T(8,128)}) custom-call(s32[768]{0:T(1024)} %reshape.57.meta_ref, bf16[256,128,128]{2,1,0:T(8,128)(2,1)} %all-to-all-done.1.inc_ref, bf16[16,1024,128]{2,1,0:T(8,128)(2,1)} %bitcast.26), custom_call_target="tpu_custom_call" | custom-call | tf_op jit(solution)/shard_map/pallas_call | solution.py:85
  191.6 67.4 %shard_map.70 = f32[8,128,128]{2,1,0:T(8,128)} custom-call(f32[8,32,128,128]{3,2,1,0:T(8,128)} %get-tuple-element.5.part_ref), custom_call_target="tpu_custom_call" | custom-call | tf_op jit(solution)/shard_map/pallas_call | solution.py:226
  259.0 2.0 copy.29
  (12 shorter events, 0.2 us)
Async XLA Ops:
  8.9 23.1 %all-to-all-start = ((s32[128,2,3]{2,1,0:T(2,128)}), s32[128,2,3]{2,1,0:T(2,128)S(1)}, u32[]{:S(2)}, u32[]{:S(2)}) async-start(s32[128,2,3]{2,1,0:T(2,128)} %select_select_fusion), calls=%async_computation | async-start | bytes 262144 | tf_op jit(solution)/shard_map/all_to_all | solution.py:274
  31.9 116.5 %all-to-all-start.1 = ((bf16[256,128,128]{2,1,0:T(8,128)(2,1)}), bf16[256,128,128]{2,1,0:T(8,128)(2,1)}, u32[]{:S(2)}, u32[]{:S(2)}) async-start(bf16[256,128,128]{2,1,0:T(8,128)(2,1)} %shard_map.68), calls=%async_computation.1 | async-start | bytes 16777216 | tf_op jit(solution)/shard_map/all_to_all | solution.py:275

commit v21 on v14

--- a/solution.py
+++ b/solution.py
@@ -176,11 +176,15 @@
             device_id_type=MESH,
         )
 
-    for q in range(quarters):
-        core_copy(q).start()
-
-    for q in range(quarters):
+    ahead = 2
+    order = [q for pair in zip(range(quarters // 2), range(quarters // 2, quarters)) for q in pair]
+    for n in range(ahead):
+        core_copy(order[n]).start()
+
+    for n, q in enumerate(order):
         core_copy(q).wait()
+        if n + ahead < quarters:
+            core_copy(order[n + ahead]).start()
 
         def core_sum(i, carry):
             red[q, i] = part_ref[q, c * half + i] + core_buf[q, i]
@@ -190,7 +194,7 @@
         first_copy(q, 0).start()
 
     for s in range(steps):
-        for q in range(quarters):
+        for q in order:
             first_copy(q, s).wait()
             d, a, b, first, second = plan(q)
             blk = (a - d * (s + 2) + 3 * ring) % ring

time: 261 us -> 259 us (level)
  Pallas kernels: 122 us -> 119 us
where the time goes in v21:
time: 259 us; the launch traced here: 258 us
  Pallas kernels  119 us (46%)
  waiting for transfers between devices  99.1 us (38%)
  starting transfers between devices  21.4 us (8%)
  local copies, waits for them, and re-layouts  11.8 us (5%)
  other arithmetic  5.46 us (2%)
    all_to_all x1, waiting for transfers between devices, on_device(): lax.all_to_all(departing_tiles, ('opair', 'vpair'), split_axis=0, concat_...  99.1 us
    pallas_call x1, Pallas kernels, reduce_scatter(): pl.pallas_call(functools.partial(rs_kernel, ring), out_shape=jax.ShapeDty...  64.8 us
    pallas_call x1, Pallas kernels, place_and_contract(): pl.pallas_call(functools.partial(place_kernel, quarters, ring), out_shape...  42.7 us
    pallas_call x1, Pallas kernels, gather_tiles(): pl.pallas_call(gather_kernel, out_shape=jax.ShapeDtypeStruct(grid_tiles.s...  12 us
    all_to_all x1, starting transfers between devices, on_device(): lax.all_to_all(labels, ('opair', 'vpair'), split_axis=0, concat_axis=0, t...  11.1 us
    all_to_all x1, starting transfers between devices, on_device(): lax.all_to_all(departing_tiles, ('opair', 'vpair'), split_axis=0, concat_...  10.2 us
    reshape x1, local copies, waits for them, and re-layouts, on_device(): integrals.reshape(kc_local, tile_width, integrals.shape[1])  6.37 us
  transfers between devices with their start and end apart: 2, of which 1 were waited for; matrix products, arithmetic and copies ran while one was open for 3% of the time, Pallas kernels for 5%

profile of v21, /device:TPU:0, one launch (start us, length us, event | category | flops | bytes accessed | tf_op | source)
XLA Modules:
  0.0 258.0 jit_solution(17196518882549921865)
XLA Ops:
  0.6 0.7 fusion.11
  1.3 0.7 fusion.9
  2.0 0.1 copy.24
  2.1 0.2 fusion
  2.4 0.2 fusion.2
  2.6 0.7 compare_select_fusion
  3.3 1.4 scatter_custom_fusion
  4.7 0.6 fusion.10
  5.3 0.7 and_select_fusion.1
  6.0 0.7 and_select_fusion
  6.7 0.2 ge.17
  6.8 0.2 le.15
  7.0 0.1 copy.26
  7.2 0.7 gather_fusion
  7.9 1.0 select_select_fusion
  8.9 11.1 %all-to-all-start = ((s32[128,2,3]{2,1,0:T(2,128)}), s32[128,2,3]{2,1,0:T(2,128)S(1)}, u32[]{:S(2)}, u32[]{:S(2)}) async-start(s32[128,2,3]{2,1,0:T(2,128)} %select_select_fusion), calls=%async_computation | async-start | bytes 262144 | tf_op jit(solution)/shard_map/all_to_all | solution.py:278
  20.0 12.0 %shard_map.68 = bf16[256,128,128]{2,1,0:T(8,128)(2,1)} custom-call(s32[256]{0:T(256)} %get-tuple-element.6.src_ref, bf16[256,128,128]{2,1,0:T(8,128)(2,1)} %grid_ref.1), custom_call_target="tpu_custom_call" | custom-call | tf_op jit(solution)/shard_map/pallas_call | solution.py:36
  32.0 10.2 %all-to-all-start.1 = ((bf16[256,128,128]{2,1,0:T(8,128)(2,1)}), bf16[256,128,128]{2,1,0:T(8,128)(2,1)}, u32[]{:S(2)}, u32[]{:S(2)}) async-start(bf16[256,128,128]{2,1,0:T(8,128)(2,1)} %shard_map.68), calls=%async_computation.1 | async-start | bytes 16777216 | tf_op jit(solution)/shard_map/all_to_all | solution.py:279
  42.3 6.4 %copy.28 = bf16[16,128,1024]{1,2,0:T(8,128)(2,1)} copy(bf16[16,128,1024]{2,1,0:T(8,128)(2,1)} %bitcast.27) | data formatting | bytes 8388608 | tf_op jit(solution)/shard_map/reshape | solution.py:264
  48.7 0.6 reshape.57.meta_ref
  49.3 99.1 %all-to-all-done.1.inc_ref = bf16[256,128,128]{2,1,0:T(8,128)(2,1)} async-done(((bf16[256,128,128]{2,1,0:T(8,128)(2,1)}), bf16[256,128,128]{2,1,0:T(8,128)(2,1)}, u32[]{:S(2)}, u32[]{:S(2)}) %all-to-all-start.1) | async-done | bytes 8388640 | tf_op jit(solution)/shard_map/all_to_all | solution.py:279
  148.5 42.7 %shard_map.69 = (bf16[128,128,128]{2,1,0:T(8,128)(2,1)}, f32[8,32,128,128]{3,2,1,0:T(8,128)}) custom-call(s32[768]{0:T(1024)} %reshape.57.meta_ref, bf16[256,128,128]{2,1,0:T(8,128)(2,1)} %all-to-all-done.1.inc_ref, bf16[16,1024,128]{2,1,0:T(8,128)(2,1)} %bitcast.26), custom_call_target="tpu_custom_call" | custom-call | tf_op jit(solution)/shard_map/pallas_call | solution.py:88
  191.1 64.8 %shard_map.70 = f32[8,128,128]{2,1,0:T(8,128)} custom-call(f32[8,32,128,128]{3,2,1,0:T(8,128)} %get-tuple-element.5.part_ref), custom_call_target="tpu_custom_call" | custom-call | tf_op jit(solution)/shard_map/pallas_call | solution.py:230
  255.9 2.0 copy.29
  (12 shorter events, 0.2 us)
Async XLA Ops:
  8.9 23.1 %all-to-all-start = ((s32[128,2,3]{2,1,0:T(2,128)}), s32[128,2,3]{2,1,0:T(2,128)S(1)}, u32[]{:S(2)}, u32[]{:S(2)}) async-start(s32[128,2,3]{2,1,0:T(2,128)} %select_select_fusion), calls=%async_computation | async-start | bytes 262144 | tf_op jit(solution)/shard_map/all_to_all | solution.py:278
  32.0 116.4 %all-to-all-start.1 = ((bf16[256,128,128]{2,1,0:T(8,128)(2,1)}), bf16[256,128,128]{2,1,0:T(8,128)(2,1)}, u32[]{:S(2)}, u32[]{:S(2)}) async-start(bf16[256,128,128]{2,1,0:T(8,128)(2,1)} %shard_map.68), calls=%async_computation.1 | async-start | bytes 16777216 | tf_op jit(solution)/shard_map/all_to_all | solution.py:279

commit v22 on v21

--- a/solution.py
+++ b/solution.py
@@ -210,7 +210,7 @@
                 second_copy(q, 0).start()
 
     for s in range(steps):
-        for q in range(quarters):
+        for q in order:
             second_copy(q, s).wait()
             d, a, b, first, second = plan(q)
             blk = (b - d * (s + 2) + 3 * ring) % ring

time: 259 us -> 258 us (level)
  no operation moved by 1% of the time
where the time goes in v22:
time: 258 us; the launch traced here: 257 us
  Pallas kernels  119 us (46%)
  waiting for transfers between devices  99.1 us (38%)
  starting transfers between devices  21.4 us (8%)
  local copies, waits for them, and re-layouts  11.8 us (5%)
  other arithmetic  5.46 us (2%)
    all_to_all x1, waiting for transfers between devices, on_device(): lax.all_to_all(departing_tiles, ('opair', 'vpair'), split_axis=0, concat_...  99.1 us
    pallas_call x1, Pallas kernels, reduce_scatter(): pl.pallas_call(functools.partial(rs_kernel, ring), out_shape=jax.ShapeDty...  63.9 us
    pallas_call x1, Pallas kernels, place_and_contract(): pl.pallas_call(functools.partial(place_kernel, quarters, ring), out_shape...  42.7 us
    pallas_call x1, Pallas kernels, gather_tiles(): pl.pallas_call(gather_kernel, out_shape=jax.ShapeDtypeStruct(grid_tiles.s...  12 us
    all_to_all x1, starting transfers between devices, on_device(): lax.all_to_all(labels, ('opair', 'vpair'), split_axis=0, concat_axis=0, t...  11.1 us
    all_to_all x1, starting transfers between devices, on_device(): lax.all_to_all(departing_tiles, ('opair', 'vpair'), split_axis=0, concat_...  10.2 us
    reshape x1, local copies, waits for them, and re-layouts, on_device(): integrals.reshape(kc_local, tile_width, integrals.shape[1])  6.37 us
  transfers between devices with their start and end apart: 2, of which 1 were waited for; matrix products, arithmetic and copies ran while one was open for 3% of the time, Pallas kernels for 5%

profile of v22, /device:TPU:0, one launch (start us, length us, event | category | flops | bytes accessed | tf_op | source)
XLA Modules:
  0.0 257.1 jit_solution(16785855090862941659)
XLA Ops:
  0.6 0.7 fusion.11
  1.3 0.7 fusion.9
  2.0 0.1 copy.24
  2.1 0.2 fusion
  2.4 0.2 fusion.2
  2.6 0.7 compare_select_fusion
  3.3 1.4 scatter_custom_fusion
  4.7 0.6 fusion.10
  5.3 0.7 and_select_fusion.1
  6.0 0.7 and_select_fusion
  6.7 0.2 ge.17
  6.8 0.2 le.15
  7.0 0.1 copy.26
  7.2 0.7 gather_fusion
  7.9 1.0 select_select_fusion
  8.9 11.1 %all-to-all-start = ((s32[128,2,3]{2,1,0:T(2,128)}), s32[128,2,3]{2,1,0:T(2,128)S(1)}, u32[]{:S(2)}, u32[]{:S(2)}) async-start(s32[128,2,3]{2,1,0:T(2,128)} %select_select_fusion), calls=%async_computation | async-start | bytes 262144 | tf_op jit(solution)/shard_map/all_to_all | solution.py:278
  20.0 12.0 %shard_map.68 = bf16[256,128,128]{2,1,0:T(8,128)(2,1)} custom-call(s32[256]{0:T(256)} %get-tuple-element.6.src_ref, bf16[256,128,128]{2,1,0:T(8,128)(2,1)} %grid_ref.1), custom_call_target="tpu_custom_call" | custom-call | tf_op jit(solution)/shard_map/pallas_call | solution.py:36
  32.0 10.2 %all-to-all-start.1 = ((bf16[256,128,128]{2,1,0:T(8,128)(2,1)}), bf16[256,128,128]{2,1,0:T(8,128)(2,1)}, u32[]{:S(2)}, u32[]{:S(2)}) async-start(bf16[256,128,128]{2,1,0:T(8,128)(2,1)} %shard_map.68), calls=%async_computation.1 | async-start | bytes 16777216 | tf_op jit(solution)/shard_map/all_to_all | solution.py:279
  42.3 6.4 %copy.28 = bf16[16,128,1024]{1,2,0:T(8,128)(2,1)} copy(bf16[16,128,1024]{2,1,0:T(8,128)(2,1)} %bitcast.27) | data formatting | bytes 8388608 | tf_op jit(solution)/shard_map/reshape | solution.py:264
  48.7 0.6 reshape.57.meta_ref
  49.3 99.1 %all-to-all-done.1.inc_ref = bf16[256,128,128]{2,1,0:T(8,128)(2,1)} async-done(((bf16[256,128,128]{2,1,0:T(8,128)(2,1)}), bf16[256,128,128]{2,1,0:T(8,128)(2,1)}, u32[]{:S(2)}, u32[]{:S(2)}) %all-to-all-start.1) | async-done | bytes 8388640 | tf_op jit(solution)/shard_map/all_to_all | solution.py:279
  148.4 42.7 %shard_map.69 = (bf16[128,128,128]{2,1,0:T(8,128)(2,1)}, f32[8,32,128,128]{3,2,1,0:T(8,128)}) custom-call(s32[768]{0:T(1024)} %reshape.57.meta_ref, bf16[256,128,128]{2,1,0:T(8,128)(2,1)} %all-to-all-done.1.inc_ref, bf16[16,1024,128]{2,1,0:T(8,128)(2,1)} %bitcast.26), custom_call_target="tpu_custom_call" | custom-call | tf_op jit(solution)/shard_map/pallas_call | solution.py:88
  191.1 63.9 %shard_map.70 = f32[8,128,128]{2,1,0:T(8,128)} custom-call(f32[8,32,128,128]{3,2,1,0:T(8,128)} %get-tuple-element.5.part_ref), custom_call_target="tpu_custom_call" | custom-call | tf_op jit(solution)/shard_map/pallas_call | solution.py:230
  255.1 2.0 copy.29
  (12 shorter events, 0.2 us)
Async XLA Ops:
  8.9 23.1 %all-to-all-start = ((s32[128,2,3]{2,1,0:T(2,128)}), s32[128,2,3]{2,1,0:T(2,128)S(1)}, u32[]{:S(2)}, u32[]{:S(2)}) async-start(s32[128,2,3]{2,1,0:T(2,128)} %select_select_fusion), calls=%async_computation | async-start | bytes 262144 | tf_op jit(solution)/shard_map/all_to_all | solution.py:278
  32.0 116.4 %all-to-all-start.1 = ((bf16[256,128,128]{2,1,0:T(8,128)(2,1)}), bf16[256,128,128]{2,1,0:T(8,128)(2,1)}, u32[]{:S(2)}, u32[]{:S(2)}) async-start(bf16[256,128,128]{2,1,0:T(8,128)(2,1)} %shard_map.68), calls=%async_computation.1 | async-start | bytes 16777216 | tf_op jit(solution)/shard_map/all_to_all | solution.py:279
